TPU v7x, 32 devices: a whole 2x2x4 slice. The times are simulated.
32 devices in a mesh: dp: 8 (over y, x, core), ctx: 4 (over z).
Axes of the slice: x: 2, y: 2, z: 4, core: 2. Of those that a mesh axis runs over, the one named last changes fastest.
Arguments:
- inputs: bfloat16 [8, 1024, 2048], P('dp', 'ctx'), may hold values from -6 to 6
- lengths: int32 [8], P('dp'), may hold values from 512 to 1024, as said below
- norm_gain: bfloat16 [2048], replicated, may hold values from 0.5 to 1.5
- up_weight: bfloat16 [2048, 8192], P('dp'), may hold values from -0.125 to 0.125
- conv_weight: bfloat16 [4, 4096], replicated, may hold values from -3 to 3
- conv_bias: bfloat16 [4096], replicated, may hold values from -3 to 3
- qkv_weight: bfloat16 [3, 4, 4, 4, 256], replicated, may hold values from -3 to 3
- gate_weight: bfloat16 [8, 12288], replicated, may hold values from -0.109375 to 0.109375
- gate_bias: bfloat16 [8], replicated, may hold values from -1 to 8.5
- skip_weight: bfloat16 [4096], replicated, may hold values from 0.5 to 1.5
- outnorm_weight: bfloat16 [4096], replicated, may hold values from 0.5 to 1.5
- down_weight: bfloat16 [4096, 2048], P('dp'), may hold values from -0.09375 to 0.09375
- grad_out: bfloat16 [8, 1024, 2048], P('dp', 'ctx'), may hold values from -6 to 6
Outputs:
- outputs: bfloat16 [8, 1024, 2048], P('dp', 'ctx')
- grad_inputs: float32 [8, 1024, 2048], P('dp', 'ctx')
- grad_norm_gain: float32 [2048], replicated
- grad_up_weight: float32 [2048, 8192], P('dp')
- grad_conv_weight: float32 [4, 4096], replicated
- grad_conv_bias: float32 [4096], replicated
- grad_qkv_weight: float32 [3, 4, 4, 4, 256], replicated
- grad_gate_weight: float32 [8, 12288], replicated
- grad_gate_bias: float32 [8], replicated
- grad_skip_weight: float32 [4096], replicated
- grad_outnorm_weight: float32 [4096], replicated
- grad_down_weight: float32 [4096, 2048], P('dp')
Inputs may be any that keep to these rules, and one draw needn't show every extreme that they name: `lengths`: each entry counts the real tokens of a sequence from its start; one sequence has exactly 1024, another exactly 512.
All inputs are finite; a program needn't handle non-finite values.
Results may differ from a plain program's by a relative error of at most 0.04.
Values may be sent and summed in bfloat16 or wider, within the bound.
No kernel may reach another device: no remote copies, remote signals or barrier semaphores. Data moves between devices by JAX's collectives and lax.ppermute only.
A program may use at most 448 MiB of HBM per device.

v0:
```python
from functools import partial

import jax
import jax.numpy as jnp
from jax import lax
from jax.sharding import PartitionSpec as P

highest = lax.Precision.HIGHEST
epsilon = 1e-05


def shifted(x, axis, by):
    length = lax.axis_size(axis)
    pairs = [(i, i + by) for i in range(length) if 0 <= i + by < length]
    return lax.ppermute(x, axis, pairs)


def low(value_in):
    rounded = lax.optimization_barrier(value_in.astype(jnp.bfloat16)).astype(jnp.float32)
    return value_in + lax.stop_gradient(rounded - value_in)


def layer_norm_low(rows_in, gain_row):
    centred = rows_in - jnp.mean(rows_in, axis=-1, keepdims=True)
    spread = jnp.mean(centred * centred, axis=-1, keepdims=True)
    return low(centred * lax.rsqrt(spread + epsilon) * gain_row)


def headwise(values_in, blocks_in):
    row_count, width_all = values_in.shape
    head_count, block_size, block_out, block_count = blocks_in.shape
    grouped = values_in.reshape(row_count, head_count, block_size, block_count)
    mixed_rows = jnp.einsum("thij,hioj->thoj", grouped, blocks_in, precision=highest)
    return mixed_rows.reshape(row_count, width_all)


def split_heads(rows_in, head_count):
    return rows_in.reshape(rows_in.shape[0], head_count, -1).transpose(1, 0, 2)


def mid_section(mixer_in, rim_rows, conv_taps, conv_shift, qkv_blocks, gate_matrix, gate_offset):
    row_count, width_all = mixer_in.shape
    kernel_size = conv_taps.shape[0]
    head_count = qkv_blocks.shape[1]
    padded_in = jnp.concatenate([rim_rows, mixer_in], axis=0)
    conv_pre = conv_shift[None, :] + conv_taps[0][None, :] * padded_in[0:row_count]
    for tap_index in range(1, kernel_size):
        conv_pre = (
            conv_pre + conv_taps[tap_index][None, :] * padded_in[tap_index : tap_index + row_count]
        )
    conv_out = jax.nn.silu(conv_pre)
    key_scale = (width_all // head_count) ** (-0.5)
    queries = low(headwise(conv_out, qkv_blocks[0]))
    key_rows = low(headwise(conv_out, qkv_blocks[1]) * key_scale)
    value_rows = low(headwise(mixer_in, qkv_blocks[2]))
    joined = jnp.concatenate([queries, key_rows, value_rows], axis=1)
    gate_pre = jnp.dot(joined, gate_matrix.T, precision=highest) + gate_offset[None, :]
    return (
        queries,
        key_rows,
        value_rows,
        gate_pre[:, :head_count],
        jax.nn.log_sigmoid(gate_pre[:, head_count:]),
        conv_out,
    )


def cell_scores(queries, key_rows, head_count):
    return jnp.einsum(
        "htk,hsk->hts",
        split_heads(queries, head_count),
        split_heads(key_rows, head_count),
        precision=highest,
    )


def cell_rest(scores, queries, value_rows, in_gate, log_forget, state_in):
    row_count, width_all = queries.shape
    head_count = state_in.shape[0]
    query_heads = split_heads(queries, head_count)
    value_heads = split_heads(value_rows, head_count)
    decay_sum = jnp.cumsum(log_forget, axis=0).T
    gate_row = in_gate.T
    causal = jnp.arange(row_count)[:, None] >= jnp.arange(row_count)[None, :]
    exponent = decay_sum[:, :, None] - decay_sum[:, None, :] + gate_row[:, None, :]
    weights = jnp.where(causal[None], jnp.exp(jnp.where(causal[None], exponent, 0.0)), 0.0)
    mix_weights = low(weights * scores)
    within = jnp.einsum("hts,hsd->htd", mix_weights, value_heads, precision=highest)
    carried = jnp.einsum("htk,hkd->htd", query_heads, low(state_in), precision=highest)
    numerator = within + jnp.exp(decay_sum)[:, :, None] * carried
    return numerator.transpose(1, 0, 2).reshape(row_count, width_all)


def summary(key_rows, value_rows, in_gate, log_forget):
    head_count = in_gate.shape[1]
    decay_sum = jnp.cumsum(log_forget, axis=0)
    span_decay = decay_sum[-1]
    weights = jnp.exp(span_decay[None, :] - decay_sum + in_gate)
    weighted = low(split_heads(key_rows, head_count) * weights.T[:, :, None])
    state_part = jnp.einsum(
        "htk,htd->hkd", weighted, split_heads(value_rows, head_count), precision=highest
    )
    return (state_part, span_decay)


def tail_section(numerator, conv_out, gate_in, outnorm_scale, skip_scale, head_count):
    row_count, width_all = numerator.shape
    grouped = numerator.reshape(row_count, head_count, -1)
    centred = grouped - jnp.mean(grouped, axis=-1, keepdims=True)
    spread = jnp.mean(centred * centred, axis=-1, keepdims=True)
    normed = (centred * lax.rsqrt(spread + epsilon)).reshape(row_count, width_all) * outnorm_scale
    return low((normed + skip_scale * conv_out) * jax.nn.silu(gate_in))


def on_device(
    inputs,
    lengths,
    norm_gain,
    up_weight,
    conv_weight,
    conv_bias,
    qkv_weight,
    gate_weight,
    gate_bias,
    skip_weight,
    outnorm_weight,
    down_weight,
    grad_out,
):
    span_len = inputs.shape[1]
    inner_width = conv_weight.shape[1]
    head_count = qkv_weight.shape[1]
    kernel_size = conv_weight.shape[0]
    ctx_count = lax.axis_size("ctx")
    ctx_index = lax.axis_index("ctx")
    positions = ctx_index * span_len + jnp.arange(span_len)
    live_rows = (positions < lengths[0]).astype(jnp.float32)[:, None]
    rows_in = inputs[0].astype(jnp.float32)
    norm_scale = norm_gain.astype(jnp.float32)
    conv_taps = conv_weight.astype(jnp.float32)
    conv_shift = conv_bias.astype(jnp.float32)
    qkv_blocks = qkv_weight.astype(jnp.float32)
    gate_matrix = gate_weight.astype(jnp.float32)
    gate_offset = gate_bias.astype(jnp.float32)
    skip_scale = skip_weight.astype(jnp.float32)
    outnorm_scale = outnorm_weight.astype(jnp.float32)
    contract_last = (((1,), (1,)), ((), ()))
    contract_first = (((0,), (0,)), ((), ()))
    normed, front_back = jax.vjp(layer_norm_low, rows_in, norm_scale)
    normed_low = normed.astype(jnp.bfloat16)
    columns = normed_low
    upward = jnp.dot(
        columns,
        lax.all_gather(up_weight, "dp", axis=0, tiled=True),
        preferred_element_type=jnp.float32,
    )
    mixer_low = upward[:, :inner_width].astype(jnp.bfloat16)
    mixer_in = mixer_low.astype(jnp.float32)
    gate_in = upward[:, inner_width:]
    rim_rows = shifted(mixer_low[span_len - kernel_size + 1 :], "ctx", 1).astype(jnp.float32)
    mid_result, mid_back = jax.vjp(
        mid_section, mixer_in, rim_rows, conv_taps, conv_shift, qkv_blocks, gate_matrix, gate_offset
    )
    queries, key_rows, value_rows, in_gate, log_forget, conv_out = mid_result
    summed, summary_back = jax.vjp(summary, key_rows, value_rows, in_gate, log_forget)
    state_part, span_decay = summed

    def relay(turn, carried):
        return shifted(jnp.exp(span_decay)[:, None, None] * carried + state_part, "ctx", 1)

    state_in = lax.fori_loop(0, ctx_count - 1, relay, jnp.zeros_like(state_part))
    scores, score_back = jax.vjp(partial(cell_scores, head_count=head_count), queries, key_rows)
    numerator, rest_back = jax.vjp(
        cell_rest, scores, queries, value_rows, in_gate, log_forget, state_in
    )
    hidden_state, tail_back = jax.vjp(
        partial(tail_section, head_count=head_count),
        numerator,
        conv_out,
        gate_in,
        outnorm_scale,
        skip_scale,
    )
    hidden_low = hidden_state.astype(jnp.bfloat16)
    columns = hidden_low
    branch = jnp.dot(
        columns,
        lax.all_gather(down_weight, "dp", axis=0, tiled=True),
        preferred_element_type=jnp.float32,
    )
    outputs = (live_rows * (rows_in + branch)).astype(jnp.bfloat16)[None]
    out_grad = grad_out[0].astype(jnp.float32) * live_rows
    branch_grad = out_grad.astype(jnp.bfloat16)
    hidden_grad = lax.dot_general(
        branch_grad,
        lax.all_gather(down_weight, "dp", axis=0, tiled=True),
        contract_last,
        preferred_element_type=jnp.float32,
    )
    numer_raw, conv_tail_grad, gate_in_grad, outnorm_grad, skip_grad = tail_back(hidden_grad)
    numer_low = numer_raw.astype(jnp.bfloat16)
    numer_grad = numer_low.astype(jnp.float32)
    scores_raw, query_part, value_grad, ingate_grad, forget_grad, state_grad = rest_back(numer_grad)
    query_extra, key_grad = score_back(scores_raw.astype(jnp.bfloat16).astype(jnp.float32))
    query_grad = query_part + query_extra

    def relay_back(turn, carried):
        return shifted(jnp.exp(span_decay)[:, None, None] * carried + state_grad, "ctx", -1)

    later_grad = lax.fori_loop(0, ctx_count - 1, relay_back, jnp.zeros_like(state_grad))
    decay_grad = jnp.exp(span_decay) * jnp.sum(later_grad * state_in, axis=(1, 2))
    later_rounded = later_grad.astype(jnp.bfloat16).astype(jnp.float32)
    key_extra, value_extra, ingate_extra, forget_extra = summary_back((later_rounded, decay_grad))
    mid_grads = mid_back(
        (
            query_grad,
            key_grad + key_extra,
            value_grad + value_extra,
            ingate_grad + ingate_extra,
            forget_grad + forget_extra,
            conv_tail_grad,
        )
    )
    (
        mixer_grad,
        rim_grad,
        conv_taps_grad,
        conv_shift_grad,
        qkv_grad,
        gate_matrix_grad,
        gate_offset_grad,
    ) = mid_grads
    rim_returned = shifted(rim_grad.astype(jnp.bfloat16), "ctx", -1).astype(rim_grad.dtype)
    mixer_grad = mixer_grad + jnp.pad(rim_returned, ((span_len - kernel_size + 1, 0), (0, 0)))
    upward_grad = jnp.concatenate([mixer_grad, gate_in_grad], axis=1).astype(jnp.bfloat16)
    normed_grad = lax.dot_general(
        upward_grad,
        lax.all_gather(up_weight, "dp", axis=0, tiled=True),
        contract_last,
        preferred_element_type=jnp.float32,
    )
    front_grad, norm_scale_grad = front_back(normed_grad)
    input_grad = (out_grad + front_grad)[None]
    columns = normed_low
    up_part = lax.psum_scatter(
        lax.dot_general(
            columns, upward_grad, contract_first, preferred_element_type=jnp.float32
        ).astype(jnp.bfloat16),
        "dp",
        scatter_dimension=0,
        tiled=True,
    )
    columns = hidden_low
    down_part = lax.psum_scatter(
        lax.dot_general(
            columns, branch_grad, contract_first, preferred_element_type=jnp.float32
        ).astype(jnp.bfloat16),
        "dp",
        scatter_dimension=0,
        tiled=True,
    )
    up_total, down_total = (
        lax.psum(up_part, "ctx").astype(jnp.float32),
        lax.psum(down_part, "ctx").astype(jnp.float32),
    )
    small_total = lax.psum(
        (
            norm_scale_grad,
            conv_taps_grad,
            conv_shift_grad,
            qkv_grad,
            gate_matrix_grad,
            gate_offset_grad,
            skip_grad,
            outnorm_grad,
        ),
        ("dp", "ctx"),
    )
    return (
        outputs,
        input_grad,
        small_total[0],
        up_total,
        small_total[1],
        small_total[2],
        small_total[3],
        small_total[4],
        small_total[5],
        small_total[6],
        small_total[7],
        down_total,
    )


def solution(mesh):
    return jax.shard_map(
        on_device,
        mesh=mesh,
        in_specs=(
            P("dp", "ctx", None),
            P("dp"),
            P(),
            P("dp", None),
            P(),
            P(),
            P(),
            P(),
            P(),
            P(),
            P(),
            P("dp", None),
            P("dp", "ctx", None),
        ),
        out_specs=(
            P("dp", "ctx", None),
            P("dp", "ctx", None),
            P(),
            P("dp", None),
            P(),
            P(),
            P(),
            P(),
            P(),
            P(),
            P(),
            P("dp", None),
        ),
        check_vma=False,
    )
```

profile of v0, /device:TPU:16, one launch (start us, length us, event | category | flops | bytes accessed | tf_op | source)
XLA Modules:
  0.0 3724.0 jit_solution(15394948117392416776)
XLA Ops:
  16.5 155.4 %all-gather.3.cloned.1.call-done = bf16[2048,8192]{1,0:T(8,128)(2,1)} async-done(((bf16[256,8192]{1,0:T(8,128)(2,1)}), bf16[2048,8192]{1,0:T(8,128)(2,1)}) %all-gather.3.cloned.1.call-update) | async-done | bytes 33554448 | tf_op jit(solution)/shard_map/all_gather | solution.py:154
  171.9 19.3 fusion.142
  212.5 51.2 %all-gather.5.cloned.1.call-done = bf16[4096,2048]{1,0:T(8,128)(2,1)} async-done(((bf16[512,2048]{1,0:T(8,128)(2,1)}), bf16[4096,2048]{1,0:T(8,128)(2,1)}) %all-gather.5.cloned.1.call-update) | async-done | bytes 16777232 | tf_op jit(solution)/shard_map/all_gather | solution.py:188
  263.7 12.3 broadcast_multiply_fusion
  327.4 7.8 fusion.91
  342.9 10.2 fusion.100
  356.2 29.3 fusion.54
  385.5 8.0 broadcast.160.clone
  393.5 1143.1 %while.24 = (s32[]{:T(128)}, f32[4,1024,1024]{2,1,0:T(8,128)}, f32[4,1,1]{0,2,1:T(1,128)S(1)}, f32[4,1024,1024]{2,1,0:T(8,128)}, s32[]{:T(128)}) while((s32[]{:T(128)}, f32[4,1024,1024]{2,1,0:T(8,128)}, f32[4,1,1]{0,2,1:T(1,128)S(1)}, f32[4,1024,1024]{2,1,0:T(8,128)}, s32[]{:T(128)}) %tuple.133), condition=%wide.region_5.6_spmd, body=%wide.region_4.5_spmd.sunk | while | flops 8388610 | bytes 117440624 | solution.py:171
  393.5 17.3 multiply_add_fusion.10
  414.2 361.2 %collective-permute-done = f32[4,1024,1024]{2,1,0:T(8,128)} collective-permute-done((f32[4,1024,1024]{2,1,0:T(8,128)}, f32[4,1024,1024]{2,1,0:T(8,128)}, u32[]{:S(2)}, u32[]{:S(2)}) %collective-permute-start) | collective-permute-done | bytes 16777248 | tf_op jit(solution)/shard_map/while/body/eval_jaxpr/ppermute | solution.py:15
  775.4 17.3 multiply_add_fusion.10
  796.1 360.4 %collective-permute-done = f32[4,1024,1024]{2,1,0:T(8,128)} collective-permute-done((f32[4,1024,1024]{2,1,0:T(8,128)}, f32[4,1024,1024]{2,1,0:T(8,128)}, u32[]{:S(2)}, u32[]{:S(2)}) %collective-permute-start) | collective-permute-done | bytes 16777248 | tf_op jit(solution)/shard_map/while/body/eval_jaxpr/ppermute | solution.py:15
  1156.5 17.3 multiply_add_fusion.10
  1177.2 359.5 %collective-permute-done = f32[4,1024,1024]{2,1,0:T(8,128)} collective-permute-done((f32[4,1024,1024]{2,1,0:T(8,128)}, f32[4,1024,1024]{2,1,0:T(8,128)}, u32[]{:S(2)}, u32[]{:S(2)}) %collective-permute-start) | collective-permute-done | bytes 16777248 | tf_op jit(solution)/shard_map/while/body/eval_jaxpr/ppermute | solution.py:15
  1536.6 9.3 convert_element_type.160
  1546.7 22.0 fusion.1
  1568.7 12.2 fusion.143
  1591.2 21.5 fusion
  1612.7 18.2 fusion.4
  1630.9 7.9 broadcast.160
  1638.8 1134.9 %while.25 = (s32[]{:T(128)}, f32[4,1024,1024]{2,1,0:T(8,128)}, f32[4,1,1]{0,2,1:T(1,128)S(1)}, f32[4,1024,1024]{2,1,0:T(8,128)}, s32[]{:T(128)}) while((s32[]{:T(128)}, f32[4,1024,1024]{2,1,0:T(8,128)}, f32[4,1,1]{0,2,1:T(1,128)S(1)}, f32[4,1024,1024]{2,1,0:T(8,128)}, s32[]{:T(128)}) %tuple.134), condition=%wide.region_11.12_spmd, body=%wide.region_10.11_spmd.sunk | while | flops 8388610 | bytes 117440624 | solution.py:210
  1638.8 17.3 multiply_add_fusion.11
  1658.6 359.5 %collective-permute-done.1 = f32[4,1024,1024]{2,1,0:T(8,128)} collective-permute-done((f32[4,1024,1024]{2,1,0:T(8,128)}, f32[4,1024,1024]{2,1,0:T(8,128)}, u32[]{:S(2)}, u32[]{:S(2)}) %collective-permute-start.1) | collective-permute-done | bytes 16777248 | tf_op jit(solution)/shard_map/while/body/eval_jaxpr/ppermute | solution.py:15
  2018.0 17.3 multiply_add_fusion.11
  2037.8 358.6 %collective-permute-done.1 = f32[4,1024,1024]{2,1,0:T(8,128)} collective-permute-done((f32[4,1024,1024]{2,1,0:T(8,128)}, f32[4,1024,1024]{2,1,0:T(8,128)}, u32[]{:S(2)}, u32[]{:S(2)}) %collective-permute-start.1) | collective-permute-done | bytes 16777248 | tf_op jit(solution)/shard_map/while/body/eval_jaxpr/ppermute | solution.py:15
  2396.3 17.3 multiply_add_fusion.11
  2416.1 357.6 %collective-permute-done.1 = f32[4,1024,1024]{2,1,0:T(8,128)} collective-permute-done((f32[4,1024,1024]{2,1,0:T(8,128)}, f32[4,1024,1024]{2,1,0:T(8,128)}, u32[]{:S(2)}, u32[]{:S(2)}) %collective-permute-start.1) | collective-permute-done | bytes 16777248 | tf_op jit(solution)/shard_map/while/body/eval_jaxpr/ppermute | solution.py:15
  2773.7 12.8 multiply_reduce_fusion
  2786.6 14.3 fusion.39
  2800.9 18.8 fusion.36
  2900.5 7.9 fusion.63
  2934.8 8.3 fusion.66
  2956.3 20.6 multiply_reduce_fusion.1
  2977.0 11.3 convolution_convert_fusion.1
  3002.0 10.1 broadcast_multiply_fusion.1
  3012.1 7.9 pad_add_fusion.1
  3051.7 17.8 convolution_convert_fusion
  3071.1 8.2 fusion.81
  3079.4 9.0 fusion.84
  3088.4 9.7 fusion.87
  3106.4 11.2 fusion.2
  3118.6 193.5 %reduce-scatter.3.cloned.1.call-done = bf16[256,8192]{1,0:T(8,128)(2,1)} async-done(((bf16[2048,8192]{1,0:T(8,128)(2,1)}), bf16[256,8192]{1,0:T(8,128)(2,1)}) %reduce-scatter.3.cloned.1.call-update) | async-done | bytes 4194320 | tf_op jit(solution)/shard_map/reduce_scatter | solution.py:245
  3312.3 12.7 fusion.53
  3325.0 15.6 fusion.71
  3341.6 40.7 %all-reduce.15 = (f32[2048]{0:T(1024)}, f32[4096]{0:T(1024)}, f32[8]{0:T(128)}, f32[4096]{0:T(1024)}, f32[4096]{0:T(1024)}) all-reduce(f32[2048]{0:T(1024)S(1)} %get-tuple-element.147, f32[4096]{0:T(1024)S(1)} %get-tuple-element.193, f32[8]{0:T(128)S(1)} %fusion.106, ...), channel_id=1, replica_groups=mesh['dp'=8,'ctx'=4] {'dp','ctx'}, use_global_device_ids=true, to_apply=%region_25.26 | all-reduce | flops 14344 | bytes 114752 | tf_op jit(solution)/shard_map/psum | solution.py:266
  3385.6 95.9 %all-reduce.21.cloned.1.call-done = (f32[4,4096]{1,0:T(4,128)}, f32[3,4,4,4,256]{2,3,4,1,0:T(4,128)}, f32[8,12288]{1,0:T(8,128)}) async-done(((f32[4,4096]{1,0:T(4,128)}, f32[3,4,4,4,256]{2,3,4,1,0:T(4,128)}, f32[8,12288]{1,0:T(8,128)}), (f32[4,4096]{1,0:T(4,128)}, f32[3,4,4,4,256]{2,3,4,1,0:T(4,128)}, f32[8,12288]{1,0:T(8,128)})) %all-reduce.21.cloned.1.call-update) | async-done | bytes 655376 | tf_op jit(solution)/shard_map/psum | solution.py:266
  3487.6 218.6 %all-reduce.23.cloned.1.call-done = (bf16[256,8192]{1,0:T(8,128)(2,1)}, bf16[512,2048]{1,0:T(8,128)(2,1)}) async-done(((bf16[256,8192]{1,0:T(8,128)(2,1)}, bf16[512,2048]{1,0:T(8,128)(2,1)}), (bf16[256,8192]{1,0:T(8,128)(2,1)}, bf16[512,2048]{1,0:T(8,128)(2,1)})) %all-reduce.23.cloned.1.call-update) | async-done | bytes 6291472 | tf_op jit(solution)/shard_map/psum | solution.py:263
  (335 shorter events, 317.7 us)
Async XLA Ops:
  7.2 320.2 %copy-start = (bf16[8,12288]{1,0:T(8,128)(2,1)S(1)}, bf16[8,12288]{1,0:T(8,128)(2,1)}, u32[]{:S(2)}) copy-start(bf16[8,12288]{1,0:T(8,128)(2,1)} %param.24) | copy-start | bytes 589828
  7.3 164.6 %all-gather.3.cloned.1.call-start = ((), (), s32[]{:S(2)}) async-start(), calls=%async_computation.2 | async-start | bytes 37748736 | tf_op jit(solution)/shard_map/all_gather | solution.py:154
  8.0 255.7 %all-gather.5.cloned.1.call-start = ((), (), s32[]{:S(2)}) async-start(), calls=%async_computation.3 | async-start | bytes 18874368 | tf_op jit(solution)/shard_map/all_gather | solution.py:188
  8.8 3109.9 %reduce-scatter.5.cloned.1.call-start = ((), (), s32[]{:S(2)}) async-start(), calls=%async_computation.5 | async-start | bytes 18874368 | tf_op jit(solution)/shard_map/reduce_scatter | solution.py:254
  10.0 181.2 %copy-start.50 = (f32[2048]{0:T(1024)}, f32[2048]{0:T(1024)S(1)}, u32[]{:S(2)}) copy-start(f32[2048]{0:T(1024)S(1)} %convert_element_type.143) | copy-start | bytes 24580
  10.0 253.7 %copy-start.71 = (f32[4096]{0:T(1024)}, f32[4096]{0:T(1024)S(1)}, u32[]{:S(2)}) copy-start(f32[4096]{0:T(1024)S(1)} %convert_element_type.162) | copy-start | bytes 49156
  14.3 194.2 %copy-start.36 = (bf16[1,4,4,4,256]{2,3,4,1,0:T(4,128)(2,1)}, bf16[1,4,4,4,256]{2,3,4,1,0:T(4,128)(2,1)S(1)}, u32[]{:S(2)}) copy-start(bf16[1,4,4,4,256]{2,3,4,1,0:T(4,128)(2,1)S(1)} %copy.127) | copy-start | bytes 98308
  14.5 176.7 %copy-start.57 = (f32[256]{0:T(256)}, f32[256]{0:T(256)S(1)}, u32[]{:S(2)}) copy-start(f32[256]{0:T(256)S(1)} %broadcast_multiply_fusion.6) | copy-start | bytes 3076
  15.0 176.2 %copy-start.59 = (f32[256]{0:T(256)}, f32[256]{0:T(256)S(1)}, u32[]{:S(2)}) copy-start(f32[256]{0:T(256)S(1)} %fusion.114) | copy-start | bytes 3076
  15.4 175.8 %copy-start.46 = (bf16[256,2048]{1,0:T(8,128)(2,1)}, bf16[256,2048]{1,0:T(8,128)(2,1)S(1)}, u32[]{:S(2)}) copy-start(bf16[256,2048]{1,0:T(8,128)(2,1)S(1)} %fusion.57) | copy-start | bytes 3145732
  16.4 263.4 %copy-start.61 = (f32[1,4096]{1,0:T(1,128)}, f32[1,4096]{1,0:T(1,128)S(1)}, u32[]{:S(2)}) copy-start(f32[1,4096]{1,0:T(1,128)S(1)} %get-tuple-element.212) | copy-start | bytes 49156
  16.4 263.4 %copy-start.63 = (f32[1,4096]{1,0:T(1,128)}, f32[1,4096]{1,0:T(1,128)S(1)}, u32[]{:S(2)}) copy-start(f32[1,4096]{1,0:T(1,128)S(1)} %get-tuple-element.213) | copy-start | bytes 49156
  16.4 263.4 %copy-start.65 = (f32[1,4096]{1,0:T(1,128)}, f32[1,4096]{1,0:T(1,128)S(1)}, u32[]{:S(2)}) copy-start(f32[1,4096]{1,0:T(1,128)S(1)} %get-tuple-element.214) | copy-start | bytes 49156
  16.5 263.4 %copy-start.67 = (f32[1,4096]{1,0:T(1,128)}, f32[1,4096]{1,0:T(1,128)S(1)}, u32[]{:S(2)}) copy-start(f32[1,4096]{1,0:T(1,128)S(1)} %get-tuple-element.215) | copy-start | bytes 49156
  192.7 87.1 %collective-permute-start.2 = (bf16[3,4096]{1,0:T(4,128)(2,1)}, bf16[3,4096]{1,0:T(4,128)(2,1)S(1)}, u32[]{:S(2)}, u32[]{:S(2)}) collective-permute-start(bf16[3,4096]{1,0:T(4,128)(2,1)} %slice.91), channel_id=1, source_target_pairs={{0,1},{1,2},{2,3},{4,5},{5,6},{6,7},{8,9},{9,10},{10,11},{12,13},{... | collective-permute-start | bytes 73736 | tf_op jit(solution)/shard_map/ppermute | solution.py:15
  209.8 53.9 %copy-start.47 = (bf16[1,256,2048]{2,1,0:T(8,128)(2,1)S(1)}, bf16[1,256,2048]{2,1,0:T(8,128)(2,1)}, u32[]{:S(2)}) copy-start(bf16[1,256,2048]{2,1,0:T(8,128)(2,1)} %param.29) | copy-start | bytes 3145732
  209.8 53.9 %copy-start.86 = (f32[256]{0:T(256)S(1)}, f32[256]{0:T(256)}, u32[]{:S(2)}) copy-start(f32[256]{0:T(256)} %compare_convert_fusion) | copy-start | bytes 3076
  353.1 1215.6 %copy-start.45 = (bf16[4,256,256]{2,1,0:T(8,128)(2,1)}, bf16[4,256,256]{2,1,0:T(8,128)(2,1)S(1)}, u32[]{:S(2)}) copy-start(bf16[4,256,256]{2,1,0:T(8,128)(2,1)S(1)} %get-tuple-element.229) | copy-start | bytes 1572868
  353.4 32.1 copy-start.26
  410.8 364.6 %collective-permute-start = (f32[4,1024,1024]{2,1,0:T(8,128)}, f32[4,1024,1024]{2,1,0:T(8,128)}, u32[]{:S(2)}, u32[]{:S(2)}) collective-permute-start(f32[4,1024,1024]{2,1,0:T(8,128)} %multiply_add_fusion.10), channel_id=1, source_target_pairs={{0,1},{1,2},{2,3},{4,5},{5,6},{6,7},{8,9},{9,10},{10,11},{12,13},{... | collective-permute-start | bytes 50331656 | tf_op jit(solution)/shard_map/while/body/eval_jaxpr/ppermute | solution.py:15
  792.7 363.8 %collective-permute-start = (f32[4,1024,1024]{2,1,0:T(8,128)}, f32[4,1024,1024]{2,1,0:T(8,128)}, u32[]{:S(2)}, u32[]{:S(2)}) collective-permute-start(f32[4,1024,1024]{2,1,0:T(8,128)} %multiply_add_fusion.10), channel_id=1, source_target_pairs={{0,1},{1,2},{2,3},{4,5},{5,6},{6,7},{8,9},{9,10},{10,11},{12,13},{... | collective-permute-start | bytes 50331656 | tf_op jit(solution)/shard_map/while/body/eval_jaxpr/ppermute | solution.py:15
  1173.8 362.8 %collective-permute-start = (f32[4,1024,1024]{2,1,0:T(8,128)}, f32[4,1024,1024]{2,1,0:T(8,128)}, u32[]{:S(2)}, u32[]{:S(2)}) collective-permute-start(f32[4,1024,1024]{2,1,0:T(8,128)} %multiply_add_fusion.10), channel_id=1, source_target_pairs={{0,1},{1,2},{2,3},{4,5},{5,6},{6,7},{8,9},{9,10},{10,11},{12,13},{... | collective-permute-start | bytes 50331656 | tf_op jit(solution)/shard_map/while/body/eval_jaxpr/ppermute | solution.py:15
  1568.7 12.2 copy-start.17
  1587.1 25.6 copy-start.14
  1656.1 361.9 %collective-permute-start.1 = (f32[4,1024,1024]{2,1,0:T(8,128)}, f32[4,1024,1024]{2,1,0:T(8,128)}, u32[]{:S(2)}, u32[]{:S(2)}) collective-permute-start(f32[4,1024,1024]{2,1,0:T(8,128)} %multiply_add_fusion.11), channel_id=1, source_target_pairs={{1,0},{2,1},{3,2},{5,4},{6,5},{7,6},{9,8},{10,9},{11,10},{13,12},{... | collective-permute-start | bytes 50331656 | tf_op jit(solution)/shard_map/while/body/eval_jaxpr/ppermute | solution.py:15
  2035.3 361.0 %collective-permute-start.1 = (f32[4,1024,1024]{2,1,0:T(8,128)}, f32[4,1024,1024]{2,1,0:T(8,128)}, u32[]{:S(2)}, u32[]{:S(2)}) collective-permute-start(f32[4,1024,1024]{2,1,0:T(8,128)} %multiply_add_fusion.11), channel_id=1, source_target_pairs={{1,0},{2,1},{3,2},{5,4},{6,5},{7,6},{9,8},{10,9},{11,10},{13,12},{... | collective-permute-start | bytes 50331656 | tf_op jit(solution)/shard_map/while/body/eval_jaxpr/ppermute | solution.py:15
  2413.6 360.1 %collective-permute-start.1 = (f32[4,1024,1024]{2,1,0:T(8,128)}, f32[4,1024,1024]{2,1,0:T(8,128)}, u32[]{:S(2)}, u32[]{:S(2)}) collective-permute-start(f32[4,1024,1024]{2,1,0:T(8,128)} %multiply_add_fusion.11), channel_id=1, source_target_pairs={{1,0},{2,1},{3,2},{5,4},{6,5},{7,6},{9,8},{10,9},{11,10},{13,12},{... | collective-permute-start | bytes 50331656 | tf_op jit(solution)/shard_map/while/body/eval_jaxpr/ppermute | solution.py:15
  2773.7 12.8 copy-start.2
  2773.7 12.8 copy-start.27
  2773.7 12.9 copy-start.55
  2786.6 14.3 copy-start.12
  2863.3 11.6 copy-start.83
  2956.3 20.7 copy-start.48
  2956.3 20.6 copy-start.87
  2977.0 11.3 copy-start.34
  2988.3 323.9 %reduce-scatter.3.cloned.1.call-start = ((), (), s32[]{:S(2)}) async-start(), calls=%async_computation.4 | async-start | bytes 37748736 | tf_op jit(solution)/shard_map/reduce_scatter | solution.py:245
  3012.1 12.6 copy-start.22
  3022.0 23.5 collective-permute-start.3
  3069.5 412.0 %all-reduce.21.cloned.1.call-start = ((), (), s32[]{:S(2)}) async-start(), calls=%async_computation.6 | async-start | bytes 13500416 | tf_op jit(solution)/shard_map/psum | solution.py:266
  3088.4 17.5 copy-start.79
  3088.4 17.5 copy-start.81
  3106.4 11.2 copy-start.74
  3118.4 193.9 %copy-start.35 = (bf16[256,4096]{1,0:T(8,128)(2,1)S(1)}, bf16[256,4096]{1,0:T(8,128)(2,1)}, u32[]{:S(2)}) copy-start(bf16[256,4096]{1,0:T(8,128)(2,1)} %copy-done.34) | copy-start | bytes 6291460
  3118.4 193.9 %copy-start.88 = (f32[256]{0:T(256)S(1)}, f32[256]{0:T(256)}, u32[]{:S(2)}) copy-start(f32[256]{0:T(256)} %compare_convert_fusion) | copy-start | bytes 3076
  3118.4 587.9 %all-reduce.23.cloned.1.call-start = ((), (), s32[]{:S(2)}) async-start(), calls=%async_computation.7 | async-start | bytes 12582912 | tf_op jit(solution)/shard_map/psum | solution.py:263
  3312.3 12.7 copy-start.43
  3312.3 12.7 copy-start.44
  3325.0 15.6 copy-start.90
  (63 other events, 351.9 us)
Sparse Core Ops, SparseCore 0:
  10.0 161.8 all-gather.2
  173.8 89.8 all-gather.4
  2988.4 115.0 reduce-scatter.4
  3106.9 205.2 reduce-scatter.2
  3319.8 161.6 all-reduce.20
  3484.0 222.2 all-reduce.22
where the time goes:
time: 3730 us; the launch traced here: 3720 us
  waiting for transfers between devices  2870 us (77%)
  matrix products  347 us (9%)
  other arithmetic  244 us (7%)
  local copies, waits for them, and re-layouts  180 us (5%)
  blocking collectives  40.7 us (1%)
    ppermute x8, waiting for transfers between devices, shifted(): return lax.ppermute(x, axis, pairs)  2160 us
    psum x1, waiting for transfers between devices, on_device(): lax.psum(up_part, 'ctx').astype(jnp.float32)  219 us
    reduce_scatter x1, waiting for transfers between devices, on_device(): lax.psum_scatter(lax.dot_general(columns, upward_grad, contract_first, pr...  194 us
    all_gather x1, waiting for transfers between devices, on_device(): lax.all_gather(up_weight, 'dp', axis=0, tiled=True)  155 us
    psum x1, waiting for transfers between devices, on_device(): lax.psum((norm_scale_grad, conv_taps_grad, conv_shift_grad, qkv_grad, gat...  95.9 us
  transfers between devices with their start and end apart: 14, of which 11 were waited for; matrix products, arithmetic and copies ran while one was open for 6% of the time, Pallas kernels for 0%

commit v1 on v0

v1 whole, which is shorter than its diff:
```python
from functools import partial

import jax
import jax.numpy as jnp
from jax import lax
from jax.experimental import pallas as pl
from jax.experimental.pallas import tpu as pltpu
from jax.sharding import PartitionSpec as P

epsilon = 1e-05
f32 = jnp.float32
bf16 = jnp.bfloat16


def dot_nn(a, b):
    return lax.dot_general(a, b, (((1,), (0,)), ((), ())), preferred_element_type=f32)


def dot_nt(a, b):
    return lax.dot_general(a, b, (((1,), (1,)), ((), ())), preferred_element_type=f32)


def dot_tn(a, b):
    return lax.dot_general(a, b, (((0,), (0,)), ((), ())), preferred_element_type=f32)


def normalize(rows):
    centred = rows - jnp.mean(rows, axis=-1, keepdims=True)
    scale = lax.rsqrt(jnp.mean(centred * centred, axis=-1, keepdims=True) + epsilon)
    return centred * scale, scale


def normalize_back(grad, normed, scale):
    return scale * (
        grad
        - jnp.mean(grad, axis=-1, keepdims=True)
        - normed * jnp.mean(grad * normed, axis=-1, keepdims=True)
    )


def silu_parts(x):
    sig = jax.nn.sigmoid(x)
    return sig, x * sig


def fold8(x):
    rows = x.shape[0]
    out = x[0:8]
    for at in range(8, rows, 8):
        out = out + x[at : at + 8]
    return out


def whole(shape):
    return pl.BlockSpec(shape, lambda *g: (0,) * len(shape), pipeline_mode=pl.Buffered(1))


def call(kernel, place, grid, in_specs, out_specs, out_shape, scratch, estimate, name, *args):
    return pl.pallas_call(
        kernel,
        grid_spec=pltpu.PrefetchScalarGridSpec(
            num_scalar_prefetch=1,
            grid=(grid,),
            in_specs=in_specs,
            out_specs=out_specs,
            scratch_shapes=scratch,
        ),
        out_shape=out_shape,
        compiler_params=kernel_params(),
        cost_estimate=estimate,
        name=name,
    )(place, *args)


def kernel_params(limit=48):
    return pltpu.CompilerParams(
        dimension_semantics=("arbitrary",), vmem_limit_bytes=limit * 1024 * 1024
    )


def cost(flops, moved, transcendentals=0):
    return pl.CostEstimate(
        flops=int(flops), bytes_accessed=int(moved), transcendentals=int(transcendentals)
    )


def row_chunks(rows, size, body, together=1):
    def step(n, carry):
        for m in range(together):
            body(pl.multiple_of((n * together + m) * size, size))
        return carry

    lax.fori_loop(0, rows // (size * together), step, 0)


def front_kernel(
    key_scale, at_ref, mix_ref, prev_ref, taps_ref, shift_ref, maps_ref, gates_ref,
    pre_ref, q_ref, k_ref, v_ref, part_ref, pad_ref,
):
    rows, width = mix_ref.shape
    taps = taps_ref.shape[0]
    lanes = maps_ref.shape[1]
    block = width // lanes
    first = pl.program_id(0) == 0
    before = prev_ref[...].astype(f32)[prev_ref.shape[0] - 8 :]
    pad_ref[0:8, :] = jnp.where(first, jnp.zeros_like(before), before)
    pad_ref[8 : 8 + rows, :] = mix_ref[...].astype(f32)

    def chunk(at):
        size = 16
        conv, mixed = [], []
        for i in range(block):
            cols = slice(i * lanes, (i + 1) * lanes)
            x = pad_ref[pl.ds(at, size + 8), cols]
            pre = shift_ref[:, cols]
            for j in range(taps):
                lag = taps - 1 - j
                pre = pre + taps_ref[j : j + 1, cols] * x[8 - lag : 8 - lag + size]
            pre_ref[pl.ds(at, size), cols] = pre
            conv.append(silu_parts(pre)[1])
            mixed.append(x[8:])

        def mapped(m, parts, o):
            out = parts[0] * maps_ref[m * block * block + o : m * block * block + o + 1, :]
            for i in range(1, block):
                r = (m * block + i) * block + o
                out = out + parts[i] * maps_ref[r : r + 1, :]
            return out

        for o in range(block):
            cols = slice(o * lanes, (o + 1) * lanes)
            q_ref[pl.ds(at, size), cols] = mapped(0, conv, o).astype(bf16)
            k_ref[pl.ds(at, size), cols] = (mapped(1, conv, o) * key_scale).astype(bf16)
            v_ref[pl.ds(at, size), cols] = mapped(2, mixed, o).astype(bf16)

    row_chunks(rows, 16, chunk)
    part_ref[...] = (
        dot_nt(gates_ref[0], q_ref[...])
        + dot_nt(gates_ref[1], k_ref[...])
        + dot_nt(gates_ref[2], v_ref[...])
    )


def front(place, mixer, conv_taps, conv_shift, maps, gate_rows, key_scale, span):
    total, width = mixer.shape
    count = total // span
    step = span // 16

    def own(i, at):
        return (lax.rem(i + count - at[0], count), 0)

    def ahead(i, at):
        return (lax.rem(i + count - 1 - at[0] + count, count) * step + step - 1, 0)

    tile = pl.BlockSpec((span, width), lambda i, at: (i, 0))
    gates_of = gate_rows.shape[1]
    return call(
        partial(front_kernel, key_scale),
        place,
        count,
        [
            pl.BlockSpec((span, width), own),
            pl.BlockSpec((16, width), ahead),
            whole(conv_taps.shape),
            whole(conv_shift.shape),
            whole(maps.shape),
            whole(gate_rows.shape),
        ],
        [tile, tile, tile, tile, pl.BlockSpec((gates_of, span), lambda i, at: (0, i))],
        [
            jax.ShapeDtypeStruct((total, width), f32),
            *[jax.ShapeDtypeStruct((total, width), bf16)] * 3,
            jax.ShapeDtypeStruct((gates_of, total), f32),
        ],
        [pltpu.VMEM((span + 8, width), f32)],
        cost(6e9, 12 * total * width, total * width),
        "front",
        mixer, mixer, conv_taps, conv_shift, maps, gate_rows,
    )


def gates_kernel(span, share, head_ref, *refs):
    parts, bias_ref, out_ref = refs[:-2], refs[-2], refs[-1]
    pre = parts[0][...]
    for p in parts[1:]:
        pre = pre + p[...]
    if share != 1.0:
        pre = pre * share
    pre = pre + bias_ref[...]
    rows, total = pre.shape
    head = head_ref[0]
    at = lax.broadcasted_iota(jnp.int32, pre.shape, 0)
    lane = lax.broadcasted_iota(jnp.int32, (8, total), 1)
    in_gate = jnp.sum(jnp.where(at == head, pre, 0.0), axis=0, keepdims=True)
    forget = jnp.sum(jnp.where(at == head + rows // 2, pre, 0.0), axis=0, keepdims=True)
    forget = jnp.broadcast_to(forget, (8, total))
    log_forget = jnp.minimum(forget, 0.0) - jnp.log1p(jnp.exp(-jnp.abs(forget)))
    place = lane % span
    running = log_forget
    by = 1
    while by < span:
        running = running + jnp.where(place >= by, pltpu.roll(running, by, 1), 0.0)
        by *= 2
    whole_sum = jnp.where(place == span - 1, running, 0.0)
    by = 1
    while by < span:
        whole_sum = whole_sum + pltpu.roll(whole_sum, total - by, 1) * jnp.where(
            place < span - by, 1.0, 0.0
        )
        by *= 2
    out_ref[0:1, :] = in_gate
    out_ref[1:2, :] = running[0:1]
    out_ref[2:3, :] = whole_sum[0:1]
    out_ref[3:4, :] = jax.nn.sigmoid(-forget)[0:1]
    out_ref[4:8, :] = jnp.zeros((4, total), f32)


def gates(head, parts, bias, span, share):
    rows, total = parts[0].shape
    full = pl.BlockSpec((rows, total), lambda i, s: (0, 0))
    return pl.pallas_call(
        partial(gates_kernel, span, share),
        grid_spec=pltpu.PrefetchScalarGridSpec(
            num_scalar_prefetch=1,
            grid=(1,),
            in_specs=[full] * len(parts) + [pl.BlockSpec((rows, 1), lambda i, s: (0, 0))],
            out_specs=pl.BlockSpec((8, total), lambda i, s: (0, 0)),
        ),
        out_shape=jax.ShapeDtypeStruct((8, total), f32),
        name="gates",
    )(head.reshape(1).astype(jnp.int32), *parts, bias)


def column_of(row):
    n = row.shape[1]
    eye = lax.broadcasted_iota(jnp.int32, (n, n), 0) == lax.broadcasted_iota(jnp.int32, (n, n), 1)
    return jnp.sum(jnp.where(eye, jnp.broadcast_to(row, (n, n)), 0.0), axis=1, keepdims=True)


def row_of(column):
    n = column.shape[0]
    eye = lax.broadcasted_iota(jnp.int32, (n, n), 0) == lax.broadcasted_iota(jnp.int32, (n, n), 1)
    return jnp.sum(jnp.where(eye, jnp.broadcast_to(column, (n, n)), 0.0), axis=0, keepdims=True)


def tile_weights(gate_ref, column, reach, lanes, n, causal):
    row = gate_ref[0:1, lanes] - gate_ref[1:2, lanes] + reach
    exponent = column + row
    if not causal:
        return jnp.exp(exponent)
    keep = lax.broadcasted_iota(jnp.int32, (n, n), 0) >= lax.broadcasted_iota(jnp.int32, (n, n), 1)
    return jnp.where(keep, jnp.exp(jnp.where(keep, exponent, 0.0)), 0.0)


def cell_kernel(
    at_ref, gate_ref, q_ref, k_ref, v_ref, pre_ref, gin_ref, skip_ref, og_ref,
    mix_ref, num_ref, hid_ref,
):
    n, width = q_ref.shape
    tb = pl.program_id(0)
    here = pl.ds(pl.multiple_of(tb * n, n), n)
    column = column_of(gate_ref[1:2, here])

    def one(sb, reach, causal):
        lanes = pl.ds(pl.multiple_of(sb * n, n), n)
        w = tile_weights(gate_ref, column, reach, lanes, n, causal)
        mix = (w * dot_nt(q_ref[...], k_ref[lanes, :])).astype(bf16)
        mix_ref[:, lanes] = mix
        return dot_nn(mix, v_ref[lanes, :])

    num_ref[...] = one(tb, jnp.zeros((1, n), f32), True)

    def earlier(step, reach):
        sb = tb - 1 - step
        reach = reach + gate_ref[2:3, pl.ds(pl.multiple_of(sb * n, n), n)]
        num_ref[...] += one(sb, reach, False)
        return reach

    lax.fori_loop(0, tb, earlier, jnp.zeros((1, n), f32))
    skip, og = skip_ref[...], og_ref[...]

    def chunk(at):
        rows = pl.ds(at, 16)
        hat, _ = normalize(num_ref[rows, :])
        conv = silu_parts(pre_ref[rows, :])[1]
        act = silu_parts(gin_ref[rows, :])[1]
        hid_ref[rows, :] = ((hat * og + skip * conv) * act).astype(bf16)

    row_chunks(n, 16, chunk, 4)


def cell(place, gate, q, k, v, pre, gate_in, skip, out_gain, span):
    total, width = q.shape
    count = total // span

    def own(i, at):
        return (lax.rem(i + count - at[0], count), 0)

    tile = pl.BlockSpec((span, width), lambda i, at: (i, 0))
    moved = pl.BlockSpec((span, width), own)
    full = whole((total, width))
    return call(
        cell_kernel,
        place,
        count,
        [whole(gate.shape), tile, full, full, tile, moved, whole(skip.shape), whole(out_gain.shape)],
        [pl.BlockSpec((span, total), lambda i, at: (i, 0)), tile, moved],
        [
            jax.ShapeDtypeStruct((total, total), bf16),
            jax.ShapeDtypeStruct((total, width), f32),
            jax.ShapeDtypeStruct((total, width), bf16),
        ],
        [],
        cost(2.5 * total * width * total, 20 * total * width, 3 * total * width),
        "cell",
        gate, q, k, v, pre, gate_in, skip, out_gain,
    )


def tail_back_kernel(
    at_ref, bg_ref, num_ref, pre_ref, gin_ref, down_ref, skip_ref, og_ref,
    ng_ref, gg_ref, ct_ref, sums_ref, hg_ref,
):
    hg_ref[...] = dot_nt(bg_ref[...], down_ref[...])

    @pl.when(pl.program_id(0) == 0)
    def _():
        sums_ref[...] = jnp.zeros_like(sums_ref)

    skip, og = skip_ref[...], og_ref[...]

    def chunk(at):
        rows = pl.ds(at, 16)
        hat, scale = normalize(num_ref[rows, :])
        conv = silu_parts(pre_ref[rows, :])[1]
        before = hat * og + skip * conv
        gin = gin_ref[rows, :]
        sig, act = silu_parts(gin)
        hg = hg_ref[rows, :]
        gg_ref[rows, :] = (hg * before * (sig * (1.0 + gin * (1.0 - sig)))).astype(bf16)
        bgrad = hg * act
        sums_ref[0:8, :] += fold8(bgrad * conv)
        sums_ref[8:16, :] += fold8(bgrad * hat)
        ct_ref[rows, :] = bgrad * skip
        ng_ref[rows, :] = normalize_back(bgrad * og, hat, scale).astype(bf16)

    row_chunks(hg_ref.shape[0], 16, chunk, 4)


def tail_back(place, bg, num, pre, gate_in, w_down, skip, out_gain, span):
    model = bg.shape[1]
    total, width = num.shape
    count = total // span

    def own(i, at):
        return (lax.rem(i + count - at[0], count), 0)

    tile = pl.BlockSpec((span, width), lambda i, at: (i, 0))
    moved = pl.BlockSpec((span, width), own)
    return call(
        tail_back_kernel,
        place,
        count,
        [
            pl.BlockSpec((span, model), own), tile, tile, moved,
            whole(w_down.shape), whole(skip.shape), whole(out_gain.shape),
        ],
        [tile, moved, tile, pl.BlockSpec((16, width), lambda i, at: (0, 0))],
        [
            jax.ShapeDtypeStruct((total, width), bf16),
            jax.ShapeDtypeStruct((total, width), bf16),
            jax.ShapeDtypeStruct((total, width), f32),
            jax.ShapeDtypeStruct((16, width), f32),
        ],
        [pltpu.VMEM((span, width), f32)],
        cost(2 * total * model * width, 24 * total * width, 2 * total * width),
        "tail_back",
        bg, num, pre, gate_in, w_down, skip, out_gain,
    )


def cell_back_kernel(
    gate_ref, q_ref, k_ref, v_ref, mix_ref, ng_ref,
    dq_ref, dk_ref, dv_ref, gout_ref, sums_ref,
):
    n, width = q_ref.shape
    total = k_ref.shape[0]
    tb = pl.program_id(0)
    here = pl.ds(pl.multiple_of(tb * n, n), n)
    column = column_of(gate_ref[1:2, here])

    @pl.when(tb == 0)
    def _():
        sums_ref[...] = jnp.zeros_like(sums_ref)

    def one(sb, reach, causal):
        lanes = pl.ds(pl.multiple_of(sb * n, n), n)
        w = tile_weights(gate_ref, column, reach, lanes, n, causal)
        mix = mix_ref[:, lanes]
        ng = ng_ref[...]
        mix_grad = dot_nt(ng, v_ref[lanes, :])
        exponent_grad = mix_grad * mix.astype(f32)
        scores_grad = (w * mix_grad).astype(bf16)
        sums_ref[0:1, lanes] += jnp.sum(exponent_grad, axis=0, keepdims=True)
        return (
            jnp.sum(exponent_grad, axis=1, keepdims=True),
            dot_nn(scores_grad, k_ref[lanes, :]),
            dot_tn(scores_grad, q_ref[...]),
            dot_tn(mix, ng),
            lanes,
        )

    by_row, dq, dk, dv, lanes = one(tb, jnp.zeros((1, n), f32), True)
    dq_ref[...] = dq
    dk_ref[lanes, :] = dk
    dv_ref[lanes, :] = dv

    def earlier(step, carry):
        reach, by_row = carry
        sb = tb - 1 - step
        reach = reach + gate_ref[2:3, pl.ds(pl.multiple_of(sb * n, n), n)]
        more, dq, dk, dv, lanes = one(sb, reach, False)
        dq_ref[...] += dq
        dk_ref[lanes, :] += dk
        dv_ref[lanes, :] += dv
        return reach, by_row + more

    _, by_row = lax.fori_loop(0, tb, earlier, (jnp.zeros((1, n), f32), by_row))
    sums_ref[1:2, here] = row_of(by_row)

    @pl.when(tb == pl.num_programs(0) - 1)
    def _():
        by_source = sums_ref[0:1, :]
        lane = lax.broadcasted_iota(jnp.int32, (8, total), 1)
        running = jnp.broadcast_to(sums_ref[1:2, :] - by_source, (8, total))
        by = 1
        while by < total:
            running = running + jnp.where(
                lane < total - by, pltpu.roll(running, total - by, 1), 0.0
            )
            by *= 2
        gout_ref[0:1, :] = by_source
        gout_ref[1:2, :] = running[0:1] * gate_ref[3:4, :]


def cell_back(gate, q, k, v, mix, num_grad, span):
    total, width = q.shape
    tile = pl.BlockSpec((span, width), lambda i: (i, 0))
    full = whole((total, width))
    return pl.pallas_call(
        cell_back_kernel,
        grid=(total // span,),
        in_specs=[
            whole(gate.shape), tile, full, full,
            pl.BlockSpec((span, total), lambda i: (i, 0)), tile,
        ],
        out_specs=[
            tile,
            pl.BlockSpec((total, width), lambda i: (0, 0)),
            pl.BlockSpec((total, width), lambda i: (0, 0)),
            pl.BlockSpec((2, total), lambda i: (0, 0)),
        ],
        out_shape=[
            *[jax.ShapeDtypeStruct((total, width), f32)] * 3,
            jax.ShapeDtypeStruct((2, total), f32),
        ],
        scratch_shapes=[pltpu.VMEM((8, total), f32)],
        compiler_params=kernel_params(),
        cost_estimate=cost(
            5 * total * total * width, 24 * total * width, total * total
        ),
        name="cell_back",
    )(gate, q, k, v, mix, num_grad)


def back_kernel(
    key_scale, heads, at_ref, dq_ref, dk_ref, dv_ref, q_ref, k_ref, v_ref, pre_ref, mix_ref, ct_ref,
    taps_ref, maps_ref, gates_ref, *refs,
):
    gate_parts, sums_ref = refs[:heads], refs[heads]
    mg_ref, pack_ref, tg_ref, wg_ref, grow_ref, gsum_ref, gb_ref, pg_ref, mv_ref = refs[heads + 1 :]
    rows, width = dq_ref.shape
    taps = taps_ref.shape[0]
    lanes = maps_ref.shape[1]
    block = width // lanes
    per_map = block * block

    @pl.when(pl.program_id(0) == 0)
    def _():
        tg_ref[...] = jnp.zeros_like(tg_ref)
        wg_ref[...] = jnp.zeros_like(wg_ref)
        grow_ref[...] = jnp.zeros_like(grow_ref)
        gsum_ref[...] = jnp.zeros_like(gsum_ref)
        pg_ref[rows : rows + 8, :] = jnp.zeros((8, width), f32)

    gg = jnp.concatenate([p[...] for p in gate_parts], axis=0)
    gsum_ref[...] += jnp.broadcast_to(jnp.sum(gg, axis=1, keepdims=True), gsum_ref.shape)
    high = gg.astype(bf16)
    low = (gg - high.astype(f32)).astype(bf16)
    for m, x_ref in enumerate((q_ref, k_ref, v_ref)):
        gb_ref[m] = dot_tn(high, gates_ref[m]) + dot_tn(low, gates_ref[m])
        grow_ref[m] += dot_nn(high, x_ref[...]) + dot_nn(low, x_ref[...])

    size = 16

    def chunk(at):
        here = pl.ds(at, size)

        def cols(i):
            return slice(i * lanes, (i + 1) * lanes)

        def weight(m, i, o):
            r = (m * block + i) * block + o
            return maps_ref[r : r + 1, :]

        pre = [pre_ref[here, cols(i)] for i in range(block)]
        parts = [silu_parts(p) for p in pre]
        conv_grad = [ct_ref[here, cols(i)] for i in range(block)]
        for m, (g_ref, scale) in enumerate(((dq_ref, None), (dk_ref, key_scale))):
            for o in range(block):
                g = g_ref[here, cols(o)] + gb_ref[m, here, cols(o)]
                if scale is not None:
                    g = g * scale
                for i in range(block):
                    conv_grad[i] = conv_grad[i] + g * weight(m, i, o)
                    wg_ref[m * per_map + i * block + o] += fold8(parts[i][1] * g)
        for i in range(block):
            sig = parts[i][0]
            pg_ref[here, cols(i)] = conv_grad[i] * (sig * (1.0 + pre[i] * (1.0 - sig)))
        mixed = [mix_ref[here, cols(i)].astype(f32) for i in range(block)]
        grads = [None] * block
        for o in range(block):
            g = dv_ref[here, cols(o)] + gb_ref[2, here, cols(o)]
            for i in range(block):
                term = g * weight(2, i, o)
                grads[i] = term if grads[i] is None else grads[i] + term
                wg_ref[2 * per_map + i * block + o] += fold8(mixed[i] * g)
        for i in range(block):
            mv_ref[here, cols(i)] = grads[i]

    row_chunks(rows, size, chunk)

    def second(at):
        here = pl.ds(at, size)
        for i in range(block):
            cols = slice(i * lanes, (i + 1) * lanes)
            x = pg_ref[pl.ds(at, size + 8), cols]
            m = mix_ref[here, cols].astype(f32)
            grad = mv_ref[here, cols]
            for j in range(taps):
                lead = taps - 1 - j
                moved = x[lead : lead + size]
                grad = grad + taps_ref[j : j + 1, cols] * moved
                tg_ref[j, :, cols] += fold8(moved * m)
            tg_ref[taps, :, cols] += fold8(x[0:size])
            mg_ref[here, cols] = grad.astype(bf16)

    row_chunks(rows, size, second)
    pg_ref[rows : rows + 8, :] = pg_ref[0:8, :]

    @pl.when(pl.program_id(0) == pl.num_programs(0) - 1)
    def _():
        pack_ref[...] = jnp.zeros_like(pack_ref)
        at = 0
        for j in range(taps + 1):
            pack_ref[at : at + 1, :] = jnp.sum(tg_ref[j], axis=0, keepdims=True)
            at += 1
        for r in range(3 * block):
            for o in range(block):
                pack_ref[at : at + 1, o * lanes : (o + 1) * lanes] = jnp.sum(
                    wg_ref[r * block + o], axis=0, keepdims=True
                )
            at += 1
        for m in range(3):
            pack_ref[at : at + 2 * heads, :] = grow_ref[m]
            at += 2 * heads
        for j in range(2):
            pack_ref[at : at + 1, :] = jnp.sum(sums_ref[8 * j : 8 * j + 8], axis=0, keepdims=True)
            at += 1
        sums = gsum_ref[...]
        diagonal = lax.broadcasted_iota(jnp.int32, sums.shape, 0) == lax.broadcasted_iota(
            jnp.int32, sums.shape, 1
        )
        pack_ref[at : at + 1, 0:128] = jnp.sum(
            jnp.where(diagonal, sums, 0.0), axis=0, keepdims=True
        )


def back(
    place, dq, dk, dv, gate_parts, q, k, v, pre, mixer, conv_tail, conv_taps, maps, gate_rows,
    tail_sums, key_scale, span, pack_rows,
):
    total, width = dq.shape
    count = total // span
    taps = conv_taps.shape[0]
    lanes = maps.shape[1]
    heads = len(gate_parts)

    def own(i, at):
        return (lax.rem(2 * count - 1 - i - at[0], count), 0)

    tile = pl.BlockSpec((span, width), lambda i, at: (count - 1 - i, 0))
    moved = pl.BlockSpec((span, width), own)
    return call(
        partial(back_kernel, key_scale, heads),
        place,
        count,
        [
            tile, tile, tile, tile, tile, tile, tile, moved, tile,
            whole(conv_taps.shape), whole(maps.shape), whole(gate_rows.shape),
            *[pl.BlockSpec((2, span), lambda i, at: (0, count - 1 - i))] * heads,
            whole(tail_sums.shape),
        ],
        [moved, pl.BlockSpec((pack_rows, width), lambda i, at: (0, 0))],
        [
            jax.ShapeDtypeStruct((total, width), bf16),
            jax.ShapeDtypeStruct((pack_rows, width), f32),
        ],
        [
            pltpu.VMEM((taps + 1, 8, width), f32),
            pltpu.VMEM((maps.shape[0], 8, lanes), f32),
            pltpu.VMEM(gate_rows.shape, f32),
            pltpu.VMEM((2 * heads, 128), f32),
            pltpu.VMEM((3, span, width), f32),
            pltpu.VMEM((span + 8, width), f32),
            pltpu.VMEM((span, width), f32),
        ],
        cost(12e9, 30 * total * width, 2 * total * width),
        "back",
        dq, dk, dv, q, k, v, pre, mixer, conv_tail, conv_taps, maps, gate_rows, *gate_parts,
        tail_sums,
    )


def assemble_kernel(count, at_ref, *refs):
    out_ref = refs[-1]
    inputs = refs[:-1]
    step = pl.program_id(0)
    halves = len(inputs) // (2 * count - 1)
    for half in range(halves):
        own, others = inputs[half * (2 * count - 1)], inputs[half * (2 * count - 1) + 1 : (half + 1) * (2 * count - 1)]
        at = half * count

        @pl.when(step == at)
        def _(ref=own):
            out_ref[...] = ref[...].astype(f32)

        for r in range(1, count):
            ahead, behind = others[2 * (r - 1)], others[2 * (count - r - 1) + 1]

            @pl.when((step == at + r) & (at_ref[0] + r < count))
            def _(ref=ahead):
                out_ref[...] = ref[...].astype(f32)

            @pl.when((step == at + r) & (at_ref[0] + r >= count))
            def _(ref=behind):
                out_ref[...] = ref[...].astype(f32)


def flat(own, hops):
    return [own] + [x for pair in hops for x in pair]


def assemble(place, own_mix, mix_hops, own_gate, gate_hops, copies):
    rows, width = own_mix.shape
    count = len(mix_hops) + 1
    heads = count // copies

    def out_map(i, at):
        half = i // count
        source = lax.rem(i - half * count + at[0], count)
        return (0, half * heads + source // copies)

    parts = flat(own_mix, mix_hops) + flat(own_gate, gate_hops)
    return call(
        partial(assemble_kernel, count),
        place,
        2 * count,
        [whole((rows, width))] * len(parts),
        pl.BlockSpec((rows, width), out_map),
        jax.ShapeDtypeStruct((rows, 2 * heads * width), f32),
        [],
        cost(0, 12 * count * rows * width),
        "assemble",
        *parts,
    )


def assemble_rows(place, own, hops):
    rows, width = own.shape
    count = len(hops) + 1
    parts = flat(own, hops)
    return call(
        partial(assemble_kernel, count),
        place,
        count,
        [whole((rows, width))] * len(parts),
        pl.BlockSpec((rows, width), lambda i, at: (lax.rem(i + at[0], count), 0)),
        jax.ShapeDtypeStruct((count * rows, width), f32),
        [],
        cost(0, 6 * count * rows * width),
        "assemble_rows",
        *parts,
    )


def mix_grads_kernel(x_ref, g_ref, w_ref, gain_ref, pack_ref, out_ref):
    rows = x_ref.shape[1]
    grad = dot_tn(x_ref[...], g_ref[...])
    out_ref[0, :rows, :] = grad.astype(bf16)
    gain = row_of(jnp.sum(grad * w_ref[...].astype(f32), axis=1, keepdims=True)) + gain_ref[0]
    width = out_ref.shape[2]
    extra = out_ref.shape[1] - rows
    pack = pack_ref[0]
    parts = [pack, jnp.concatenate([gain, jnp.zeros((1, width - rows), f32)], axis=1)]
    fill = extra - pack.shape[0] - 1
    if fill:
        parts.append(jnp.zeros((fill, width), f32))
    out_ref[0, rows:, :] = jnp.concatenate(parts, axis=0).astype(bf16)


def mix_grads(normed, mixer_grad, w_mix, gain_part, pack, dp):
    total, width = normed.shape
    cols = mixer_grad.shape[1]
    rows = width // dp
    pack = pack.reshape(dp, pack.shape[0] // dp, cols)
    extra = -(-(pack.shape[1] + 1) // 16) * 16
    return pl.pallas_call(
        mix_grads_kernel,
        grid=(dp,),
        in_specs=[
            pl.BlockSpec((total, rows), lambda i: (0, i)),
            whole(mixer_grad.shape),
            pl.BlockSpec((rows, cols), lambda i: (i, 0)),
            pl.BlockSpec((1, 1, rows), lambda i: (i, 0, 0)),
            pl.BlockSpec((1,) + pack.shape[1:], lambda i: (i, 0, 0)),
        ],
        out_specs=pl.BlockSpec((1, rows + extra, cols), lambda i: (i, 0, 0)),
        out_shape=jax.ShapeDtypeStruct((dp, rows + extra, cols), bf16),
        compiler_params=kernel_params(),
        cost_estimate=cost(2 * total * width * cols, 2 * (total * width + 3 * width * cols)),
        name="mix_grads",
    )(normed, mixer_grad, w_mix, gain_part.reshape(dp, 1, rows), pack)


def unpack_kernel(per, taps, heads, block, x_ref, gain_ref, norm_ref, convw_ref, convb_ref, maps_ref, gates_ref, bias_ref, skip_ref, og_ref):
    copies = x_ref.shape[0] // heads
    dp = x_ref.shape[1]
    width = x_ref.shape[3]
    lanes = width // block
    inner = heads * width
    rows = norm_ref.shape[1] // dp

    def row(h, r):
        return x_ref[h * copies, r // per, r % per : r % per + 1, :]

    for d in range(dp):
        total = x_ref[0, d, per : per + 1, 0:rows]
        for h in range(1, heads):
            total = total + x_ref[h * copies, d, per : per + 1, 0:rows]
        norm_ref[:, d * rows : (d + 1) * rows] = total / gain_ref[:, d * rows : (d + 1) * rows]
    for h in range(heads):
        cols = slice(h * width, (h + 1) * width)
        for j in range(taps):
            convw_ref[j : j + 1, cols] = row(h, j)
        convb_ref[:, cols] = row(h, taps)
        at = taps + 1
        for m in range(3):
            for i in range(block):
                values = row(h, at)
                for o in range(block):
                    maps_ref[m, h, i, o : o + 1, :] = values[:, o * lanes : (o + 1) * lanes]
                at += 1
        for m in range(3):
            for j in range(heads):
                for p in range(2):
                    g = p * heads + (h + j) % heads
                    start = m * inner + h * width
                    gates_ref[g : g + 1, start : start + width] = row(h, at)
                    at += 1
        skip_ref[:, cols] = row(h, at)
        og_ref[:, cols] = row(h, at + 1)
        if h == 0:
            bias_ref[...] = row(h, at + 2)[:, 0:128]


def unpack(small, gain, taps, heads, block):
    per, width = small.shape[2] - 1, small.shape[3]
    inner = heads * width
    shapes = [
        gain.shape, (taps, inner), (1, inner), (3, heads, block, block, width // block),
        (2 * heads, 3 * inner), (1, 128), (1, inner), (1, inner),
    ]
    return pl.pallas_call(
        partial(unpack_kernel, per, taps, heads, block),
        grid=(1,),
        in_specs=[whole(small.shape), whole(gain.shape)],
        out_specs=[pl.BlockSpec(x, lambda i, n=len(x): (0,) * n) for x in shapes],
        out_shape=[jax.ShapeDtypeStruct(x, f32) for x in shapes],
        compiler_params=kernel_params(),
        name="unpack",
    )(small, gain)


def after(x, *others):
    if isinstance(x, list):
        return list(lax.optimization_barrier((*x, *others))[: len(x)])
    return lax.optimization_barrier((x, *others))[0]


def fence(*values):
    return lax.optimization_barrier(values)


def pass_on(pair, axis, s):
    n = lax.axis_size(axis)
    return (
        lax.ppermute(pair[0], axis, [(i, i - 1) for i in range(1, n - s + 1)]),
        lax.ppermute(pair[1], axis, [(i, i + 1) for i in range(s - 1, n - 1)]),
    )


def in_turn(x, pairs, axis):
    n = lax.axis_size(axis)
    index = lax.axis_index(axis)
    parts = [x] + [
        jnp.where(index + r < n, pairs[r - 1][0], pairs[n - r - 1][1]) for r in range(1, n)
    ]
    return jnp.concatenate(parts, axis=0)


def scatter_on(blocks, moving, axis, s):
    n = lax.axis_size(axis)
    ahead, behind = blocks[n - s], blocks[s]
    if s > 1:
        ahead = (ahead.astype(f32) + moving[0].astype(f32)).astype(bf16)
        behind = (behind.astype(f32) + moving[1].astype(f32)).astype(bf16)
    return (
        lax.ppermute(ahead, axis, [(i, i + 1) for i in range(s)]),
        lax.ppermute(behind, axis, [(i, i - 1) for i in range(n - s, n)]),
    )


def scatter_sum(own, terms):
    total = own.astype(f32)
    for term in terms:
        total = total + term.astype(f32)
    return total


def spread(x, axis, offsets):
    n = lax.axis_size(axis)
    return [
        x if r == 0 else lax.ppermute(x, axis, [(i, (i - r) % n) for i in range(n)]) for r in offsets
    ]


def on_device(
    inputs,
    lengths,
    norm_gain,
    up_weight,
    conv_weight,
    conv_bias,
    qkv_weight,
    gate_weight,
    gate_bias,
    skip_weight,
    outnorm_weight,
    down_weight,
    grad_out,
):
    span = inputs.shape[1]
    width = inputs.shape[2]
    inner = conv_weight.shape[1]
    taps = conv_weight.shape[0]
    heads = qkv_weight.shape[1]
    block = qkv_weight.shape[2]
    head_dim = inner // heads
    dp = lax.axis_size("dp")
    ctx = lax.axis_size("ctx")
    copies = ctx // heads
    total = ctx * span
    ctx_index = lax.axis_index("ctx")
    place = ctx_index.reshape(1).astype(jnp.int32)
    head = ctx_index // copies
    share = 1.0 / copies

    def columns_of(w, start):
        return lax.dynamic_slice_in_dim(w, start, head_dim, axis=w.ndim - 1)

    def by_offset(x):
        return [x[r * span : (r + 1) * span] for r in range(ctx)]

    live = (ctx_index * span + jnp.arange(span) < lengths[0]).astype(f32)[:, None]
    x_own = inputs[0].astype(f32)
    out_grad = grad_out[0].astype(f32) * live
    gain = norm_gain.astype(f32)[None]
    own_hat, own_scale = normalize(x_own)
    own_normed = (own_hat * gain).astype(bf16)
    own_mix = columns_of(up_weight, head * head_dim)
    own_gate = columns_of(up_weight, inner + head * head_dim)
    own_bg = out_grad.astype(bf16)
    unit = down_weight.shape[0] // ctx
    units = [
        ((h * dp + d) * copies + r, d * ctx + h * copies + r)
        for h in range(heads)
        for d in range(dp)
        for r in range(copies)
    ]
    w_mix = lax.all_gather(own_mix, "dp", axis=0, tiled=True)
    hops = [pass_on((own_normed, own_normed), "ctx", 1)]
    hops[0], own_normed, own_gate = fence(hops[0], own_normed, own_gate)
    w_gate = lax.all_gather(own_gate, "dp", axis=0, tiled=True)
    for s in range(2, ctx):
        hops.append(pass_on(hops[-1], "ctx", s))
        if s < ctx - 1:
            hops[-1], w_mix, down_weight = fence(hops[-1], w_mix, down_weight)
    w_down = lax.all_gather(down_weight, "dp", axis=0, tiled=True)
    hops, w_mix, own_bg = fence(hops, w_mix, own_bg)

    conv_taps = columns_of(conv_weight, head * head_dim).astype(f32)
    conv_shift = columns_of(conv_bias, head * head_dim).astype(f32)[None]
    skip = columns_of(skip_weight, head * head_dim).astype(f32)[None]
    out_gain = columns_of(outnorm_weight, head * head_dim).astype(f32)[None]
    maps = lax.dynamic_slice_in_dim(qkv_weight, head, 1, axis=1).astype(f32)
    maps = maps.reshape(3 * block * block, head_dim // block)
    gate_rows = columns_of(gate_weight.reshape(2 * heads, 3, inner), head * head_dim)
    gate_rows = gate_rows.transpose(1, 0, 2)
    turned = gate_rows.reshape(3, 2, heads, head_dim).transpose(0, 2, 1, 3)
    turned = jnp.concatenate([turned, turned], axis=1)
    turned = lax.dynamic_slice_in_dim(turned, head, heads, axis=1)
    turned = turned.reshape(3, 2 * heads, head_dim)
    key_scale = head_dim ** (-0.5)
    pack_rows = -(-(taps + 4 + 3 * block + 6 * heads) // dp) * dp

    bg_hops = [pass_on((own_bg, own_bg), "ctx", 1)]
    normed = in_turn(own_normed, hops, "ctx")
    mixer = dot_nn(normed, w_mix).astype(bf16)
    pre, queries, keys, values, gate_part = front(
        place, mixer, conv_taps, conv_shift, maps, gate_rows, key_scale, span
    )
    bg_hops, normed, mixer, pre, gate_part = fence(bg_hops, normed, mixer, pre, gate_part)
    gate_parts = spread(gate_part, "ctx", range(ctx))
    gate_in = dot_nn(normed, w_gate)
    gate = gates(head, gate_parts, gate_bias.astype(f32)[:, None], span, share)
    bg_hops, gate, gate_in = fence(bg_hops, gate, gate_in)
    for s in range(2, ctx - 1):
        bg_hops.append(pass_on(bg_hops[-1], "ctx", s))
    mix, num, hidden = cell(
        place, gate, queries, keys, values, pre, gate_in, skip, out_gain, span
    )
    bg_hops, mix, num, hidden = fence(bg_hops, mix, num, hidden)
    bg_hops.append(pass_on(bg_hops[-1], "ctx", ctx - 1))
    w_down = lax.dynamic_slice_in_dim(w_down, head * head_dim, head_dim, axis=0)
    branch = (dot_nn(hidden, w_down) * share).astype(bf16)
    bg_hops, branch, hidden, w_down = fence(bg_hops, branch, hidden, w_down)
    branch_blocks = by_offset(branch)
    moving = scatter_on(branch_blocks, None, "ctx", 1)
    bg = in_turn(own_bg, bg_hops, "ctx")
    down_grad = dot_tn(hidden, bg).astype(bf16)
    down_grad, bg = fence(down_grad, bg)
    down_part = lax.psum_scatter(down_grad, "dp", scatter_dimension=0, tiled=True)
    num_grad, gate_in_grad, conv_tail, tail_sums = tail_back(
        place, bg, num, pre, gate_in, w_down, skip, out_gain, span
    )
    num_grad, gate_in_grad, moving = fence(num_grad, gate_in_grad, moving)
    moving = scatter_on(branch_blocks, moving, "ctx", 2)
    up_gate = dot_tn(normed, gate_in_grad).astype(bf16)
    num_grad, up_gate, gate_in_grad = fence(num_grad, up_gate, gate_in_grad)
    gate_grad_part = lax.psum_scatter(up_gate, "dp", scatter_dimension=0, tiled=True)
    dq, dk, dv, gate_own = cell_back(gate, queries, keys, values, mix, num_grad, span)
    dq, gate_own, moving, gate_in_grad, down_part = fence(
        dq, gate_own, moving, gate_in_grad, down_part
    )
    gate_grads = spread(gate_own, "ctx", range(0, ctx, copies))
    gate_normed = dot_nt(gate_in_grad, w_gate)
    gain_part = jnp.sum(up_gate.astype(f32) * w_gate.astype(f32), axis=1)
    dq, gate_grads, moving, gate_normed, gain_part = fence(
        dq, gate_grads, moving, gate_normed, gain_part
    )
    for s in range(3, ctx):
        moving = scatter_on(branch_blocks, moving, "ctx", s)
    down_part = lax.dynamic_slice_in_dim(down_part, (ctx_index % copies) * unit, unit, axis=0)
    down_part = lax.ppermute(down_part, ("dp", "ctx"), [(b, a) for a, b in units])
    mixer_grad, pack = back(
        place, dq, dk, dv, gate_grads, queries, keys, values, pre, mixer, conv_tail,
        conv_taps, maps, turned, tail_sums, key_scale, span, pack_rows,
    )
    mixer_grad, moving, pack, down_part = fence(mixer_grad, moving, pack, down_part)
    down_hops = [pass_on((down_part, down_part), "ctx", 1)]
    up_mix = mix_grads(normed, mixer_grad, w_mix, gain_part, pack, dp)
    up_mix, mixer_grad, gate_grad_part = fence(up_mix, mixer_grad, gate_grad_part)
    mix_grad_part = lax.psum_scatter(up_mix, "dp", scatter_dimension=0, tiled=False)
    gate_hops = [pass_on((gate_grad_part, gate_grad_part), "ctx", 1)]
    normed_part = ((dot_nt(mixer_grad, w_mix) + gate_normed) * share).astype(bf16)
    normed_part, down_hops, gate_hops, moving = fence(normed_part, down_hops, gate_hops, moving)
    normed_blocks = by_offset(normed_part)
    outputs = (live * (x_own + scatter_sum(branch_blocks[0], moving))).astype(bf16)[None]
    moving = None
    mix_hops = []
    for s in range(1, ctx):
        moving = scatter_on(normed_blocks, moving, "ctx", s)
        for hops in (down_hops, gate_hops):
            if len(hops) < ctx - 1:
                hops.append(pass_on(hops[-1], "ctx", len(hops) + 1))
        if s > 1:
            have = mix_hops[-1] if mix_hops else (mix_grad_part, mix_grad_part)
            mix_hops.append(pass_on(have, "ctx", s - 1))
        if s == 1:
            moving, down_hops, gate_hops, outputs, mix_grad_part = fence(
                moving, down_hops, gate_hops, outputs, mix_grad_part
            )
            small = mix_grad_part[width // dp :][: pack_rows // dp + 1].astype(f32)
            mix_grad_part = mix_grad_part[: width // dp]
        elif s == 2:
            small = lax.all_gather(after(small, *gate_hops[-1]), "dp", axis=0)
            moving, down_hops, gate_hops, mix_hops, small = fence(
                moving, down_hops, gate_hops, mix_hops, small
            )
        else:
            if s == 3:
                small = lax.all_gather(after(small, *mix_hops[-1]), "ctx", axis=0)
            moving, down_hops, gate_hops, mix_hops, small = fence(
                moving, down_hops, gate_hops, mix_hops, small
            )
    mix_hops.append(pass_on(mix_hops[-1], "ctx", ctx - 1))
    normed_grad = scatter_sum(normed_blocks[0], moving)
    input_grad = (out_grad + normalize_back(normed_grad * gain, own_hat, own_scale))[None]
    down_total = assemble_rows(place, down_part, down_hops)
    totals = unpack(small, gain, taps, heads, block)
    bias_total = totals[5][0, : 2 * heads].reshape(heads, 2).T.reshape(-1)
    up_total = assemble(place, mix_grad_part, mix_hops, gate_grad_part, gate_hops, copies)
    return (
        outputs,
        input_grad,
        totals[0].reshape(-1),
        up_total,
        totals[1],
        totals[2].reshape(-1),
        totals[3],
        totals[4],
        bias_total,
        totals[6].reshape(-1),
        totals[7].reshape(-1),
        down_total,
    )


def solution(mesh):
    rows = P("dp", "ctx", None)
    weights = P("dp", None)
    return jax.shard_map(
        on_device,
        mesh=mesh,
        in_specs=(rows, P("dp"), P(), weights, *[P()] * 7, weights, rows),
        out_specs=(rows, rows, P(), weights, *[P()] * 7, weights),
        check_vma=False,
    )
```

time: 3730 us -> 556 us (0.15)
  waiting for transfers between devices: 2870 us -> 136 us
  matrix products: 347 us -> 57.9 us
  other arithmetic: 244 us -> 38.2 us
  local copies, waits for them, and re-layouts: 180 us -> 35.4 us
  Pallas kernels: 0 us -> 115 us
  starting transfers between devices: 24.2 us -> 124 us
    ppermute x8 -> x49, waiting for transfers between devices: 2160 us -> 136 us  [the longest x15 80.8 us: pass_on(): lax.ppermute(pair[1], axis, [(i, i + 1) for i in range(s - 1, n - 1)])]
    psum x2 -> x0, waiting for transfers between devices: 315 us -> none  [the longest x1 219 us: on_device(): lax.psum(up_part, 'ctx').astype(jnp.float32)]
    dot_general x30 -> x7, matrix products: 347 us -> 57.9 us  [the longest x3 24.8 us: dot_nn(): lax.dot_general(a, b, (((1,), (0,)), ((), ())), preferred_element_type=f32)]
    all_gather x2 -> x3, waiting for transfers between devices: 207 us -> 0.01 us  [the longest x1 0.01 us: on_device(): w_mix = lax.all_gather(own_mix, 'dp', axis=0, tiled=True)]
    reduce_scatter x2 -> x3, waiting for transfers between devices: 194 us -> 0.02 us  [the longest x1 0.02 us: on_device(): lax.psum_scatter(down_grad, 'dp', scatter_dimension=0, tiled=True)]
    pallas_call x0 -> x10, Pallas kernels: none -> 115 us  [the longest x6 82.3 us: call(): pl.pallas_call(kernel, grid_spec=pltpu.PrefetchScalarGridSpec(num_scalar_...]
    add x8 -> x0, other arithmetic: 112 us -> none  [the longest x3 51.9 us: relay_back(): jnp.exp(span_decay)[:, None, None] * carried + state_grad]
    ppermute x8 -> x49, starting transfers between devices: 23.8 us -> 124 us  [the longest x15 47.4 us: pass_on(): lax.ppermute(pair[1], axis, [(i, i + 1) for i in range(s - 1, n - 1)])]
  transfers between devices with their start and end apart: 14 -> 55, of which waited for: 11 -> 17; matrix products, arithmetic and copies ran while one was open for 6% -> 16% of each run, Pallas kernels for 0% -> 20%
where the time goes in v1:
time: 556 us; the launch traced here: 546 us
  waiting for transfers between devices  136 us (24%)
  starting transfers between devices  124 us (22%)
  Pallas kernels  115 us (21%)
  matrix products  57.9 us (10%)
  other arithmetic  38.2 us (7%)
  local copies, waits for them, and re-layouts  35.4 us (6%)
  blocking collectives  23.7 us (4%)
  between operations  16.3 us (3%)
    pallas_call x6, Pallas kernels, call(): pl.pallas_call(kernel, grid_spec=pltpu.PrefetchScalarGridSpec(num_scalar_...  82.3 us
    ppermute x15, waiting for transfers between devices, pass_on(): lax.ppermute(pair[1], axis, [(i, i + 1) for i in range(s - 1, n - 1)])  80.8 us
    ppermute x15, waiting for transfers between devices, pass_on(): lax.ppermute(pair[0], axis, [(i, i - 1) for i in range(1, n - s + 1)])  55.3 us
    ppermute x15, starting transfers between devices, pass_on(): lax.ppermute(pair[1], axis, [(i, i + 1) for i in range(s - 1, n - 1)])  47.4 us
    ppermute x15, starting transfers between devices, pass_on(): lax.ppermute(pair[0], axis, [(i, i - 1) for i in range(1, n - s + 1)])  34.1 us
    unnamed x142, local copies, waits for them, and re-layouts  25 us
    dot_general x3, matrix products, dot_nn(): lax.dot_general(a, b, (((1,), (0,)), ((), ())), preferred_element_type=f32)  24.8 us
    dot_general x2, matrix products, dot_nt(): lax.dot_general(a, b, (((1,), (1,)), ((), ())), preferred_element_type=f32)  20.6 us
  transfers between devices with their start and end apart: 55, of which 17 were waited for; matrix products, arithmetic and copies ran while one was open for 16% of the time, Pallas kernels for 20%

profile of v1, /device:TPU:16, one launch (start us, length us, event | category | flops | bytes accessed | tf_op | source)
XLA Modules:
  0.0 546.4 jit_solution(15110953974563282794)
XLA Ops:
  12.8 3.5 collective-permute-start.1
  18.6 20.9 %collective-permute-done.1 = bf16[256,2048]{1,0:T(8,128)(2,1)S(1)} collective-permute-done((bf16[256,2048]{1,0:T(8,128)(2,1)S(1)}, bf16[256,2048]{1,0:T(8,128)(2,1)S(1)}, u32[]{:S(2)}, u32[]{:S(2)}) %collective-permute-start.1) | collective-permute-done | bytes 1048608 | tf_op jit(solution)/shard_map/ppermute | solution.py:819
  39.6 3.2 collective-permute-done
  47.2 19.3 %collective-permute-done.2 = bf16[256,2048]{1,0:T(8,128)(2,1)S(1)} collective-permute-done((bf16[256,2048]{1,0:T(8,128)(2,1)S(1)}, bf16[256,2048]{1,0:T(8,128)(2,1)S(1)}, u32[]{:S(2)}, u32[]{:S(2)}) %collective-permute-start.2) | collective-permute-done | bytes 1048608 | tf_op jit(solution)/shard_map/ppermute | solution.py:818
  67.5 3.5 collective-permute-done.3
  74.1 3.3 collective-permute-start.5
  80.0 17.0 %collective-permute-done.5 = bf16[256,2048]{1,0:T(8,128)(2,1)} collective-permute-done((bf16[256,2048]{1,0:T(8,128)(2,1)}, bf16[256,2048]{1,0:T(8,128)(2,1)}, u32[]{:S(2)}, u32[]{:S(2)}) %collective-permute-start.5) | collective-permute-done | bytes 1048608 | tf_op jit(solution)/shard_map/ppermute | solution.py:819
  97.0 4.4 collective-permute-start.7
  106.3 8.7 %convolution_convert_fusion.3.mix_ref.prev_ref = bf16[1024,1024]{1,0:T(8,128)(2,1)} fusion(bf16[2048,1024]{1,0:T(8,128)(2,1)S(1)} %copy-done.69, bf16[256,2048]{1,0:T(8,128)(2,1)S(1)} %get-tuple-element.342, bf16[256,2048]{1,0:T(8,128)(2,1)S(1)} %get-tuple-element.343, bf16[256,2048]{1,0:T(8,128)(2,1)S(1)} %broadcast_select_fusion.5, ...), kind=kOutput, calls=%fused_computation.40 | convolution fusion | flops 4312793088 | bytes 10485760 | tf_op jit(solution)/shard_map/dot_general | solution.py:16
  117.3 13.9 %front.1 = (f32[1024,1024]{1,0:T(8,128)}, bf16[1024,1024]{1,0:T(8,128)(2,1)S(1)}, bf16[1024,1024]{1,0:T(8,128)(2,1)S(1)}, bf16[1024,1024]{1,0:T(8,128)(2,1)}, f32[8,1024]{1,0:T(8,128)S(1)}) custom-call(s32[1]{0:T(128)} %bitcast.3.at_ref.head_ref, bf16[1024,1024]{1,0:T(8,128)(2,1)} %convolution_convert_fusion.3.mix_ref.prev_ref, ...), custom_call_target="tpu_custom_call" | custom-call | flops 6000000000 | bytes 12582912 | tf_op jit(solution)/shard_map/front/pallas_call | solution.py:59
  139.3 10.0 %fusion.26.gin_ref = f32[1024,1024]{1,0:T(8,128)} fusion(bf16[1024,2048]{1,0:T(8,128)(2,1)} %pad_maximum_fusion.x_ref, bf16[2048,1024]{1,0:T(8,128)(2,1)} %all-gather.9.cloned.1.call-done), kind=kOutput, calls=%fused_computation.72 | convolution fusion | flops 4294967296 | bytes 12582912 | tf_op jit(solution)/shard_map/dot_general | solution.py:16
  153.0 4.0 collective-permute-start.11
  160.9 16.5 %cell.1 = (bf16[1024,1024]{1,0:T(8,128)(2,1)S(1)}, f32[1024,1024]{1,0:T(8,128)}, bf16[1024,1024]{1,0:T(8,128)(2,1)S(1)}) custom-call(s32[1]{0:T(128)} %bitcast.3.at_ref.head_ref, f32[8,1024]{1,0:T(8,128)S(1)} %copy-done.27, bf16[1024,1024]{1,0:T(8,128)(2,1)} %copy-done.2, bf16[1024,1024]{1,0:T(8,128)(2,1)} %copy-done.4, ...), custom_call_target="tpu_custom_call" | custom-call | flops 2684354560 | bytes 20971520 | tf_op jit(solution)/shard_map/cell/pallas_call | solution.py:59
  181.2 3.2 collective-permute-start.14
  186.9 6.1 %convolution_convert_fusion.2 = bf16[1024,2048]{1,0:T(8,128)(2,1)} fusion(bf16[1024,1024]{1,0:T(8,128)(2,1)S(1)} %get-tuple-element.208, bf16[1024,2048]{1,0:T(8,128)(2,1)S(1)} %constant_dynamic-slice_fusion.down_ref), kind=kOutput, calls=%fused_computation.6 | convolution fusion | flops 4297064448 | bytes 10485760 | tf_op jit(solution)/shard_map/dot_general | solution.py:16
  193.1 8.1 %collective-permute-done.14 = bf16[256,2048]{1,0:T(8,128)(2,1)} collective-permute-done((bf16[256,2048]{1,0:T(8,128)(2,1)}, bf16[256,2048]{1,0:T(8,128)(2,1)}, u32[]{:S(2)}, u32[]{:S(2)}) %collective-permute-start.14) | collective-permute-done | bytes 1048608 | tf_op jit(solution)/shard_map/ppermute | solution.py:819
  206.4 6.3 %convolution_convert_fusion.1 = bf16[1024,2048]{1,0:T(8,128)(2,1)} fusion(bf16[1024,1024]{1,0:T(8,128)(2,1)S(1)} %get-tuple-element.208, bf16[256,2048]{1,0:T(8,128)(2,1)S(1)} %broadcast_select_fusion, bf16[256,2048]{1,0:T(8,128)(2,1)S(1)} %broadcast_select_fusion.2, bf16[256,2048]{1,0:T(8,128)(2,1)S(1)} %broadcast_select_fusion.4, ...), kind=kOutput, calls=%fused_computation.5 | convolution fusion | flops 4313841664 | bytes 10485760 | tf_op jit(solution)/shard_map/dot_general | solution.py:24
  217.6 18.0 %tail_back.1 = (bf16[1024,1024]{1,0:T(8,128)(2,1)S(1)}, bf16[1024,1024]{1,0:T(8,128)(2,1)S(1)}, f32[1024,1024]{1,0:T(8,128)}, f32[16,1024]{1,0:T(8,128)S(1)}) custom-call(s32[1]{0:T(128)} %bitcast.3.at_ref.head_ref, bf16[1024,2048]{1,0:T(8,128)(2,1)} %pad_maximum_fusion.1.bg_ref, f32[1024,1024]{1,0:T(8,128)} %get-tuple-element.216.num_ref, ...), custom_call_target="tpu_custom_call" | custom-call | flops 4294967296 | bytes 25165824 | tf_op jit(solution)/shard_map/tail_back/pallas_call | solution.py:59
  238.2 6.2 %convolution_convert_fusion = bf16[2048,1024]{1,0:T(8,128)(2,1)} fusion(bf16[1024,2048]{1,0:T(8,128)(2,1)S(1)} %copy-done.44, bf16[1024,1024]{1,0:T(8,128)(2,1)S(1)} %get-tuple-element.234), kind=kOutput, calls=%fused_computation.4 | convolution fusion | flops 4297064448 | bytes 10485760 | tf_op jit(solution)/shard_map/dot_general | solution.py:24
  244.6 4.0 fusion.17
  248.6 3.5 collective-permute-start.18
  255.4 18.0 %cell_back.1 = (f32[1024,1024]{1,0:T(8,128)}, f32[1024,1024]{1,0:T(8,128)}, f32[1024,1024]{1,0:T(8,128)}, f32[2,1024]{1,0:T(2,128)S(1)}) custom-call(f32[8,1024]{1,0:T(8,128)S(1)} %copy-done.28, bf16[1024,1024]{1,0:T(8,128)(2,1)S(1)} %copy-done.3, bf16[1024,1024]{1,0:T(8,128)(2,1)S(1)} %copy-done.5, bf16[1024,1024]{1,0:T(8,128)(2,1)} %get-tuple-element.193.v_ref, ...), custom_call_target="tpu_custom_call" | custom-call | flops 5368709120 | bytes 25165824 | tf_op jit(solution)/shard_map/cell_back/pallas_call | solution.py:450
  281.9 3.7 collective-permute-start.24
  285.6 10.8 %fusion.27 = f32[1024,2048]{1,0:T(8,128)} fusion(bf16[1024,1024]{1,0:T(8,128)(2,1)} %copy-done.31, bf16[2048,1024]{1,0:T(8,128)(2,1)} %all-gather.9.cloned.1.call-done), kind=kOutput, calls=%fused_computation.73 | convolution fusion | flops 4294967296 | bytes 14680064 | tf_op jit(solution)/shard_map/dot_general | solution.py:20
  301.1 3.4 collective-permute-start.22
  304.5 25.1 %back.1 = (bf16[1024,1024]{1,0:T(8,128)(2,1)S(1)}, f32[48,1024]{1,0:T(8,128)S(1)}) custom-call(s32[1]{0:T(128)} %bitcast.3.at_ref.head_ref, f32[1024,1024]{1,0:T(8,128)} %get-tuple-element.236.dq_ref, f32[1024,1024]{1,0:T(8,128)} %get-tuple-element.237.dk_ref, f32[1024,1024]{1,0:T(8,128)} %get-tuple-element.238.dv_ref, bf16[1024,1024]{1,0:T(8,128)(2,1)S(1)} %copy-done.3, ...), custom_call_target="tpu_custom_call" | custom-call | flops 12000000000 | bytes 31457280 | tf_op jit(solution)/shard_map/back/pallas_call | solution.py:59
  333.9 10.7 %mix_grads.1 = bf16[8,272,1024]{2,1,0:T(8,128)(2,1)} custom-call(bf16[1024,2048]{1,0:T(8,128)(2,1)} %pad_maximum_fusion.x_ref, bf16[1024,1024]{1,0:T(8,128)(2,1)S(1)} %copy-done.34, bf16[2048,1024]{1,0:T(8,128)(2,1)} %all-gather.7.cloned.1.call-done.w_ref, f32[8,1,256]{2,1,0:T(1,128)S(1)} %bitcast.88, f32[8,6,1024]{2,1,0:T(8,128)S(1)} %reshape.100.pack_ref), custom_call_target="tpu_custom_call" | custom-call | flops 4294967296 | bytes 16777216 | tf_op jit(solution)/shard_map/mix_grads/pallas_call | solution.py:728
  347.5 3.9 collective-permute-start.27
  353.4 4.1 collective-permute-start.25
  357.5 9.9 %add_convert_fusion = bf16[1024,2048]{1,0:T(8,128)(2,1)S(1)} fusion(f32[1024,2048]{1,0:T(8,128)} %fusion.27, bf16[1024,1024]{1,0:T(8,128)(2,1)} %copy-done.33, bf16[2048,1024]{1,0:T(8,128)(2,1)} %all-gather.7.cloned.1.call-done.w_ref), kind=kOutput, calls=%fused_computation | convolution fusion | flops 4299161600 | bytes 18874368 | tf_op jit(solution)/shard_map/dot_general | solution.py:20
  367.5 3.8 collective-permute-done.26.refs_2_
  373.1 3.8 collective-permute-start.31
  380.1 4.6 collective-permute-start.32
  393.3 3.8 collective-permute-done.32.refs_4_
  397.1 7.3 %collective-permute-done.34.refs_11_ = bf16[256,1024]{1,0:T(8,128)(2,1)S(1)} collective-permute-done((bf16[256,1024]{1,0:T(8,128)(2,1)S(1)}, bf16[256,1024]{1,0:T(8,128)(2,1)S(1)}, u32[]{:S(2)}, u32[]{:S(2)}) %collective-permute-start.34) | collective-permute-done | bytes 524320 | tf_op jit(solution)/shard_map/ppermute | solution.py:819
  407.5 4.5 collective-permute-start.42
  427.0 3.9 collective-permute-done.40.refs_13_
  430.9 4.4 collective-permute-start.38
  436.1 8.8 %all-gather.2 = f32[8,7,1024]{2,1,0:T(8,128)S(1)} all-gather(f32[1,7,1024]{2,1,0:T(8,128)S(1)} %bitcast.93), channel_id=2, replica_groups=mesh['dp'=8,'ctx'=4] {'dp'}, dimensions={0}, use_global_device_ids=true | all-gather | bytes 258048 | tf_op jit(solution)/shard_map/all_gather | solution.py:1017
  444.9 7.3 %collective-permute-done.41.refs_1_ = bf16[256,1024]{1,0:T(8,128)(2,1)S(1)} collective-permute-done((bf16[256,1024]{1,0:T(8,128)(2,1)S(1)}, bf16[256,1024]{1,0:T(8,128)(2,1)S(1)}, u32[]{:S(2)}, u32[]{:S(2)}) %collective-permute-start.41) | collective-permute-done | bytes 524320 | tf_op jit(solution)/shard_map/ppermute | solution.py:818
  456.8 3.7 collective-permute-start.43
  464.7 21.3 %collective-permute-done.45.refs_3_ = bf16[256,1024]{1,0:T(8,128)(2,1)S(1)} collective-permute-done((bf16[256,1024]{1,0:T(8,128)(2,1)S(1)}, bf16[256,1024]{1,0:T(8,128)(2,1)S(1)}, u32[]{:S(2)}, u32[]{:S(2)}) %collective-permute-start.45) | collective-permute-done | bytes 524320 | tf_op jit(solution)/shard_map/ppermute | solution.py:818
  486.7 8.4 %collective-permute-done.46.refs_4_ = bf16[256,1024]{1,0:T(8,128)(2,1)} collective-permute-done((bf16[256,1024]{1,0:T(8,128)(2,1)S(1)}, bf16[256,1024]{1,0:T(8,128)(2,1)}, u32[]{:S(2)}, u32[]{:S(2)}) %collective-permute-start.46) | collective-permute-done | bytes 524320 | tf_op jit(solution)/shard_map/ppermute | solution.py:819
  495.2 14.9 %all-gather.1 = f32[32,7,1024]{2,0,1:T(8,128)S(1)} all-gather(f32[8,7,1024]{2,0,1:T(8,128)S(1)} %copy.33), channel_id=3, replica_groups=mesh['dp'=8,'ctx'=4] {'ctx'}, dimensions={0}, use_global_device_ids=true | all-gather | bytes 1146880 | tf_op jit(solution)/shard_map/all_gather | solution.py:1023
  513.9 3.2 fusion.23
  517.8 5.5 %collective-permute-start.48 = (bf16[256,1024]{1,0:T(8,128)(2,1)}, bf16[256,1024]{1,0:T(8,128)(2,1)S(1)}, u32[]{:S(2)}, u32[]{:S(2)}) collective-permute-start(bf16[256,1024]{1,0:T(8,128)(2,1)} %collective-permute-done.46.refs_4_), channel_id=1, source_target_pairs={{2,3},{6,7},{10,11},{14,15},{18,19},{22,23},{26,27},{30,31}} | collective-permute-start | bytes 1572872 | tf_op jit(solution)/shard_map/ppermute | solution.py:819
  528.8 3.9 fusion.12
  532.7 6.4 %assemble.1 = f32[256,8192]{1,0:T(8,128)} custom-call(s32[1]{0:T(128)} %bitcast.3.at_ref.head_ref, bf16[256,1024]{1,0:T(8,128)(2,1)S(1)} %slice.43.refs_0_, bf16[256,1024]{1,0:T(8,128)(2,1)S(1)} %copy-done.20, bf16[256,1024]{1,0:T(8,128)(2,1)S(1)} %copy-done.18, bf16[256,1024]{1,0:T(8,128)(2,1)S(1)} %copy-done.26, ...), custom_call_target="tpu_custom_call" | custom-call | bytes 12582912 | tf_op jit(solution)/shard_map/assemble/pallas_call | solution.py:59
  (279 shorter events, 137.5 us)
Async XLA Ops:
  7.2 63.8 %all-gather.7.cloned.1.call-start = ((), (), s32[]{:S(2)}) async-start(), calls=%async_computation.3 | async-start | bytes 4718592 | tf_op jit(solution)/shard_map/all_gather | solution.py:911
  9.6 129.6 %all-gather.9.cloned.1.call-start = ((), (), s32[]{:S(2)}) async-start(), calls=%async_computation.4 | async-start | bytes 4718592 | tf_op jit(solution)/shard_map/all_gather | solution.py:914
  12.8 26.8 %collective-permute-start.1 = (bf16[256,2048]{1,0:T(8,128)(2,1)S(1)}, bf16[256,2048]{1,0:T(8,128)(2,1)S(1)}, u32[]{:S(2)}, u32[]{:S(2)}) collective-permute-start(bf16[256,2048]{1,0:T(8,128)(2,1)S(1)} %fusion.7), channel_id=1, source_target_pairs={{0,1},{1,2},{2,3},{4,5},{5,6},{6,7},{8,9},{9,10},{10,11},{12,13},{... | collective-permute-start | bytes 3145736 | tf_op jit(solution)/shard_map/ppermute | solution.py:819
  16.2 26.5 %collective-permute-start = (bf16[256,2048]{1,0:T(8,128)(2,1)S(1)}, bf16[256,2048]{1,0:T(8,128)(2,1)S(1)}, u32[]{:S(2)}, u32[]{:S(2)}) collective-permute-start(bf16[256,2048]{1,0:T(8,128)(2,1)S(1)} %fusion.7), channel_id=1, source_target_pairs={{1,0},{2,1},{3,2},{5,4},{6,5},{7,6},{9,8},{10,9},{11,10},{13,12},{... | collective-permute-start | bytes 3145736 | tf_op jit(solution)/shard_map/ppermute | solution.py:818
  42.8 141.6 %all-gather.11.cloned.1.call-start = ((), (), s32[]{:S(2)}) async-start(), calls=%async_computation.5 | async-start | bytes 18874368 | tf_op jit(solution)/shard_map/all_gather | solution.py:919
  42.8 23.7 %collective-permute-start.2 = (bf16[256,2048]{1,0:T(8,128)(2,1)S(1)}, bf16[256,2048]{1,0:T(8,128)(2,1)S(1)}, u32[]{:S(2)}, u32[]{:S(2)}) collective-permute-start(bf16[256,2048]{1,0:T(8,128)(2,1)S(1)} %collective-permute-done), channel_id=1, source_target_pairs={{1,0},{2,1},{5,4},{6,5},{9,8},{10,9},{13,12},{14,13},{17,16},{18,1... | collective-permute-start | bytes 3145736 | tf_op jit(solution)/shard_map/ppermute | solution.py:818
  45.3 25.7 %collective-permute-start.3 = (bf16[256,2048]{1,0:T(8,128)(2,1)}, bf16[256,2048]{1,0:T(8,128)(2,1)}, u32[]{:S(2)}, u32[]{:S(2)}) collective-permute-start(bf16[256,2048]{1,0:T(8,128)(2,1)} %copy-done.61), channel_id=1, source_target_pairs={{1,2},{2,3},{5,6},{6,7},{9,10},{10,11},{13,14},{14,15},{17,18},{18... | collective-permute-start | bytes 3145736 | tf_op jit(solution)/shard_map/ppermute | solution.py:819
  71.0 203.6 %reduce-scatter.4.cloned.1.call-start = ((), (), s32[]{:S(2)}) async-start(), calls=%async_computation.6 | async-start | bytes 4718592 | tf_op jit(solution)/shard_map/reduce_scatter | solution.py:963
  74.1 22.9 %collective-permute-start.5 = (bf16[256,2048]{1,0:T(8,128)(2,1)}, bf16[256,2048]{1,0:T(8,128)(2,1)}, u32[]{:S(2)}, u32[]{:S(2)}) collective-permute-start(bf16[256,2048]{1,0:T(8,128)(2,1)} %collective-permute-done.3), channel_id=1, source_target_pairs={{2,3},{6,7},{10,11},{14,15},{18,19},{22,23},{26,27},{30,31}} | collective-permute-start | bytes 3145736 | tf_op jit(solution)/shard_map/ppermute | solution.py:819
  97.0 36.9 %collective-permute-start.7 = (bf16[256,2048]{1,0:T(8,128)(2,1)S(1)}, bf16[256,2048]{1,0:T(8,128)(2,1)S(1)}, u32[]{:S(2)}, u32[]{:S(2)}) collective-permute-start(bf16[256,2048]{1,0:T(8,128)(2,1)S(1)} %fusion.20), channel_id=1, source_target_pairs={{0,1},{1,2},{2,3},{4,5},{5,6},{6,7},{8,9},{9,10},{10,11},{12,13},{... | collective-permute-start | bytes 3145736 | tf_op jit(solution)/shard_map/ppermute | solution.py:819
  101.4 32.6 %collective-permute-start.6 = (bf16[256,2048]{1,0:T(8,128)(2,1)S(1)}, bf16[256,2048]{1,0:T(8,128)(2,1)}, u32[]{:S(2)}, u32[]{:S(2)}) collective-permute-start(bf16[256,2048]{1,0:T(8,128)(2,1)S(1)} %fusion.20), channel_id=1, source_target_pairs={{1,0},{2,1},{3,2},{5,4},{6,5},{7,6},{9,8},{10,9},{11,10},{13,12},{... | collective-permute-start | bytes 3145736 | tf_op jit(solution)/shard_map/ppermute | solution.py:818
  133.9 15.3 %collective-permute-start.10 = (f32[8,1024]{1,0:T(8,128)S(1)}, f32[8,1024]{1,0:T(8,128)S(1)}, u32[]{:S(2)}, u32[]{:S(2)}) collective-permute-start(f32[8,1024]{1,0:T(8,128)S(1)} %get-tuple-element.188.refs_0_), channel_id=1, source_target_pairs={{0,1},{1,2},{2,3},{3,0},{4,5},{5,6},{6,7},{7,4},{8,9},{9,10},{10,1... | collective-permute-start | bytes 98312 | tf_op jit(solution)/shard_map/ppermute | solution.py:854
  153.0 25.7 %collective-permute-start.11 = (bf16[256,2048]{1,0:T(8,128)(2,1)}, bf16[256,2048]{1,0:T(8,128)(2,1)}, u32[]{:S(2)}, u32[]{:S(2)}) collective-permute-start(bf16[256,2048]{1,0:T(8,128)(2,1)} %collective-permute-done.6), channel_id=1, source_target_pairs={{1,0},{2,1},{5,4},{6,5},{9,8},{10,9},{13,12},{14,13},{17,16},{18,1... | collective-permute-start | bytes 3145736 | tf_op jit(solution)/shard_map/ppermute | solution.py:818
  157.0 22.6 %collective-permute-start.12 = (bf16[256,2048]{1,0:T(8,128)(2,1)S(1)}, bf16[256,2048]{1,0:T(8,128)(2,1)}, u32[]{:S(2)}, u32[]{:S(2)}) collective-permute-start(bf16[256,2048]{1,0:T(8,128)(2,1)S(1)} %copy-done.55), channel_id=1, source_target_pairs={{1,2},{2,3},{5,6},{6,7},{9,10},{10,11},{13,14},{14,15},{17,18},{18... | collective-permute-start | bytes 3145736 | tf_op jit(solution)/shard_map/ppermute | solution.py:819
  181.2 19.9 %collective-permute-start.14 = (bf16[256,2048]{1,0:T(8,128)(2,1)}, bf16[256,2048]{1,0:T(8,128)(2,1)}, u32[]{:S(2)}, u32[]{:S(2)}) collective-permute-start(bf16[256,2048]{1,0:T(8,128)(2,1)} %collective-permute-done.12), channel_id=1, source_target_pairs={{2,3},{6,7},{10,11},{14,15},{18,19},{22,23},{26,27},{30,31}} | collective-permute-start | bytes 3145736 | tf_op jit(solution)/shard_map/ppermute | solution.py:819
  212.7 131.9 %reduce-scatter.6.cloned.1.call-start = ((), (), s32[]{:S(2)}) async-start(), calls=%async_computation.7 | async-start | bytes 4718592 | tf_op jit(solution)/shard_map/reduce_scatter | solution.py:971
  214.5 22.4 %collective-permute-start.16 = (bf16[256,2048]{1,0:T(8,128)(2,1)S(1)}, bf16[256,2048]{1,0:T(8,128)(2,1)}, u32[]{:S(2)}, u32[]{:S(2)}) collective-permute-start(bf16[256,2048]{1,0:T(8,128)(2,1)S(1)} %get-tuple-element.338), channel_id=1, source_target_pairs={{3,2},{7,6},{11,10},{15,14},{19,18},{23,22},{27,26},{31,30}} | collective-permute-start | bytes 3145736 | tf_op jit(solution)/shard_map/ppermute | solution.py:840
  215.8 21.1 %collective-permute-start.15 = (bf16[256,2048]{1,0:T(8,128)(2,1)S(1)}, bf16[256,2048]{1,0:T(8,128)(2,1)}, u32[]{:S(2)}, u32[]{:S(2)}) collective-permute-start(bf16[256,2048]{1,0:T(8,128)(2,1)S(1)} %get-tuple-element.339), channel_id=1, source_target_pairs={{0,1},{4,5},{8,9},{12,13},{16,17},{20,21},{24,25},{28,29}} | collective-permute-start | bytes 3145736 | tf_op jit(solution)/shard_map/ppermute | solution.py:839
  244.5 161.8 %reduce-scatter.8.cloned.1.call-start = ((), (), s32[]{:S(2)}) async-start(), calls=%async_computation.8 | async-start | bytes 5013504 | tf_op jit(solution)/shard_map/reduce_scatter | solution.py:994
  248.6 26.0 %collective-permute-start.18 = (bf16[256,2048]{1,0:T(8,128)(2,1)}, bf16[256,2048]{1,0:T(8,128)(2,1)}, u32[]{:S(2)}, u32[]{:S(2)}) collective-permute-start(bf16[256,2048]{1,0:T(8,128)(2,1)} %get-tuple-element.336), channel_id=1, source_target_pairs={{2,1},{3,2},{6,5},{7,6},{10,9},{11,10},{14,13},{15,14},{18,17},{19... | collective-permute-start | bytes 3145736 | tf_op jit(solution)/shard_map/ppermute | solution.py:840
  252.2 22.4 %collective-permute-start.17 = (bf16[256,2048]{1,0:T(8,128)(2,1)}, bf16[256,2048]{1,0:T(8,128)(2,1)}, u32[]{:S(2)}, u32[]{:S(2)}) collective-permute-start(bf16[256,2048]{1,0:T(8,128)(2,1)} %get-tuple-element.337), channel_id=1, source_target_pairs={{0,1},{1,2},{4,5},{5,6},{8,9},{9,10},{12,13},{13,14},{16,17},{17,1... | collective-permute-start | bytes 3145736 | tf_op jit(solution)/shard_map/ppermute | solution.py:839
  274.6 21.8 %collective-permute-start.21 = (f32[2,1024]{1,0:T(2,128)S(1)}, f32[2,1024]{1,0:T(2,128)S(1)}, u32[]{:S(2)}, u32[]{:S(2)}) collective-permute-start(f32[2,1024]{1,0:T(2,128)S(1)} %get-tuple-element.241.refs_0_), channel_id=1, source_target_pairs={{0,1},{1,2},{2,3},{3,0},{4,5},{5,6},{6,7},{7,4},{8,9},{9,10},{10,1... | collective-permute-start | bytes 24584 | tf_op jit(solution)/shard_map/ppermute | solution.py:854
  277.8 18.6 %collective-permute-start.20 = (f32[2,1024]{1,0:T(2,128)S(1)}, f32[2,1024]{1,0:T(2,128)S(1)}, u32[]{:S(2)}, u32[]{:S(2)}) collective-permute-start(f32[2,1024]{1,0:T(2,128)S(1)} %get-tuple-element.241.refs_0_), channel_id=1, source_target_pairs={{0,2},{1,3},{2,0},{3,1},{4,6},{5,7},{6,4},{7,5},{8,10},{9,11},{10,... | collective-permute-start | bytes 24584 | tf_op jit(solution)/shard_map/ppermute | solution.py:854
  279.0 17.4 %collective-permute-start.19 = (f32[2,1024]{1,0:T(2,128)S(1)}, f32[2,1024]{1,0:T(2,128)S(1)}, u32[]{:S(2)}, u32[]{:S(2)}) collective-permute-start(f32[2,1024]{1,0:T(2,128)S(1)} %get-tuple-element.241.refs_0_), channel_id=1, source_target_pairs={{0,3},{1,0},{2,1},{3,2},{4,7},{5,4},{6,5},{7,6},{8,11},{9,8},{10,9... | collective-permute-start | bytes 24584 | tf_op jit(solution)/shard_map/ppermute | solution.py:854
  281.9 49.0 %collective-permute-start.24 = (bf16[128,2048]{1,0:T(8,128)(2,1)}, bf16[128,2048]{1,0:T(8,128)(2,1)S(1)}, u32[]{:S(2)}, u32[]{:S(2)}) collective-permute-start(bf16[128,2048]{1,0:T(8,128)(2,1)} %reduce-scatter.4.cloned.1.call-done), channel_id=1, source_target_pairs={{0,0},{4,1},{8,2},{12,3},{16,4},{20,5},{24,6},{28,7},{1,8},{5,9},{... | collective-permute-start | bytes 1572872 | tf_op jit(solution)/shard_map/ppermute | solution.py:985
  298.6 32.3 %collective-permute-start.23 = (bf16[256,2048]{1,0:T(8,128)(2,1)S(1)}, bf16[256,2048]{1,0:T(8,128)(2,1)S(1)}, u32[]{:S(2)}, u32[]{:S(2)}) collective-permute-start(bf16[256,2048]{1,0:T(8,128)(2,1)S(1)} %get-tuple-element.334), channel_id=1, source_target_pairs={{1,0},{2,1},{3,2},{5,4},{6,5},{7,6},{9,8},{10,9},{11,10},{13,12},{... | collective-permute-start | bytes 3145736 | tf_op jit(solution)/shard_map/ppermute | solution.py:840
  301.1 29.9 %collective-permute-start.22 = (bf16[256,2048]{1,0:T(8,128)(2,1)S(1)}, bf16[256,2048]{1,0:T(8,128)(2,1)S(1)}, u32[]{:S(2)}, u32[]{:S(2)}) collective-permute-start(bf16[256,2048]{1,0:T(8,128)(2,1)S(1)} %get-tuple-element.335), channel_id=1, source_target_pairs={{0,1},{1,2},{2,3},{4,5},{5,6},{6,7},{8,9},{9,10},{10,11},{12,13},{... | collective-permute-start | bytes 3145736 | tf_op jit(solution)/shard_map/ppermute | solution.py:839
  345.6 21.9 %collective-permute-start.28 = (bf16[256,1024]{1,0:T(8,128)(2,1)S(1)}, bf16[256,1024]{1,0:T(8,128)(2,1)S(1)}, u32[]{:S(2)}, u32[]{:S(2)}) collective-permute-start(bf16[256,1024]{1,0:T(8,128)(2,1)S(1)} %copy-done.6), channel_id=1, source_target_pairs={{0,1},{1,2},{2,3},{4,5},{5,6},{6,7},{8,9},{9,10},{10,11},{12,13},{... | collective-permute-start | bytes 1572872 | tf_op jit(solution)/shard_map/ppermute | solution.py:819
  347.5 20.0 %collective-permute-start.27 = (bf16[256,1024]{1,0:T(8,128)(2,1)S(1)}, bf16[256,1024]{1,0:T(8,128)(2,1)S(1)}, u32[]{:S(2)}, u32[]{:S(2)}) collective-permute-start(bf16[256,1024]{1,0:T(8,128)(2,1)S(1)} %copy-done.6), channel_id=1, source_target_pairs={{1,0},{2,1},{3,2},{5,4},{6,5},{7,6},{9,8},{10,9},{11,10},{13,12},{... | collective-permute-start | bytes 1572872 | tf_op jit(solution)/shard_map/ppermute | solution.py:818
  351.5 19.9 %collective-permute-start.26 = (bf16[128,2048]{1,0:T(8,128)(2,1)S(1)}, bf16[128,2048]{1,0:T(8,128)(2,1)S(1)}, u32[]{:S(2)}, u32[]{:S(2)}) collective-permute-start(bf16[128,2048]{1,0:T(8,128)(2,1)S(1)} %collective-permute-done.24.refs_0_), channel_id=1, source_target_pairs={{0,1},{1,2},{2,3},{4,5},{5,6},{6,7},{8,9},{9,10},{10,11},{12,13},{... | collective-permute-start | bytes 1572872 | tf_op jit(solution)/shard_map/ppermute | solution.py:819
  353.4 19.7 %collective-permute-start.25 = (bf16[128,2048]{1,0:T(8,128)(2,1)S(1)}, bf16[128,2048]{1,0:T(8,128)(2,1)S(1)}, u32[]{:S(2)}, u32[]{:S(2)}) collective-permute-start(bf16[128,2048]{1,0:T(8,128)(2,1)S(1)} %collective-permute-done.24.refs_0_), channel_id=1, source_target_pairs={{1,0},{2,1},{3,2},{5,4},{6,5},{7,6},{9,8},{10,9},{11,10},{13,12},{... | collective-permute-start | bytes 1572872 | tf_op jit(solution)/shard_map/ppermute | solution.py:818
  373.1 15.4 %collective-permute-start.31 = (bf16[128,2048]{1,0:T(8,128)(2,1)S(1)}, bf16[128,2048]{1,0:T(8,128)(2,1)S(1)}, u32[]{:S(2)}, u32[]{:S(2)}) collective-permute-start(bf16[128,2048]{1,0:T(8,128)(2,1)S(1)} %collective-permute-done.25.refs_1_), channel_id=1, source_target_pairs={{1,0},{2,1},{5,4},{6,5},{9,8},{10,9},{13,12},{14,13},{17,16},{18,1... | collective-permute-start | bytes 1572872 | tf_op jit(solution)/shard_map/ppermute | solution.py:818
  377.2 27.3 %collective-permute-start.30 = (bf16[256,2048]{1,0:T(8,128)(2,1)S(1)}, bf16[256,2048]{1,0:T(8,128)(2,1)S(1)}, u32[]{:S(2)}, u32[]{:S(2)}) collective-permute-start(bf16[256,2048]{1,0:T(8,128)(2,1)S(1)} %get-tuple-element.332), channel_id=1, source_target_pairs={{3,2},{7,6},{11,10},{15,14},{19,18},{23,22},{27,26},{31,30}} | collective-permute-start | bytes 3145736 | tf_op jit(solution)/shard_map/ppermute | solution.py:840
  378.5 27.8 %collective-permute-start.29 = (bf16[256,2048]{1,0:T(8,128)(2,1)S(1)}, bf16[256,2048]{1,0:T(8,128)(2,1)}, u32[]{:S(2)}, u32[]{:S(2)}) collective-permute-start(bf16[256,2048]{1,0:T(8,128)(2,1)S(1)} %get-tuple-element.333), channel_id=1, source_target_pairs={{0,1},{4,5},{8,9},{12,13},{16,17},{20,21},{24,25},{28,29}} | collective-permute-start | bytes 3145736 | tf_op jit(solution)/shard_map/ppermute | solution.py:839
  380.1 17.0 %collective-permute-start.32 = (bf16[128,2048]{1,0:T(8,128)(2,1)S(1)}, bf16[128,2048]{1,0:T(8,128)(2,1)S(1)}, u32[]{:S(2)}, u32[]{:S(2)}) collective-permute-start(bf16[128,2048]{1,0:T(8,128)(2,1)S(1)} %collective-permute-done.26.refs_2_), channel_id=1, source_target_pairs={{1,2},{2,3},{5,6},{6,7},{9,10},{10,11},{13,14},{14,15},{17,18},{18... | collective-permute-start | bytes 1572872 | tf_op jit(solution)/shard_map/ppermute | solution.py:819
  388.5 16.0 %collective-permute-start.34 = (bf16[256,1024]{1,0:T(8,128)(2,1)S(1)}, bf16[256,1024]{1,0:T(8,128)(2,1)S(1)}, u32[]{:S(2)}, u32[]{:S(2)}) collective-permute-start(bf16[256,1024]{1,0:T(8,128)(2,1)S(1)} %collective-permute-done.28.refs_9_), channel_id=1, source_target_pairs={{1,2},{2,3},{5,6},{6,7},{9,10},{10,11},{13,14},{14,15},{17,18},{18... | collective-permute-start | bytes 1572872 | tf_op jit(solution)/shard_map/ppermute | solution.py:819
  407.5 16.8 %collective-permute-start.42 = (bf16[256,1024]{1,0:T(8,128)(2,1)S(1)}, bf16[256,1024]{1,0:T(8,128)(2,1)S(1)}, u32[]{:S(2)}, u32[]{:S(2)}) collective-permute-start(bf16[256,1024]{1,0:T(8,128)(2,1)S(1)} %slice.43.refs_0_), channel_id=1, source_target_pairs={{0,1},{1,2},{2,3},{4,5},{5,6},{6,7},{8,9},{9,10},{10,11},{12,13},{... | collective-permute-start | bytes 1572872 | tf_op jit(solution)/shard_map/ppermute | solution.py:819
  413.5 17.5 %collective-permute-start.40 = (bf16[256,1024]{1,0:T(8,128)(2,1)}, bf16[256,1024]{1,0:T(8,128)(2,1)}, u32[]{:S(2)}, u32[]{:S(2)}) collective-permute-start(bf16[256,1024]{1,0:T(8,128)(2,1)} %copy-done.65), channel_id=1, source_target_pairs={{2,3},{6,7},{10,11},{14,15},{18,19},{22,23},{26,27},{30,31}} | collective-permute-start | bytes 1572872 | tf_op jit(solution)/shard_map/ppermute | solution.py:819
  418.1 35.8 %collective-permute-start.36 = (bf16[256,2048]{1,0:T(8,128)(2,1)S(1)}, bf16[256,2048]{1,0:T(8,128)(2,1)S(1)}, u32[]{:S(2)}, u32[]{:S(2)}) collective-permute-start(bf16[256,2048]{1,0:T(8,128)(2,1)S(1)} %get-tuple-element.330), channel_id=1, source_target_pairs={{2,1},{3,2},{6,5},{7,6},{10,9},{11,10},{14,13},{15,14},{18,17},{19... | collective-permute-start | bytes 3145736 | tf_op jit(solution)/shard_map/ppermute | solution.py:840
  420.0 33.8 %collective-permute-start.35 = (bf16[256,2048]{1,0:T(8,128)(2,1)S(1)}, bf16[256,2048]{1,0:T(8,128)(2,1)S(1)}, u32[]{:S(2)}, u32[]{:S(2)}) collective-permute-start(bf16[256,2048]{1,0:T(8,128)(2,1)S(1)} %get-tuple-element.331), channel_id=1, source_target_pairs={{0,1},{1,2},{4,5},{5,6},{8,9},{9,10},{12,13},{13,14},{16,17},{17,1... | collective-permute-start | bytes 3145736 | tf_op jit(solution)/shard_map/ppermute | solution.py:839
  424.4 27.8 %collective-permute-start.41 = (bf16[256,1024]{1,0:T(8,128)(2,1)S(1)}, bf16[256,1024]{1,0:T(8,128)(2,1)S(1)}, u32[]{:S(2)}, u32[]{:S(2)}) collective-permute-start(bf16[256,1024]{1,0:T(8,128)(2,1)S(1)} %slice.43.refs_0_), channel_id=1, source_target_pairs={{1,0},{2,1},{3,2},{5,4},{6,5},{7,6},{9,8},{10,9},{11,10},{13,12},{... | collective-permute-start | bytes 1572872 | tf_op jit(solution)/shard_map/ppermute | solution.py:818
  426.3 25.9 %collective-permute-start.37 = (bf16[128,2048]{1,0:T(8,128)(2,1)S(1)}, bf16[128,2048]{1,0:T(8,128)(2,1)S(1)}, u32[]{:S(2)}, u32[]{:S(2)}) collective-permute-start(bf16[128,2048]{1,0:T(8,128)(2,1)S(1)} %copy-done.12), channel_id=1, source_target_pairs={{1,0},{5,4},{9,8},{13,12},{17,16},{21,20},{25,24},{29,28}} | collective-permute-start | bytes 1572872 | tf_op jit(solution)/shard_map/ppermute | solution.py:818
  430.9 22.1 %collective-permute-start.38 = (bf16[128,2048]{1,0:T(8,128)(2,1)S(1)}, bf16[128,2048]{1,0:T(8,128)(2,1)S(1)}, u32[]{:S(2)}, u32[]{:S(2)}) collective-permute-start(bf16[128,2048]{1,0:T(8,128)(2,1)S(1)} %copy-done.15), channel_id=1, source_target_pairs={{2,3},{6,7},{10,11},{14,15},{18,19},{22,23},{26,27},{30,31}} | collective-permute-start | bytes 1572872 | tf_op jit(solution)/shard_map/ppermute | solution.py:819
  454.6 56.0 %collective-permute-start.44 = (bf16[256,2048]{1,0:T(8,128)(2,1)S(1)}, bf16[256,2048]{1,0:T(8,128)(2,1)S(1)}, u32[]{:S(2)}, u32[]{:S(2)}) collective-permute-start(bf16[256,2048]{1,0:T(8,128)(2,1)S(1)} %get-tuple-element.328), channel_id=1, source_target_pairs={{1,0},{2,1},{3,2},{5,4},{6,5},{7,6},{9,8},{10,9},{11,10},{13,12},{... | collective-permute-start | bytes 3145736 | tf_op jit(solution)/shard_map/ppermute | solution.py:840
  456.8 53.8 %collective-permute-start.43 = (bf16[256,2048]{1,0:T(8,128)(2,1)S(1)}, bf16[256,2048]{1,0:T(8,128)(2,1)S(1)}, u32[]{:S(2)}, u32[]{:S(2)}) collective-permute-start(bf16[256,2048]{1,0:T(8,128)(2,1)S(1)} %get-tuple-element.329), channel_id=1, source_target_pairs={{0,1},{1,2},{2,3},{4,5},{5,6},{6,7},{8,9},{9,10},{10,11},{12,13},{... | collective-permute-start | bytes 3145736 | tf_op jit(solution)/shard_map/ppermute | solution.py:839
  460.5 25.4 %collective-permute-start.45 = (bf16[256,1024]{1,0:T(8,128)(2,1)S(1)}, bf16[256,1024]{1,0:T(8,128)(2,1)S(1)}, u32[]{:S(2)}, u32[]{:S(2)}) collective-permute-start(bf16[256,1024]{1,0:T(8,128)(2,1)S(1)} %collective-permute-done.41.refs_1_), channel_id=1, source_target_pairs={{1,0},{2,1},{5,4},{6,5},{9,8},{10,9},{13,12},{14,13},{17,16},{18,1... | collective-permute-start | bytes 1572872 | tf_op jit(solution)/shard_map/ppermute | solution.py:818
  462.7 32.3 %collective-permute-start.46 = (bf16[256,1024]{1,0:T(8,128)(2,1)S(1)}, bf16[256,1024]{1,0:T(8,128)(2,1)}, u32[]{:S(2)}, u32[]{:S(2)}) collective-permute-start(bf16[256,1024]{1,0:T(8,128)(2,1)S(1)} %collective-permute-done.42.refs_2_), channel_id=1, source_target_pairs={{1,2},{2,3},{5,6},{6,7},{9,10},{10,11},{13,14},{14,15},{17,18},{18... | collective-permute-start | bytes 1572872 | tf_op jit(solution)/shard_map/ppermute | solution.py:819
  517.1 15.6 %collective-permute-start.47 = (bf16[256,1024]{1,0:T(8,128)(2,1)S(1)}, bf16[256,1024]{1,0:T(8,128)(2,1)S(1)}, u32[]{:S(2)}, u32[]{:S(2)}) collective-permute-start(bf16[256,1024]{1,0:T(8,128)(2,1)S(1)} %copy-done.26), channel_id=1, source_target_pairs={{1,0},{5,4},{9,8},{13,12},{17,16},{21,20},{25,24},{29,28}} | collective-permute-start | bytes 1572872 | tf_op jit(solution)/shard_map/ppermute | solution.py:818
  (78 other events, 1102.3 us)
Sparse Core Ops, SparseCore 0:
  10.5 37.7 all-gather.6
  50.2 36.7 all-gather.8
  88.9 89.9 all-gather.10
  212.8 53.2 reduce-scatter.3
  269.7 55.0 reduce-scatter.5
  344.7 51.4 reduce-scatter.7

commit v2 on v1

--- a/solution.py
+++ b/solution.py
@@ -107,7 +107,7 @@
     pad_ref[8 : 8 + rows, :] = mix_ref[...].astype(f32)
 
     def chunk(at):
-        size = 16
+        size = 32
         conv, mixed = [], []
         for i in range(block):
             cols = slice(i * lanes, (i + 1) * lanes)
@@ -133,7 +133,7 @@
             k_ref[pl.ds(at, size), cols] = (mapped(1, conv, o) * key_scale).astype(bf16)
             v_ref[pl.ds(at, size), cols] = mapped(2, mixed, o).astype(bf16)
 
-    row_chunks(rows, 16, chunk)
+    row_chunks(rows, 32, chunk)
     part_ref[...] = (
         dot_nt(gates_ref[0], q_ref[...])
         + dot_nt(gates_ref[1], k_ref[...])
@@ -286,7 +286,7 @@
         act = silu_parts(gin_ref[rows, :])[1]
         hid_ref[rows, :] = ((hat * og + skip * conv) * act).astype(bf16)
 
-    row_chunks(n, 16, chunk, 4)
+    row_chunks(n, 16, chunk, 8)
 
 
 def cell(place, gate, q, k, v, pre, gate_in, skip, out_gain, span):
@@ -344,7 +344,7 @@
         ct_ref[rows, :] = bgrad * skip
         ng_ref[rows, :] = normalize_back(bgrad * og, hat, scale).astype(bf16)
 
-    row_chunks(hg_ref.shape[0], 16, chunk, 4)
+    row_chunks(hg_ref.shape[0], 16, chunk, 8)
 
 
 def tail_back(place, bg, num, pre, gate_in, w_down, skip, out_gain, span):
@@ -497,11 +497,13 @@
     gsum_ref[...] += jnp.broadcast_to(jnp.sum(gg, axis=1, keepdims=True), gsum_ref.shape)
     high = gg.astype(bf16)
     low = (gg - high.astype(f32)).astype(bf16)
+    both = jnp.concatenate([high, low], axis=0)
     for m, x_ref in enumerate((q_ref, k_ref, v_ref)):
-        gb_ref[m] = dot_tn(high, gates_ref[m]) + dot_tn(low, gates_ref[m])
-        grow_ref[m] += dot_nn(high, x_ref[...]) + dot_nn(low, x_ref[...])
-
-    size = 16
+        gb_ref[m] = dot_tn(both, gates_ref[m])
+        grow = dot_nn(both, x_ref[...])
+        grow_ref[m] += grow[: 2 * heads] + grow[2 * heads :]
+
+    size = 32
 
     def chunk(at):
         here = pl.ds(at, size)
@@ -619,7 +621,7 @@
         [
             pltpu.VMEM((taps + 1, 8, width), f32),
             pltpu.VMEM((maps.shape[0], 8, lanes), f32),
-            pltpu.VMEM(gate_rows.shape, f32),
+            pltpu.VMEM((3, 2 * heads, width), f32),
             pltpu.VMEM((2 * heads, 128), f32),
             pltpu.VMEM((3, span, width), f32),
             pltpu.VMEM((span + 8, width), f32),
@@ -643,18 +645,18 @@
 
         @pl.when(step == at)
         def _(ref=own):
-            out_ref[...] = ref[...].astype(f32)
+            out_ref[...] = ref[...].astype(out_ref.dtype)
 
         for r in range(1, count):
             ahead, behind = others[2 * (r - 1)], others[2 * (count - r - 1) + 1]
 
             @pl.when((step == at + r) & (at_ref[0] + r < count))
             def _(ref=ahead):
-                out_ref[...] = ref[...].astype(f32)
+                out_ref[...] = ref[...].astype(out_ref.dtype)
 
             @pl.when((step == at + r) & (at_ref[0] + r >= count))
             def _(ref=behind):
-                out_ref[...] = ref[...].astype(f32)
+                out_ref[...] = ref[...].astype(out_ref.dtype)
 
 
 def flat(own, hops):
@@ -704,22 +706,15 @@
     )
 
 
-def mix_grads_kernel(x_ref, g_ref, w_ref, gain_ref, pack_ref, out_ref):
+def mix_grads_kernel(x_ref, g_ref, pack_ref, out_ref):
     rows = x_ref.shape[1]
-    grad = dot_tn(x_ref[...], g_ref[...])
-    out_ref[0, :rows, :] = grad.astype(bf16)
-    gain = row_of(jnp.sum(grad * w_ref[...].astype(f32), axis=1, keepdims=True)) + gain_ref[0]
-    width = out_ref.shape[2]
-    extra = out_ref.shape[1] - rows
+    out_ref[0, :rows, :] = dot_tn(x_ref[...], g_ref[...]).astype(bf16)
     pack = pack_ref[0]
-    parts = [pack, jnp.concatenate([gain, jnp.zeros((1, width - rows), f32)], axis=1)]
-    fill = extra - pack.shape[0] - 1
-    if fill:
-        parts.append(jnp.zeros((fill, width), f32))
-    out_ref[0, rows:, :] = jnp.concatenate(parts, axis=0).astype(bf16)
-
-
-def mix_grads(normed, mixer_grad, w_mix, gain_part, pack, dp):
+    fill = jnp.zeros((out_ref.shape[1] - rows - pack.shape[0], pack.shape[1]), f32)
+    out_ref[0, rows:, :] = jnp.concatenate([pack, fill], axis=0).astype(bf16)
+
+
+def mix_grads(normed, mixer_grad, pack, dp):
     total, width = normed.shape
     cols = mixer_grad.shape[1]
     rows = width // dp
@@ -731,16 +726,14 @@
         in_specs=[
             pl.BlockSpec((total, rows), lambda i: (0, i)),
             whole(mixer_grad.shape),
-            pl.BlockSpec((rows, cols), lambda i: (i, 0)),
-            pl.BlockSpec((1, 1, rows), lambda i: (i, 0, 0)),
             pl.BlockSpec((1,) + pack.shape[1:], lambda i: (i, 0, 0)),
         ],
         out_specs=pl.BlockSpec((1, rows + extra, cols), lambda i: (i, 0, 0)),
         out_shape=jax.ShapeDtypeStruct((dp, rows + extra, cols), bf16),
         compiler_params=kernel_params(),
-        cost_estimate=cost(2 * total * width * cols, 2 * (total * width + 3 * width * cols)),
+        cost_estimate=cost(2 * total * width * cols, 2 * (total * width + 2 * width * cols)),
         name="mix_grads",
-    )(normed, mixer_grad, w_mix, gain_part.reshape(dp, 1, rows), pack)
+    )(normed, mixer_grad, pack)
 
 
 def unpack_kernel(per, taps, heads, block, x_ref, gain_ref, norm_ref, convw_ref, convb_ref, maps_ref, gates_ref, bias_ref, skip_ref, og_ref):
@@ -752,12 +745,12 @@
     rows = norm_ref.shape[1] // dp
 
     def row(h, r):
-        return x_ref[h * copies, r // per, r % per : r % per + 1, :]
+        return x_ref[h * copies, r // per, r % per : r % per + 1, :].astype(f32)
 
     for d in range(dp):
-        total = x_ref[0, d, per : per + 1, 0:rows]
+        total = x_ref[0, d, per : per + 1, 0:rows].astype(f32)
         for h in range(1, heads):
-            total = total + x_ref[h * copies, d, per : per + 1, 0:rows]
+            total = total + x_ref[h * copies, d, per : per + 1, 0:rows].astype(f32)
         norm_ref[:, d * rows : (d + 1) * rows] = total / gain_ref[:, d * rows : (d + 1) * rows]
     for h in range(heads):
         cols = slice(h * width, (h + 1) * width)
@@ -784,8 +777,8 @@
             bias_ref[...] = row(h, at + 2)[:, 0:128]
 
 
-def unpack(small, gain, taps, heads, block):
-    per, width = small.shape[2] - 1, small.shape[3]
+def unpack(small, gain, per, taps, heads, block):
+    width = small.shape[3]
     inner = heads * width
     shapes = [
         gain.shape, (taps, inner), (1, inner), (3, heads, block, block, width // block),
@@ -802,6 +795,24 @@
     )(small, gain)
 
 
+def merge(place, own, hops):
+    rows, width = own.shape
+    count = len(hops) + 1
+    parts = flat(own, hops)
+    return call(
+        partial(assemble_kernel, count),
+        place,
+        count,
+        [whole((rows, width))] * len(parts),
+        pl.BlockSpec((rows, width), lambda i, at: (i, 0)),
+        jax.ShapeDtypeStruct((count * rows, width), own.dtype),
+        [],
+        cost(0, 4 * count * rows * width),
+        "merge",
+        *parts,
+    )
+
+
 def after(x, *others):
     if isinstance(x, list):
         return list(lax.optimization_barrier((*x, *others))[: len(x)])
@@ -818,15 +829,6 @@
         lax.ppermute(pair[0], axis, [(i, i - 1) for i in range(1, n - s + 1)]),
         lax.ppermute(pair[1], axis, [(i, i + 1) for i in range(s - 1, n - 1)]),
     )
-
-
-def in_turn(x, pairs, axis):
-    n = lax.axis_size(axis)
-    index = lax.axis_index(axis)
-    parts = [x] + [
-        jnp.where(index + r < n, pairs[r - 1][0], pairs[n - r - 1][1]) for r in range(1, n)
-    ]
-    return jnp.concatenate(parts, axis=0)
 
 
 def scatter_on(blocks, moving, axis, s):
@@ -931,33 +933,35 @@
     turned = jnp.concatenate([turned, turned], axis=1)
     turned = lax.dynamic_slice_in_dim(turned, head, heads, axis=1)
     turned = turned.reshape(3, 2 * heads, head_dim)
+    turned = jnp.concatenate([turned, turned], axis=1)
     key_scale = head_dim ** (-0.5)
     pack_rows = -(-(taps + 4 + 3 * block + 6 * heads) // dp) * dp
 
     bg_hops = [pass_on((own_bg, own_bg), "ctx", 1)]
-    normed = in_turn(own_normed, hops, "ctx")
+    normed = merge(place, own_normed, hops)
     mixer = dot_nn(normed, w_mix).astype(bf16)
+    gate_in = dot_nn(normed, w_gate)
+    bg_hops, normed, mixer, gate_in = fence(bg_hops, normed, mixer, gate_in)
+    if ctx > 3:
+        bg_hops.append(pass_on(bg_hops[-1], "ctx", 2))
     pre, queries, keys, values, gate_part = front(
         place, mixer, conv_taps, conv_shift, maps, gate_rows, key_scale, span
     )
-    bg_hops, normed, mixer, pre, gate_part = fence(bg_hops, normed, mixer, pre, gate_part)
+    pre, gate_part = fence(pre, gate_part)
     gate_parts = spread(gate_part, "ctx", range(ctx))
-    gate_in = dot_nn(normed, w_gate)
     gate = gates(head, gate_parts, gate_bias.astype(f32)[:, None], span, share)
-    bg_hops, gate, gate_in = fence(bg_hops, gate, gate_in)
-    for s in range(2, ctx - 1):
+    bg_hops, gate = fence(bg_hops, gate)
+    for s in range(len(bg_hops) + 1, ctx):
         bg_hops.append(pass_on(bg_hops[-1], "ctx", s))
     mix, num, hidden = cell(
         place, gate, queries, keys, values, pre, gate_in, skip, out_gain, span
     )
-    bg_hops, mix, num, hidden = fence(bg_hops, mix, num, hidden)
-    bg_hops.append(pass_on(bg_hops[-1], "ctx", ctx - 1))
     w_down = lax.dynamic_slice_in_dim(w_down, head * head_dim, head_dim, axis=0)
     branch = (dot_nn(hidden, w_down) * share).astype(bf16)
     bg_hops, branch, hidden, w_down = fence(bg_hops, branch, hidden, w_down)
     branch_blocks = by_offset(branch)
     moving = scatter_on(branch_blocks, None, "ctx", 1)
-    bg = in_turn(own_bg, bg_hops, "ctx")
+    bg = merge(place, own_bg, bg_hops)
     down_grad = dot_tn(hidden, bg).astype(bf16)
     down_grad, bg = fence(down_grad, bg)
     down_part = lax.psum_scatter(down_grad, "dp", scatter_dimension=0, tiled=True)
@@ -975,10 +979,7 @@
     )
     gate_grads = spread(gate_own, "ctx", range(0, ctx, copies))
     gate_normed = dot_nt(gate_in_grad, w_gate)
-    gain_part = jnp.sum(up_gate.astype(f32) * w_gate.astype(f32), axis=1)
-    dq, gate_grads, moving, gate_normed, gain_part = fence(
-        dq, gate_grads, moving, gate_normed, gain_part
-    )
+    dq, gate_grads, moving, gate_normed = fence(dq, gate_grads, moving, gate_normed)
     for s in range(3, ctx):
         moving = scatter_on(branch_blocks, moving, "ctx", s)
     down_part = lax.dynamic_slice_in_dim(down_part, (ctx_index % copies) * unit, unit, axis=0)
@@ -989,7 +990,7 @@
     )
     mixer_grad, moving, pack, down_part = fence(mixer_grad, moving, pack, down_part)
     down_hops = [pass_on((down_part, down_part), "ctx", 1)]
-    up_mix = mix_grads(normed, mixer_grad, w_mix, gain_part, pack, dp)
+    up_mix = mix_grads(normed, mixer_grad, pack, dp)
     up_mix, mixer_grad, gate_grad_part = fence(up_mix, mixer_grad, gate_grad_part)
     mix_grad_part = lax.psum_scatter(up_mix, "dp", scatter_dimension=0, tiled=False)
     gate_hops = [pass_on((gate_grad_part, gate_grad_part), "ctx", 1)]
@@ -1011,24 +1012,28 @@
             moving, down_hops, gate_hops, outputs, mix_grad_part = fence(
                 moving, down_hops, gate_hops, outputs, mix_grad_part
             )
-            small = mix_grad_part[width // dp :][: pack_rows // dp + 1].astype(f32)
-            mix_grad_part = mix_grad_part[: width // dp]
+            rows = width // dp
+            per = pack_rows // dp
+            small = mix_grad_part[rows : rows + 16]
+            mix_grad_part = mix_grad_part[:rows]
+            gain_part = mix_grad_part.astype(f32) * own_mix.astype(f32)
+            gain_part = gain_part + gate_grad_part.astype(f32) * own_gate.astype(f32)
+            gain_part = jnp.pad(jnp.sum(gain_part, axis=1)[None], ((0, 0), (0, head_dim - rows)))
+            at = lax.broadcasted_iota(jnp.int32, (16, 1), 0)
+            small = jnp.where(at == per, gain_part.astype(bf16), small)[: -(-(per + 1) // 8) * 8]
         elif s == 2:
             small = lax.all_gather(after(small, *gate_hops[-1]), "dp", axis=0)
+            small = lax.all_gather(small, "ctx", axis=0)
             moving, down_hops, gate_hops, mix_hops, small = fence(
                 moving, down_hops, gate_hops, mix_hops, small
             )
         else:
-            if s == 3:
-                small = lax.all_gather(after(small, *mix_hops[-1]), "ctx", axis=0)
-            moving, down_hops, gate_hops, mix_hops, small = fence(
-                moving, down_hops, gate_hops, mix_hops, small
-            )
+            moving, down_hops, gate_hops, mix_hops = fence(moving, down_hops, gate_hops, mix_hops)
     mix_hops.append(pass_on(mix_hops[-1], "ctx", ctx - 1))
     normed_grad = scatter_sum(normed_blocks[0], moving)
     input_grad = (out_grad + normalize_back(normed_grad * gain, own_hat, own_scale))[None]
     down_total = assemble_rows(place, down_part, down_hops)
-    totals = unpack(small, gain, taps, heads, block)
+    totals = unpack(small, gain, per, taps, heads, block)
     bias_total = totals[5][0, : 2 * heads].reshape(heads, 2).T.reshape(-1)
     up_total = assemble(place, mix_grad_part, mix_hops, gate_grad_part, gate_hops, copies)
     return (

time: 556 us -> 534 us (0.960)
  waiting for transfers between devices: 136 us -> 124 us
  other arithmetic: 38.2 us -> 28.1 us
  local copies, waits for them, and re-layouts: 35.4 us -> 27.3 us
    ppermute x15, waiting for transfers between devices: 80.8 us -> 66.8 us  [pass_on(): lax.ppermute(pair[1], axis, [(i, i + 1) for i in range(s - 1, n - 1)])]
    ppermute x15, waiting for transfers between devices: 55.3 us -> 46.8 us  [pass_on(): lax.ppermute(pair[0], axis, [(i, i - 1) for i in range(1, n - s + 1)])]
    ppermute x6, starting transfers between devices: 12.6 us -> 4.58 us  [spread(): lax.ppermute(x, axis, [(i, (i - r) % n) for i in range(n)])]
    unnamed x142 -> x122, local copies, waits for them, and re-layouts: 25 us -> 17.3 us
    select_n x5 -> x1, other arithmetic: 5.8 us -> 0.08 us  [on_device(): jnp.where(at == per, gain_part.astype(bf16), small)[:-(-(per + 1) // 8) * 8]]
    pallas_call x6 -> x8, Pallas kernels: 82.3 us -> 86.1 us  [call(): pl.pallas_call(kernel, grid_spec=pltpu.PrefetchScalarGridSpec(num_scalar_...]
  transfers between devices with their start and end apart: 55 -> 55, of which waited for: 17 -> 21; matrix products, arithmetic and copies ran while one was open for 16% -> 16% of each run, Pallas kernels for 20% -> 20%
where the time goes in v2:
time: 534 us; the launch traced here: 524 us
  waiting for transfers between devices  124 us (23%)
  starting transfers between devices  121 us (23%)
  Pallas kernels  117 us (22%)
  matrix products  60.8 us (11%)
  blocking collectives  28.8 us (5%)
  other arithmetic  28.1 us (5%)
  local copies, waits for them, and re-layouts  27.3 us (5%)
  between operations  16.3 us (3%)
    pallas_call x8, Pallas kernels, call(): pl.pallas_call(kernel, grid_spec=pltpu.PrefetchScalarGridSpec(num_scalar_...  86.1 us
    ppermute x15, waiting for transfers between devices, pass_on(): lax.ppermute(pair[1], axis, [(i, i + 1) for i in range(s - 1, n - 1)])  66.8 us
    ppermute x15, starting transfers between devices, pass_on(): lax.ppermute(pair[1], axis, [(i, i + 1) for i in range(s - 1, n - 1)])  50.1 us
    ppermute x15, waiting for transfers between devices, pass_on(): lax.ppermute(pair[0], axis, [(i, i - 1) for i in range(1, n - s + 1)])  46.8 us
    ppermute x15, starting transfers between devices, pass_on(): lax.ppermute(pair[0], axis, [(i, i - 1) for i in range(1, n - s + 1)])  32.6 us
    dot_general x3, matrix products, dot_nn(): lax.dot_general(a, b, (((1,), (0,)), ((), ())), preferred_element_type=f32)  23.9 us
    dot_general x2, matrix products, dot_nt(): lax.dot_general(a, b, (((1,), (1,)), ((), ())), preferred_element_type=f32)  20.9 us
    pallas_call x1, Pallas kernels, cell_back(): pl.pallas_call(cell_back_kernel, grid=(total // span,), in_specs=[whole(g...  17.9 us
  transfers between devices with their start and end apart: 55, of which 21 were waited for; matrix products, arithmetic and copies ran while one was open for 16% of the time, Pallas kernels for 20%

profile of v2, /device:TPU:16, one launch (start us, length us, event | category | flops | bytes accessed | tf_op | source)
XLA Modules:
  0.0 523.9 jit_solution(4863789701466298226)
XLA Ops:
  10.8 3.5 collective-permute-start.1
  16.7 20.9 %collective-permute-done.1.refs_2_ = bf16[256,2048]{1,0:T(8,128)(2,1)S(1)} collective-permute-done((bf16[256,2048]{1,0:T(8,128)(2,1)S(1)}, bf16[256,2048]{1,0:T(8,128)(2,1)S(1)}, u32[]{:S(2)}, u32[]{:S(2)}) %collective-permute-start.1) | collective-permute-done | bytes 1048608 | tf_op jit(solution)/shard_map/ppermute | solution.py:830
  37.6 3.2 collective-permute-done.refs_1_
  45.3 19.3 %collective-permute-done.2.refs_3_ = bf16[256,2048]{1,0:T(8,128)(2,1)S(1)} collective-permute-done((bf16[256,2048]{1,0:T(8,128)(2,1)S(1)}, bf16[256,2048]{1,0:T(8,128)(2,1)S(1)}, u32[]{:S(2)}, u32[]{:S(2)}) %collective-permute-start.2) | collective-permute-done | bytes 1048608 | tf_op jit(solution)/shard_map/ppermute | solution.py:829
  65.6 3.3 collective-permute-done.3.refs_4_
  70.6 3.2 collective-permute-start.5
  77.6 15.9 %collective-permute-done.5.refs_6_ = bf16[256,2048]{1,0:T(8,128)(2,1)} collective-permute-done((bf16[256,2048]{1,0:T(8,128)(2,1)}, bf16[256,2048]{1,0:T(8,128)(2,1)}, u32[]{:S(2)}, u32[]{:S(2)}) %collective-permute-start.5) | collective-permute-done | bytes 1048608 | tf_op jit(solution)/shard_map/ppermute | solution.py:830
  93.5 4.4 collective-permute-start.7
  101.2 4.5 merge.2.x_ref
  105.7 7.8 %convolution_convert_fusion.3.mix_ref.prev_ref = bf16[1024,1024]{1,0:T(8,128)(2,1)} fusion(bf16[1024,2048]{1,0:T(8,128)(2,1)} %merge.2.x_ref, bf16[2048,1024]{1,0:T(8,128)(2,1)S(1)} %copy-done.59), kind=kOutput, calls=%fused_computation.37 | convolution fusion | flops 4296015872 | bytes 10485760 | tf_op jit(solution)/shard_map/dot_general | solution.py:16
  113.5 10.0 %fusion.26.gin_ref = f32[1024,1024]{1,0:T(8,128)} fusion(bf16[1024,2048]{1,0:T(8,128)(2,1)} %merge.2.x_ref, bf16[2048,1024]{1,0:T(8,128)(2,1)} %all-gather.8.cloned.1.call-done), kind=kOutput, calls=%fused_computation.67 | convolution fusion | flops 4294967296 | bytes 12582912 | tf_op jit(solution)/shard_map/dot_general | solution.py:16
  125.1 3.8 collective-permute-start.9
  129.8 13.0 %front.1 = (f32[1024,1024]{1,0:T(8,128)}, bf16[1024,1024]{1,0:T(8,128)(2,1)S(1)}, bf16[1024,1024]{1,0:T(8,128)(2,1)S(1)}, bf16[1024,1024]{1,0:T(8,128)(2,1)}, f32[8,1024]{1,0:T(8,128)S(1)}) custom-call(s32[1]{0:T(128)} %bitcast.3.at_ref.head_ref, bf16[1024,1024]{1,0:T(8,128)(2,1)} %convolution_convert_fusion.3.mix_ref.prev_ref, ...), custom_call_target="tpu_custom_call" | custom-call | flops 6000000000 | bytes 12582912 | tf_op jit(solution)/shard_map/front/pallas_call | solution.py:59
  156.9 5.6 %collective-permute-start.14 = (bf16[256,2048]{1,0:T(8,128)(2,1)}, bf16[256,2048]{1,0:T(8,128)(2,1)}, u32[]{:S(2)}, u32[]{:S(2)}) collective-permute-start(bf16[256,2048]{1,0:T(8,128)(2,1)} %collective-permute-done.9.refs_4_), channel_id=1, source_target_pairs={{2,3},{6,7},{10,11},{14,15},{18,19},{22,23},{26,27},{30,31}} | collective-permute-start | bytes 3145736 | tf_op jit(solution)/shard_map/ppermute | solution.py:830
  163.3 15.0 %cell.1 = (bf16[1024,1024]{1,0:T(8,128)(2,1)S(1)}, f32[1024,1024]{1,0:T(8,128)}, bf16[1024,1024]{1,0:T(8,128)(2,1)S(1)}) custom-call(s32[1]{0:T(128)} %bitcast.3.at_ref.head_ref, f32[8,1024]{1,0:T(8,128)S(1)} %copy-done.27, bf16[1024,1024]{1,0:T(8,128)(2,1)} %copy-done.3, bf16[1024,1024]{1,0:T(8,128)(2,1)} %copy-done.5, ...), custom_call_target="tpu_custom_call" | custom-call | flops 2684354560 | bytes 20971520 | tf_op jit(solution)/shard_map/cell/pallas_call | solution.py:59
  183.9 6.1 %convolution_convert_fusion.2 = bf16[1024,2048]{1,0:T(8,128)(2,1)} fusion(bf16[1024,1024]{1,0:T(8,128)(2,1)S(1)} %copy-done.33, bf16[1024,2048]{1,0:T(8,128)(2,1)S(1)} %constant_dynamic-slice_fusion.down_ref), kind=kOutput, calls=%fused_computation.3 | convolution fusion | flops 4297064448 | bytes 10485760 | tf_op jit(solution)/shard_map/dot_general | solution.py:16
  190.0 4.8 merge.3.bg_ref
  194.8 8.3 %convolution_convert_fusion.1 = bf16[1024,2048]{1,0:T(8,128)(2,1)} fusion(bf16[1024,1024]{1,0:T(8,128)(2,1)S(1)} %copy-done.33, bf16[1024,2048]{1,0:T(8,128)(2,1)} %merge.3.bg_ref), kind=kOutput, calls=%fused_computation.2 | convolution fusion | flops 4297064448 | bytes 10485760 | tf_op jit(solution)/shard_map/dot_general | solution.py:24
  207.8 17.4 %tail_back.1 = (bf16[1024,1024]{1,0:T(8,128)(2,1)S(1)}, bf16[1024,1024]{1,0:T(8,128)(2,1)}, f32[1024,1024]{1,0:T(8,128)}, f32[16,1024]{1,0:T(8,128)S(1)}) custom-call(s32[1]{0:T(128)} %bitcast.3.at_ref.head_ref, bf16[1024,2048]{1,0:T(8,128)(2,1)} %merge.3.bg_ref, f32[1024,1024]{1,0:T(8,128)} %get-tuple-element.204.num_ref, ...), custom_call_target="tpu_custom_call" | custom-call | flops 4294967296 | bytes 25165824 | tf_op jit(solution)/shard_map/tail_back/pallas_call | solution.py:59
  229.5 7.7 %convolution_convert_fusion = bf16[2048,1024]{1,0:T(8,128)(2,1)} fusion(bf16[1024,2048]{1,0:T(8,128)(2,1)S(1)} %copy-done.45, bf16[1024,1024]{1,0:T(8,128)(2,1)} %get-tuple-element.222), kind=kOutput, calls=%fused_computation.1 | convolution fusion | flops 4297064448 | bytes 10485760 | tf_op jit(solution)/shard_map/dot_general | solution.py:24
  237.3 4.1 fusion.17
  241.3 4.2 collective-permute-start.18
  249.0 17.9 %cell_back.1 = (f32[1024,1024]{1,0:T(8,128)}, f32[1024,1024]{1,0:T(8,128)}, f32[1024,1024]{1,0:T(8,128)}, f32[2,1024]{1,0:T(2,128)S(1)}) custom-call(f32[8,1024]{1,0:T(8,128)S(1)} %copy-done.28, bf16[1024,1024]{1,0:T(8,128)(2,1)S(1)} %copy-done.4, bf16[1024,1024]{1,0:T(8,128)(2,1)S(1)} %copy-done.6, bf16[1024,1024]{1,0:T(8,128)(2,1)} %get-tuple-element.186.v_ref, ...), custom_call_target="tpu_custom_call" | custom-call | flops 5368709120 | bytes 25165824 | tf_op jit(solution)/shard_map/cell_back/pallas_call | solution.py:450
  266.9 3.8 collective-permute-done.17
  272.7 5.0 collective-permute-start.24
  277.7 10.8 %fusion.27 = f32[1024,2048]{1,0:T(8,128)} fusion(bf16[1024,1024]{1,0:T(8,128)(2,1)} %get-tuple-element.222, bf16[2048,1024]{1,0:T(8,128)(2,1)} %all-gather.8.cloned.1.call-done), kind=kOutput, calls=%fused_computation.68 | convolution fusion | flops 4294967296 | bytes 14680064 | tf_op jit(solution)/shard_map/dot_general | solution.py:20
  290.9 4.8 collective-permute-start.23
  297.6 22.1 %back.1 = (bf16[1024,1024]{1,0:T(8,128)(2,1)S(1)}, f32[48,1024]{1,0:T(8,128)S(1)}) custom-call(s32[1]{0:T(128)} %bitcast.3.at_ref.head_ref, f32[1024,1024]{1,0:T(8,128)} %get-tuple-element.223.dq_ref, f32[1024,1024]{1,0:T(8,128)} %get-tuple-element.224.dk_ref, f32[1024,1024]{1,0:T(8,128)} %get-tuple-element.225.dv_ref, bf16[1024,1024]{1,0:T(8,128)(2,1)S(1)} %copy-done.4, ...), custom_call_target="tpu_custom_call" | custom-call | flops 12000000000 | bytes 31457280 | tf_op jit(solution)/shard_map/back/pallas_call | solution.py:59
  324.0 9.4 %mix_grads.1 = bf16[8,272,1024]{2,1,0:T(8,128)(2,1)} custom-call(bf16[1024,2048]{1,0:T(8,128)(2,1)} %merge.2.x_ref, bf16[1024,1024]{1,0:T(8,128)(2,1)S(1)} %copy-done.35, f32[8,6,1024]{2,1,0:T(8,128)S(1)} %reshape.101.pack_ref), custom_call_target="tpu_custom_call" | custom-call | flops 4294967296 | bytes 12582912 | tf_op jit(solution)/shard_map/mix_grads/pallas_call | solution.py:723
  336.4 4.4 collective-permute-start.27
  342.7 4.2 collective-permute-start.25
  346.9 10.1 %add_convert_fusion = bf16[1024,2048]{1,0:T(8,128)(2,1)S(1)} fusion(f32[1024,2048]{1,0:T(8,128)} %fusion.27, bf16[1024,1024]{1,0:T(8,128)(2,1)} %copy-done.34, bf16[2048,1024]{1,0:T(8,128)(2,1)} %all-gather.6.cloned.1.call-done), kind=kOutput, calls=%fused_computation | convolution fusion | flops 4299161600 | bytes 18874368 | tf_op jit(solution)/shard_map/dot_general | solution.py:20
  357.1 3.6 collective-permute-done.26.refs_2_
  361.9 4.4 collective-permute-start.31
  369.5 4.6 collective-permute-start.32
  382.9 3.6 collective-permute-done.32.refs_4_
  386.6 7.3 %collective-permute-done.34.refs_11_ = bf16[256,1024]{1,0:T(8,128)(2,1)S(1)} collective-permute-done((bf16[256,1024]{1,0:T(8,128)(2,1)S(1)}, bf16[256,1024]{1,0:T(8,128)(2,1)S(1)}, u32[]{:S(2)}, u32[]{:S(2)}) %collective-permute-start.34) | collective-permute-done | bytes 524320 | tf_op jit(solution)/shard_map/ppermute | solution.py:830
  396.2 4.5 collective-permute-start.42
  415.7 3.9 collective-permute-done.40.refs_13_
  419.6 4.4 collective-permute-start.38
  424.5 14.3 %all-gather = bf16[64,1024]{1,0:T(8,128)(2,1)S(1)} all-gather(bf16[8,1024]{1,0:T(8,128)(2,1)S(1)} %slice_select_fusion), channel_id=2, replica_groups=mesh['dp'=8,'ctx'=4] {'dp'}, dimensions={0}, use_global_device_ids=true | all-gather | bytes 147456 | tf_op jit(solution)/shard_map/all_gather | solution.py:1025
  438.8 14.5 %all-gather.1 = bf16[32,8,1024]{2,1,0:T(8,128)(2,1)S(1)} all-gather(bf16[8,8,1024]{2,1,0:T(8,128)(2,1)S(1)} %bitcast.94), channel_id=3, replica_groups=mesh['dp'=8,'ctx'=4] {'ctx'}, dimensions={0}, use_global_device_ids=true | all-gather | bytes 655360 | tf_op jit(solution)/shard_map/all_gather | solution.py:1026
  457.5 4.9 collective-permute-start.43
  468.8 20.5 %collective-permute-done.45.refs_3_ = bf16[256,1024]{1,0:T(8,128)(2,1)} collective-permute-done((bf16[256,1024]{1,0:T(8,128)(2,1)}, bf16[256,1024]{1,0:T(8,128)(2,1)}, u32[]{:S(2)}, u32[]{:S(2)}) %collective-permute-start.45) | collective-permute-done | bytes 524320 | tf_op jit(solution)/shard_map/ppermute | solution.py:829
  489.3 4.6 collective-permute-done.46.refs_4_
  497.9 4.4 collective-permute-start.48
  504.9 4.4 fusion.12
  509.8 6.8 %assemble.1 = f32[256,8192]{1,0:T(8,128)} custom-call(s32[1]{0:T(128)} %bitcast.3.at_ref.head_ref, bf16[256,1024]{1,0:T(8,128)(2,1)S(1)} %slice.44.refs_0_, bf16[256,1024]{1,0:T(8,128)(2,1)} %collective-permute-done.41.refs_1_, bf16[256,1024]{1,0:T(8,128)(2,1)} %collective-permute-done.42.refs_2_, bf16[256,1024]{1,0:T(8,128)(2,1)} %collective-permute-done.45.refs_3_, ...), custom_call_target="tpu_custom_call" | custom-call | bytes 12582912 | tf_op jit(solution)/shard_map/assemble/pallas_call | solution.py:59
  (257 shorter events, 118.3 us)
Async XLA Ops:
  7.2 61.7 %all-gather.6.cloned.1.call-start = ((), (), s32[]{:S(2)}) async-start(), calls=%async_computation.3 | async-start | bytes 4718592 | tf_op jit(solution)/shard_map/all_gather | solution.py:913
  9.7 103.9 %all-gather.8.cloned.1.call-start = ((), (), s32[]{:S(2)}) async-start(), calls=%async_computation.4 | async-start | bytes 4718592 | tf_op jit(solution)/shard_map/all_gather | solution.py:916
  10.8 26.8 %collective-permute-start.1 = (bf16[256,2048]{1,0:T(8,128)(2,1)S(1)}, bf16[256,2048]{1,0:T(8,128)(2,1)S(1)}, u32[]{:S(2)}, u32[]{:S(2)}) collective-permute-start(bf16[256,2048]{1,0:T(8,128)(2,1)S(1)} %fusion.7.refs_0_), channel_id=1, source_target_pairs={{0,1},{1,2},{2,3},{4,5},{5,6},{6,7},{8,9},{9,10},{10,11},{12,13},{... | collective-permute-start | bytes 3145736 | tf_op jit(solution)/shard_map/ppermute | solution.py:830
  14.3 26.5 %collective-permute-start = (bf16[256,2048]{1,0:T(8,128)(2,1)S(1)}, bf16[256,2048]{1,0:T(8,128)(2,1)S(1)}, u32[]{:S(2)}, u32[]{:S(2)}) collective-permute-start(bf16[256,2048]{1,0:T(8,128)(2,1)S(1)} %fusion.7.refs_0_), channel_id=1, source_target_pairs={{1,0},{2,1},{3,2},{5,4},{6,5},{7,6},{9,8},{10,9},{11,10},{13,12},{... | collective-permute-start | bytes 3145736 | tf_op jit(solution)/shard_map/ppermute | solution.py:829
  40.9 140.1 %all-gather.10.cloned.1.call-start = ((), (), s32[]{:S(2)}) async-start(), calls=%async_computation.5 | async-start | bytes 18874368 | tf_op jit(solution)/shard_map/all_gather | solution.py:921
  40.9 23.7 %collective-permute-start.2 = (bf16[256,2048]{1,0:T(8,128)(2,1)S(1)}, bf16[256,2048]{1,0:T(8,128)(2,1)S(1)}, u32[]{:S(2)}, u32[]{:S(2)}) collective-permute-start(bf16[256,2048]{1,0:T(8,128)(2,1)S(1)} %collective-permute-done.refs_1_), channel_id=1, source_target_pairs={{1,0},{2,1},{5,4},{6,5},{9,8},{10,9},{13,12},{14,13},{17,16},{18,1... | collective-permute-start | bytes 3145736 | tf_op jit(solution)/shard_map/ppermute | solution.py:829
  43.3 25.5 %collective-permute-start.3 = (bf16[256,2048]{1,0:T(8,128)(2,1)S(1)}, bf16[256,2048]{1,0:T(8,128)(2,1)}, u32[]{:S(2)}, u32[]{:S(2)}) collective-permute-start(bf16[256,2048]{1,0:T(8,128)(2,1)S(1)} %collective-permute-done.1.refs_2_), channel_id=1, source_target_pairs={{1,2},{2,3},{5,6},{6,7},{9,10},{10,11},{13,14},{14,15},{17,18},{18... | collective-permute-start | bytes 3145736 | tf_op jit(solution)/shard_map/ppermute | solution.py:830
  68.9 201.8 %reduce-scatter.4.cloned.1.call-start = ((), (), s32[]{:S(2)}) async-start(), calls=%async_computation.6 | async-start | bytes 4718592 | tf_op jit(solution)/shard_map/reduce_scatter | solution.py:967
  70.6 22.9 %collective-permute-start.5 = (bf16[256,2048]{1,0:T(8,128)(2,1)}, bf16[256,2048]{1,0:T(8,128)(2,1)}, u32[]{:S(2)}, u32[]{:S(2)}) collective-permute-start(bf16[256,2048]{1,0:T(8,128)(2,1)} %collective-permute-done.3.refs_4_), channel_id=1, source_target_pairs={{2,3},{6,7},{10,11},{14,15},{18,19},{22,23},{26,27},{30,31}} | collective-permute-start | bytes 3145736 | tf_op jit(solution)/shard_map/ppermute | solution.py:830
  93.5 30.0 %collective-permute-start.7 = (bf16[256,2048]{1,0:T(8,128)(2,1)S(1)}, bf16[256,2048]{1,0:T(8,128)(2,1)S(1)}, u32[]{:S(2)}, u32[]{:S(2)}) collective-permute-start(bf16[256,2048]{1,0:T(8,128)(2,1)S(1)} %fusion.20.refs_0_), channel_id=1, source_target_pairs={{0,1},{1,2},{2,3},{4,5},{5,6},{6,7},{8,9},{9,10},{10,11},{12,13},{... | collective-permute-start | bytes 3145736 | tf_op jit(solution)/shard_map/ppermute | solution.py:830
  97.9 25.6 %collective-permute-start.6 = (bf16[256,2048]{1,0:T(8,128)(2,1)S(1)}, bf16[256,2048]{1,0:T(8,128)(2,1)}, u32[]{:S(2)}, u32[]{:S(2)}) collective-permute-start(bf16[256,2048]{1,0:T(8,128)(2,1)S(1)} %fusion.20.refs_0_), channel_id=1, source_target_pairs={{1,0},{2,1},{3,2},{5,4},{6,5},{7,6},{9,8},{10,9},{11,10},{13,12},{... | collective-permute-start | bytes 3145736 | tf_op jit(solution)/shard_map/ppermute | solution.py:829
  123.5 31.7 %collective-permute-start.8 = (bf16[256,2048]{1,0:T(8,128)(2,1)}, bf16[256,2048]{1,0:T(8,128)(2,1)S(1)}, u32[]{:S(2)}, u32[]{:S(2)}) collective-permute-start(bf16[256,2048]{1,0:T(8,128)(2,1)} %collective-permute-done.6.refs_1_), channel_id=1, source_target_pairs={{1,0},{2,1},{5,4},{6,5},{9,8},{10,9},{13,12},{14,13},{17,16},{18,1... | collective-permute-start | bytes 3145736 | tf_op jit(solution)/shard_map/ppermute | solution.py:829
  125.1 30.1 %collective-permute-start.9 = (bf16[256,2048]{1,0:T(8,128)(2,1)S(1)}, bf16[256,2048]{1,0:T(8,128)(2,1)}, u32[]{:S(2)}, u32[]{:S(2)}) collective-permute-start(bf16[256,2048]{1,0:T(8,128)(2,1)S(1)} %collective-permute-done.7.refs_2_), channel_id=1, source_target_pairs={{1,2},{2,3},{5,6},{6,7},{9,10},{10,11},{13,14},{14,15},{17,18},{18... | collective-permute-start | bytes 3145736 | tf_op jit(solution)/shard_map/ppermute | solution.py:830
  155.2 34.8 %collective-permute-start.13 = (bf16[256,2048]{1,0:T(8,128)(2,1)S(1)}, bf16[256,2048]{1,0:T(8,128)(2,1)}, u32[]{:S(2)}, u32[]{:S(2)}) collective-permute-start(bf16[256,2048]{1,0:T(8,128)(2,1)S(1)} %collective-permute-done.8.refs_3_), channel_id=1, source_target_pairs={{1,0},{5,4},{9,8},{13,12},{17,16},{21,20},{25,24},{29,28}} | collective-permute-start | bytes 3145736 | tf_op jit(solution)/shard_map/ppermute | solution.py:829
  156.9 33.1 %collective-permute-start.14 = (bf16[256,2048]{1,0:T(8,128)(2,1)}, bf16[256,2048]{1,0:T(8,128)(2,1)}, u32[]{:S(2)}, u32[]{:S(2)}) collective-permute-start(bf16[256,2048]{1,0:T(8,128)(2,1)} %collective-permute-done.9.refs_4_), channel_id=1, source_target_pairs={{2,3},{6,7},{10,11},{14,15},{18,19},{22,23},{26,27},{30,31}} | collective-permute-start | bytes 3145736 | tf_op jit(solution)/shard_map/ppermute | solution.py:830
  203.1 130.4 %reduce-scatter.6.cloned.1.call-start = ((), (), s32[]{:S(2)}) async-start(), calls=%async_computation.7 | async-start | bytes 4718592 | tf_op jit(solution)/shard_map/reduce_scatter | solution.py:975
  204.9 24.6 %collective-permute-start.16 = (bf16[256,2048]{1,0:T(8,128)(2,1)S(1)}, bf16[256,2048]{1,0:T(8,128)(2,1)}, u32[]{:S(2)}, u32[]{:S(2)}) collective-permute-start(bf16[256,2048]{1,0:T(8,128)(2,1)S(1)} %get-tuple-element.322), channel_id=1, source_target_pairs={{3,2},{7,6},{11,10},{15,14},{19,18},{23,22},{27,26},{31,30}} | collective-permute-start | bytes 3145736 | tf_op jit(solution)/shard_map/ppermute | solution.py:842
  206.2 23.3 %collective-permute-start.15 = (bf16[256,2048]{1,0:T(8,128)(2,1)S(1)}, bf16[256,2048]{1,0:T(8,128)(2,1)}, u32[]{:S(2)}, u32[]{:S(2)}) collective-permute-start(bf16[256,2048]{1,0:T(8,128)(2,1)S(1)} %get-tuple-element.323), channel_id=1, source_target_pairs={{0,1},{4,5},{8,9},{12,13},{16,17},{20,21},{24,25},{28,29}} | collective-permute-start | bytes 3145736 | tf_op jit(solution)/shard_map/ppermute | solution.py:841
  237.2 157.7 %reduce-scatter.8.cloned.1.call-start = ((), (), s32[]{:S(2)}) async-start(), calls=%async_computation.8 | async-start | bytes 5013504 | tf_op jit(solution)/shard_map/reduce_scatter | solution.py:995
  241.3 25.5 %collective-permute-start.18 = (bf16[256,2048]{1,0:T(8,128)(2,1)}, bf16[256,2048]{1,0:T(8,128)(2,1)}, u32[]{:S(2)}, u32[]{:S(2)}) collective-permute-start(bf16[256,2048]{1,0:T(8,128)(2,1)} %get-tuple-element.320), channel_id=1, source_target_pairs={{2,1},{3,2},{6,5},{7,6},{10,9},{11,10},{14,13},{15,14},{18,17},{19... | collective-permute-start | bytes 3145736 | tf_op jit(solution)/shard_map/ppermute | solution.py:842
  245.6 25.1 %collective-permute-start.17 = (bf16[256,2048]{1,0:T(8,128)(2,1)}, bf16[256,2048]{1,0:T(8,128)(2,1)}, u32[]{:S(2)}, u32[]{:S(2)}) collective-permute-start(bf16[256,2048]{1,0:T(8,128)(2,1)} %get-tuple-element.321), channel_id=1, source_target_pairs={{0,1},{1,2},{4,5},{5,6},{8,9},{9,10},{12,13},{13,14},{16,17},{17,1... | collective-permute-start | bytes 3145736 | tf_op jit(solution)/shard_map/ppermute | solution.py:841
  270.7 17.8 %collective-permute-start.21 = (f32[2,1024]{1,0:T(2,128)S(1)}, f32[2,1024]{1,0:T(2,128)S(1)}, u32[]{:S(2)}, u32[]{:S(2)}) collective-permute-start(f32[2,1024]{1,0:T(2,128)S(1)} %get-tuple-element.227.refs_0_), channel_id=1, source_target_pairs={{0,1},{1,2},{2,3},{3,0},{4,5},{5,6},{6,7},{7,4},{8,9},{9,10},{10,1... | collective-permute-start | bytes 24584 | tf_op jit(solution)/shard_map/ppermute | solution.py:856
  270.7 17.8 %collective-permute-start.20 = (f32[2,1024]{1,0:T(2,128)S(1)}, f32[2,1024]{1,0:T(2,128)S(1)}, u32[]{:S(2)}, u32[]{:S(2)}) collective-permute-start(f32[2,1024]{1,0:T(2,128)S(1)} %get-tuple-element.227.refs_0_), channel_id=1, source_target_pairs={{0,2},{1,3},{2,0},{3,1},{4,6},{5,7},{6,4},{7,5},{8,10},{9,11},{10,... | collective-permute-start | bytes 24584 | tf_op jit(solution)/shard_map/ppermute | solution.py:856
  271.7 16.8 %collective-permute-start.19 = (f32[2,1024]{1,0:T(2,128)S(1)}, f32[2,1024]{1,0:T(2,128)S(1)}, u32[]{:S(2)}, u32[]{:S(2)}) collective-permute-start(f32[2,1024]{1,0:T(2,128)S(1)} %get-tuple-element.227.refs_0_), channel_id=1, source_target_pairs={{0,3},{1,0},{2,1},{3,2},{4,7},{5,4},{6,5},{7,6},{8,11},{9,8},{10,9... | collective-permute-start | bytes 24584 | tf_op jit(solution)/shard_map/ppermute | solution.py:856
  272.7 47.1 %collective-permute-start.24 = (bf16[128,2048]{1,0:T(8,128)(2,1)}, bf16[128,2048]{1,0:T(8,128)(2,1)S(1)}, u32[]{:S(2)}, u32[]{:S(2)}) collective-permute-start(bf16[128,2048]{1,0:T(8,128)(2,1)} %reduce-scatter.4.cloned.1.call-done), channel_id=1, source_target_pairs={{0,0},{4,1},{8,2},{12,3},{16,4},{20,5},{24,6},{28,7},{1,8},{5,9},{... | collective-permute-start | bytes 1572872 | tf_op jit(solution)/shard_map/ppermute | solution.py:986
  290.9 30.1 %collective-permute-start.23 = (bf16[256,2048]{1,0:T(8,128)(2,1)S(1)}, bf16[256,2048]{1,0:T(8,128)(2,1)S(1)}, u32[]{:S(2)}, u32[]{:S(2)}) collective-permute-start(bf16[256,2048]{1,0:T(8,128)(2,1)S(1)} %get-tuple-element.318), channel_id=1, source_target_pairs={{1,0},{2,1},{3,2},{5,4},{6,5},{7,6},{9,8},{10,9},{11,10},{13,12},{... | collective-permute-start | bytes 3145736 | tf_op jit(solution)/shard_map/ppermute | solution.py:842
  295.7 25.3 %collective-permute-start.22 = (bf16[256,2048]{1,0:T(8,128)(2,1)S(1)}, bf16[256,2048]{1,0:T(8,128)(2,1)S(1)}, u32[]{:S(2)}, u32[]{:S(2)}) collective-permute-start(bf16[256,2048]{1,0:T(8,128)(2,1)S(1)} %get-tuple-element.319), channel_id=1, source_target_pairs={{0,1},{1,2},{2,3},{4,5},{5,6},{6,7},{8,9},{9,10},{10,11},{12,13},{... | collective-permute-start | bytes 3145736 | tf_op jit(solution)/shard_map/ppermute | solution.py:841
  334.5 22.6 %collective-permute-start.28 = (bf16[256,1024]{1,0:T(8,128)(2,1)S(1)}, bf16[256,1024]{1,0:T(8,128)(2,1)S(1)}, u32[]{:S(2)}, u32[]{:S(2)}) collective-permute-start(bf16[256,1024]{1,0:T(8,128)(2,1)S(1)} %copy-done.2), channel_id=1, source_target_pairs={{0,1},{1,2},{2,3},{4,5},{5,6},{6,7},{8,9},{9,10},{10,11},{12,13},{... | collective-permute-start | bytes 1572872 | tf_op jit(solution)/shard_map/ppermute | solution.py:830
  336.4 20.7 %collective-permute-start.27 = (bf16[256,1024]{1,0:T(8,128)(2,1)S(1)}, bf16[256,1024]{1,0:T(8,128)(2,1)S(1)}, u32[]{:S(2)}, u32[]{:S(2)}) collective-permute-start(bf16[256,1024]{1,0:T(8,128)(2,1)S(1)} %copy-done.2), channel_id=1, source_target_pairs={{1,0},{2,1},{3,2},{5,4},{6,5},{7,6},{9,8},{10,9},{11,10},{13,12},{... | collective-permute-start | bytes 1572872 | tf_op jit(solution)/shard_map/ppermute | solution.py:829
  340.8 19.9 %collective-permute-start.26 = (bf16[128,2048]{1,0:T(8,128)(2,1)S(1)}, bf16[128,2048]{1,0:T(8,128)(2,1)S(1)}, u32[]{:S(2)}, u32[]{:S(2)}) collective-permute-start(bf16[128,2048]{1,0:T(8,128)(2,1)S(1)} %collective-permute-done.24.refs_0_), channel_id=1, source_target_pairs={{0,1},{1,2},{2,3},{4,5},{5,6},{6,7},{8,9},{9,10},{10,11},{12,13},{... | collective-permute-start | bytes 1572872 | tf_op jit(solution)/shard_map/ppermute | solution.py:830
  342.7 19.2 %collective-permute-start.25 = (bf16[128,2048]{1,0:T(8,128)(2,1)S(1)}, bf16[128,2048]{1,0:T(8,128)(2,1)S(1)}, u32[]{:S(2)}, u32[]{:S(2)}) collective-permute-start(bf16[128,2048]{1,0:T(8,128)(2,1)S(1)} %collective-permute-done.24.refs_0_), channel_id=1, source_target_pairs={{1,0},{2,1},{3,2},{5,4},{6,5},{7,6},{9,8},{10,9},{11,10},{13,12},{... | collective-permute-start | bytes 1572872 | tf_op jit(solution)/shard_map/ppermute | solution.py:829
  361.9 16.0 %collective-permute-start.31 = (bf16[128,2048]{1,0:T(8,128)(2,1)S(1)}, bf16[128,2048]{1,0:T(8,128)(2,1)S(1)}, u32[]{:S(2)}, u32[]{:S(2)}) collective-permute-start(bf16[128,2048]{1,0:T(8,128)(2,1)S(1)} %collective-permute-done.25.refs_1_), channel_id=1, source_target_pairs={{1,0},{2,1},{5,4},{6,5},{9,8},{10,9},{13,12},{14,13},{17,16},{18,1... | collective-permute-start | bytes 1572872 | tf_op jit(solution)/shard_map/ppermute | solution.py:829
  366.6 27.3 %collective-permute-start.30 = (bf16[256,2048]{1,0:T(8,128)(2,1)S(1)}, bf16[256,2048]{1,0:T(8,128)(2,1)S(1)}, u32[]{:S(2)}, u32[]{:S(2)}) collective-permute-start(bf16[256,2048]{1,0:T(8,128)(2,1)S(1)} %get-tuple-element.316), channel_id=1, source_target_pairs={{3,2},{7,6},{11,10},{15,14},{19,18},{23,22},{27,26},{31,30}} | collective-permute-start | bytes 3145736 | tf_op jit(solution)/shard_map/ppermute | solution.py:842
  367.9 27.1 %collective-permute-start.29 = (bf16[256,2048]{1,0:T(8,128)(2,1)S(1)}, bf16[256,2048]{1,0:T(8,128)(2,1)}, u32[]{:S(2)}, u32[]{:S(2)}) collective-permute-start(bf16[256,2048]{1,0:T(8,128)(2,1)S(1)} %get-tuple-element.317), channel_id=1, source_target_pairs={{0,1},{4,5},{8,9},{12,13},{16,17},{20,21},{24,25},{28,29}} | collective-permute-start | bytes 3145736 | tf_op jit(solution)/shard_map/ppermute | solution.py:841
  369.5 17.0 %collective-permute-start.32 = (bf16[128,2048]{1,0:T(8,128)(2,1)S(1)}, bf16[128,2048]{1,0:T(8,128)(2,1)S(1)}, u32[]{:S(2)}, u32[]{:S(2)}) collective-permute-start(bf16[128,2048]{1,0:T(8,128)(2,1)S(1)} %collective-permute-done.26.refs_2_), channel_id=1, source_target_pairs={{1,2},{2,3},{5,6},{6,7},{9,10},{10,11},{13,14},{14,15},{17,18},{18... | collective-permute-start | bytes 1572872 | tf_op jit(solution)/shard_map/ppermute | solution.py:830
  377.9 16.0 %collective-permute-start.34 = (bf16[256,1024]{1,0:T(8,128)(2,1)S(1)}, bf16[256,1024]{1,0:T(8,128)(2,1)S(1)}, u32[]{:S(2)}, u32[]{:S(2)}) collective-permute-start(bf16[256,1024]{1,0:T(8,128)(2,1)S(1)} %collective-permute-done.28.refs_9_), channel_id=1, source_target_pairs={{1,2},{2,3},{5,6},{6,7},{9,10},{10,11},{13,14},{14,15},{17,18},{18... | collective-permute-start | bytes 1572872 | tf_op jit(solution)/shard_map/ppermute | solution.py:830
  396.2 16.8 %collective-permute-start.42 = (bf16[256,1024]{1,0:T(8,128)(2,1)S(1)}, bf16[256,1024]{1,0:T(8,128)(2,1)}, u32[]{:S(2)}, u32[]{:S(2)}) collective-permute-start(bf16[256,1024]{1,0:T(8,128)(2,1)S(1)} %slice.44.refs_0_), channel_id=1, source_target_pairs={{0,1},{1,2},{2,3},{4,5},{5,6},{6,7},{8,9},{9,10},{10,11},{12,13},{... | collective-permute-start | bytes 1572872 | tf_op jit(solution)/shard_map/ppermute | solution.py:830
  400.6 14.3 %collective-permute-start.39 = (bf16[256,1024]{1,0:T(8,128)(2,1)}, bf16[256,1024]{1,0:T(8,128)(2,1)S(1)}, u32[]{:S(2)}, u32[]{:S(2)}) collective-permute-start(bf16[256,1024]{1,0:T(8,128)(2,1)} %copy-done.15), channel_id=1, source_target_pairs={{1,0},{5,4},{9,8},{13,12},{17,16},{21,20},{25,24},{29,28}} | collective-permute-start | bytes 1572872 | tf_op jit(solution)/shard_map/ppermute | solution.py:829
  401.3 18.2 %collective-permute-start.40 = (bf16[256,1024]{1,0:T(8,128)(2,1)}, bf16[256,1024]{1,0:T(8,128)(2,1)}, u32[]{:S(2)}, u32[]{:S(2)}) collective-permute-start(bf16[256,1024]{1,0:T(8,128)(2,1)} %copy-done.53), channel_id=1, source_target_pairs={{2,3},{6,7},{10,11},{14,15},{18,19},{22,23},{26,27},{30,31}} | collective-permute-start | bytes 1572872 | tf_op jit(solution)/shard_map/ppermute | solution.py:830
  406.2 47.1 %collective-permute-start.36 = (bf16[256,2048]{1,0:T(8,128)(2,1)S(1)}, bf16[256,2048]{1,0:T(8,128)(2,1)S(1)}, u32[]{:S(2)}, u32[]{:S(2)}) collective-permute-start(bf16[256,2048]{1,0:T(8,128)(2,1)S(1)} %get-tuple-element.314), channel_id=1, source_target_pairs={{2,1},{3,2},{6,5},{7,6},{10,9},{11,10},{14,13},{15,14},{18,17},{19... | collective-permute-start | bytes 3145736 | tf_op jit(solution)/shard_map/ppermute | solution.py:842
  408.6 44.7 %collective-permute-start.35 = (bf16[256,2048]{1,0:T(8,128)(2,1)S(1)}, bf16[256,2048]{1,0:T(8,128)(2,1)S(1)}, u32[]{:S(2)}, u32[]{:S(2)}) collective-permute-start(bf16[256,2048]{1,0:T(8,128)(2,1)S(1)} %get-tuple-element.315), channel_id=1, source_target_pairs={{0,1},{1,2},{4,5},{5,6},{8,9},{9,10},{12,13},{13,14},{16,17},{17,1... | collective-permute-start | bytes 3145736 | tf_op jit(solution)/shard_map/ppermute | solution.py:841
  413.0 40.3 %collective-permute-start.41 = (bf16[256,1024]{1,0:T(8,128)(2,1)S(1)}, bf16[256,1024]{1,0:T(8,128)(2,1)}, u32[]{:S(2)}, u32[]{:S(2)}) collective-permute-start(bf16[256,1024]{1,0:T(8,128)(2,1)S(1)} %slice.44.refs_0_), channel_id=1, source_target_pairs={{1,0},{2,1},{3,2},{5,4},{6,5},{7,6},{9,8},{10,9},{11,10},{13,12},{... | collective-permute-start | bytes 1572872 | tf_op jit(solution)/shard_map/ppermute | solution.py:829
  415.0 38.3 %collective-permute-start.37 = (bf16[128,2048]{1,0:T(8,128)(2,1)S(1)}, bf16[128,2048]{1,0:T(8,128)(2,1)S(1)}, u32[]{:S(2)}, u32[]{:S(2)}) collective-permute-start(bf16[128,2048]{1,0:T(8,128)(2,1)S(1)} %copy-done.18), channel_id=1, source_target_pairs={{1,0},{5,4},{9,8},{13,12},{17,16},{21,20},{25,24},{29,28}} | collective-permute-start | bytes 1572872 | tf_op jit(solution)/shard_map/ppermute | solution.py:829
  419.6 33.7 %collective-permute-start.38 = (bf16[128,2048]{1,0:T(8,128)(2,1)S(1)}, bf16[128,2048]{1,0:T(8,128)(2,1)S(1)}, u32[]{:S(2)}, u32[]{:S(2)}) collective-permute-start(bf16[128,2048]{1,0:T(8,128)(2,1)S(1)} %copy-done.21), channel_id=1, source_target_pairs={{2,3},{6,7},{10,11},{14,15},{18,19},{22,23},{26,27},{30,31}} | collective-permute-start | bytes 1572872 | tf_op jit(solution)/shard_map/ppermute | solution.py:830
  455.6 38.3 %collective-permute-start.44 = (bf16[256,2048]{1,0:T(8,128)(2,1)}, bf16[256,2048]{1,0:T(8,128)(2,1)}, u32[]{:S(2)}, u32[]{:S(2)}) collective-permute-start(bf16[256,2048]{1,0:T(8,128)(2,1)} %get-tuple-element.312), channel_id=1, source_target_pairs={{1,0},{2,1},{3,2},{5,4},{6,5},{7,6},{9,8},{10,9},{11,10},{13,12},{... | collective-permute-start | bytes 3145736 | tf_op jit(solution)/shard_map/ppermute | solution.py:842
  457.5 36.4 %collective-permute-start.43 = (bf16[256,2048]{1,0:T(8,128)(2,1)}, bf16[256,2048]{1,0:T(8,128)(2,1)}, u32[]{:S(2)}, u32[]{:S(2)}) collective-permute-start(bf16[256,2048]{1,0:T(8,128)(2,1)} %get-tuple-element.313), channel_id=1, source_target_pairs={{0,1},{1,2},{2,3},{4,5},{5,6},{6,7},{8,9},{9,10},{10,11},{12,13},{... | collective-permute-start | bytes 3145736 | tf_op jit(solution)/shard_map/ppermute | solution.py:841
  462.4 26.8 %collective-permute-start.45 = (bf16[256,1024]{1,0:T(8,128)(2,1)}, bf16[256,1024]{1,0:T(8,128)(2,1)}, u32[]{:S(2)}, u32[]{:S(2)}) collective-permute-start(bf16[256,1024]{1,0:T(8,128)(2,1)} %collective-permute-done.41.refs_1_), channel_id=1, source_target_pairs={{1,0},{2,1},{5,4},{6,5},{9,8},{10,9},{13,12},{14,13},{17,16},{18,1... | collective-permute-start | bytes 1572872 | tf_op jit(solution)/shard_map/ppermute | solution.py:829
  464.9 29.0 %collective-permute-start.46 = (bf16[256,1024]{1,0:T(8,128)(2,1)}, bf16[256,1024]{1,0:T(8,128)(2,1)}, u32[]{:S(2)}, u32[]{:S(2)}) collective-permute-start(bf16[256,1024]{1,0:T(8,128)(2,1)} %collective-permute-done.42.refs_2_), channel_id=1, source_target_pairs={{1,2},{2,3},{5,6},{6,7},{9,10},{10,11},{13,14},{14,15},{17,18},{18... | collective-permute-start | bytes 1572872 | tf_op jit(solution)/shard_map/ppermute | solution.py:830
  (68 other events, 975.7 us)
Sparse Core Ops, SparseCore 0:
  9.9 37.7 all-gather.5
  49.6 36.7 all-gather.7
  88.3 89.8 all-gather.9
  203.2 51.3 reduce-scatter.3
  258.1 58.5 reduce-scatter.5
  333.6 53.3 reduce-scatter.7

commit v3 on v2

--- a/solution.py
+++ b/solution.py
@@ -663,29 +663,38 @@
     return [own] + [x for pair in hops for x in pair]
 
 
-def assemble(place, own_mix, mix_hops, own_gate, gate_hops, copies):
-    rows, width = own_mix.shape
-    count = len(mix_hops) + 1
+def assemble_half_kernel(count, kept, at_ref, *refs):
+    assemble_kernel(count, at_ref, *(refs[1:] if kept else refs))
+
+
+def assemble_half(place, own, hops, copies, half, kept):
+    rows, width = own.shape
+    count = len(hops) + 1
     heads = count // copies
 
     def out_map(i, at):
-        half = i // count
-        source = lax.rem(i - half * count + at[0], count)
-        return (0, half * heads + source // copies)
-
-    parts = flat(own_mix, mix_hops) + flat(own_gate, gate_hops)
-    return call(
-        partial(assemble_kernel, count),
-        place,
-        2 * count,
-        [whole((rows, width))] * len(parts),
-        pl.BlockSpec((rows, width), out_map),
-        jax.ShapeDtypeStruct((rows, 2 * heads * width), f32),
-        [],
-        cost(0, 12 * count * rows * width),
-        "assemble",
-        *parts,
-    )
+        return (0, half * heads + lax.rem(i + at[0], count) // copies)
+
+    parts = flat(own, hops)
+    specs = [whole((rows, width))] * len(parts)
+    aliases = {}
+    if kept is not None:
+        parts, specs = [kept] + parts, [pl.BlockSpec(memory_space=pl.ANY)] + specs
+        aliases = {1: 0}
+    return pl.pallas_call(
+        partial(assemble_half_kernel, count, kept is not None),
+        grid_spec=pltpu.PrefetchScalarGridSpec(
+            num_scalar_prefetch=1,
+            grid=(count,),
+            in_specs=specs,
+            out_specs=pl.BlockSpec((rows, width), out_map),
+        ),
+        out_shape=jax.ShapeDtypeStruct((rows, 2 * heads * width), f32),
+        input_output_aliases=aliases,
+        compiler_params=kernel_params(),
+        cost_estimate=cost(0, 6 * count * rows * width),
+        name="assemble_half",
+    )(place, *parts)
 
 
 def assemble_rows(place, own, hops):
@@ -1035,7 +1044,8 @@
     down_total = assemble_rows(place, down_part, down_hops)
     totals = unpack(small, gain, per, taps, heads, block)
     bias_total = totals[5][0, : 2 * heads].reshape(heads, 2).T.reshape(-1)
-    up_total = assemble(place, mix_grad_part, mix_hops, gate_grad_part, gate_hops, copies)
+    up_total = assemble_half(place, gate_grad_part, gate_hops, copies, 1, None)
+    up_total = assemble_half(place, mix_grad_part, mix_hops, copies, 0, up_total)
     return (
         outputs,
         input_grad,

time: 534 us -> 534 us (level)
    pallas_call x8 -> x7, Pallas kernels: 86.1 us -> 79.3 us  [call(): pl.pallas_call(kernel, grid_spec=pltpu.PrefetchScalarGridSpec(num_scalar_...]
    pallas_call x0 -> x2, Pallas kernels: none -> 6.65 us  [assemble_half(): pl.pallas_call(partial(assemble_half_kernel, count, kept is not None), gr...]
    unnamed x122 -> x130, local copies, waits for them, and re-layouts: 17.3 us -> 21.7 us
  transfers between devices with their start and end apart: 55 -> 55, of which waited for: 21 -> 19; matrix products, arithmetic and copies ran while one was open for 16% -> 16% of each run, Pallas kernels for 20% -> 21%
where the time goes in v3:
time: 534 us; the launch traced here: 525 us
  waiting for transfers between devices  123 us (23%)
  starting transfers between devices  120 us (22%)
  Pallas kernels  117 us (22%)
  matrix products  60.8 us (11%)
  local copies, waits for them, and re-layouts  31.7 us (6%)
  blocking collectives  28.6 us (5%)
  other arithmetic  28 us (5%)
  between operations  16.4 us (3%)
    pallas_call x7, Pallas kernels, call(): pl.pallas_call(kernel, grid_spec=pltpu.PrefetchScalarGridSpec(num_scalar_...  79.3 us
    ppermute x15, waiting for transfers between devices, pass_on(): lax.ppermute(pair[1], axis, [(i, i + 1) for i in range(s - 1, n - 1)])  66.4 us
    ppermute x15, starting transfers between devices, pass_on(): lax.ppermute(pair[1], axis, [(i, i + 1) for i in range(s - 1, n - 1)])  49.2 us
    ppermute x15, waiting for transfers between devices, pass_on(): lax.ppermute(pair[0], axis, [(i, i - 1) for i in range(1, n - s + 1)])  46.8 us
    ppermute x15, starting transfers between devices, pass_on(): lax.ppermute(pair[0], axis, [(i, i - 1) for i in range(1, n - s + 1)])  32.5 us
    dot_general x3, matrix products, dot_nn(): lax.dot_general(a, b, (((1,), (0,)), ((), ())), preferred_element_type=f32)  23.9 us
    unnamed x130, local copies, waits for them, and re-layouts  21.7 us
    dot_general x2, matrix products, dot_nt(): lax.dot_general(a, b, (((1,), (1,)), ((), ())), preferred_element_type=f32)  20.8 us
  transfers between devices with their start and end apart: 55, of which 19 were waited for; matrix products, arithmetic and copies ran while one was open for 16% of the time, Pallas kernels for 21%

profile of v3, /device:TPU:16, one launch (start us, length us, event | category | flops | bytes accessed | tf_op | source)
XLA Modules:
  0.0 525.4 jit_solution(5898693178923238175)
XLA Ops:
  10.8 3.5 collective-permute-start.1
  16.7 20.9 %collective-permute-done.1.refs_2_ = bf16[256,2048]{1,0:T(8,128)(2,1)S(1)} collective-permute-done((bf16[256,2048]{1,0:T(8,128)(2,1)S(1)}, bf16[256,2048]{1,0:T(8,128)(2,1)S(1)}, u32[]{:S(2)}, u32[]{:S(2)}) %collective-permute-start.1) | collective-permute-done | bytes 1048608 | tf_op jit(solution)/shard_map/ppermute | solution.py:839
  37.6 3.2 collective-permute-done.refs_1_
  45.3 19.3 %collective-permute-done.2.refs_3_ = bf16[256,2048]{1,0:T(8,128)(2,1)S(1)} collective-permute-done((bf16[256,2048]{1,0:T(8,128)(2,1)S(1)}, bf16[256,2048]{1,0:T(8,128)(2,1)S(1)}, u32[]{:S(2)}, u32[]{:S(2)}) %collective-permute-start.2) | collective-permute-done | bytes 1048608 | tf_op jit(solution)/shard_map/ppermute | solution.py:838
  65.6 3.3 collective-permute-done.3.refs_4_
  70.6 3.2 collective-permute-start.5
  77.6 15.9 %collective-permute-done.5.refs_6_ = bf16[256,2048]{1,0:T(8,128)(2,1)} collective-permute-done((bf16[256,2048]{1,0:T(8,128)(2,1)}, bf16[256,2048]{1,0:T(8,128)(2,1)}, u32[]{:S(2)}, u32[]{:S(2)}) %collective-permute-start.5) | collective-permute-done | bytes 1048608 | tf_op jit(solution)/shard_map/ppermute | solution.py:839
  93.5 4.4 collective-permute-start.7
  101.2 4.5 merge.2.x_ref
  105.7 7.8 %convolution_convert_fusion.3.mix_ref.prev_ref = bf16[1024,1024]{1,0:T(8,128)(2,1)} fusion(bf16[1024,2048]{1,0:T(8,128)(2,1)} %merge.2.x_ref, bf16[2048,1024]{1,0:T(8,128)(2,1)S(1)} %copy-done.63), kind=kOutput, calls=%fused_computation.37 | convolution fusion | flops 4296015872 | bytes 10485760 | tf_op jit(solution)/shard_map/dot_general | solution.py:16
  113.5 10.0 %fusion.26.gin_ref = f32[1024,1024]{1,0:T(8,128)} fusion(bf16[1024,2048]{1,0:T(8,128)(2,1)} %merge.2.x_ref, bf16[2048,1024]{1,0:T(8,128)(2,1)} %all-gather.8.cloned.1.call-done), kind=kOutput, calls=%fused_computation.67 | convolution fusion | flops 4294967296 | bytes 12582912 | tf_op jit(solution)/shard_map/dot_general | solution.py:16
  125.1 3.8 collective-permute-start.9
  129.7 13.0 %front.1 = (f32[1024,1024]{1,0:T(8,128)}, bf16[1024,1024]{1,0:T(8,128)(2,1)S(1)}, bf16[1024,1024]{1,0:T(8,128)(2,1)S(1)}, bf16[1024,1024]{1,0:T(8,128)(2,1)}, f32[8,1024]{1,0:T(8,128)S(1)}) custom-call(s32[1]{0:T(128)} %bitcast.3.at_ref.head_ref, bf16[1024,1024]{1,0:T(8,128)(2,1)} %convolution_convert_fusion.3.mix_ref.prev_ref, ...), custom_call_target="tpu_custom_call" | custom-call | flops 6000000000 | bytes 12582912 | tf_op jit(solution)/shard_map/front/pallas_call | solution.py:59
  156.9 5.6 %collective-permute-start.14 = (bf16[256,2048]{1,0:T(8,128)(2,1)}, bf16[256,2048]{1,0:T(8,128)(2,1)}, u32[]{:S(2)}, u32[]{:S(2)}) collective-permute-start(bf16[256,2048]{1,0:T(8,128)(2,1)} %collective-permute-done.9.refs_4_), channel_id=1, source_target_pairs={{2,3},{6,7},{10,11},{14,15},{18,19},{22,23},{26,27},{30,31}} | collective-permute-start | bytes 3145736 | tf_op jit(solution)/shard_map/ppermute | solution.py:839
  163.2 15.0 %cell.1 = (bf16[1024,1024]{1,0:T(8,128)(2,1)S(1)}, f32[1024,1024]{1,0:T(8,128)}, bf16[1024,1024]{1,0:T(8,128)(2,1)S(1)}) custom-call(s32[1]{0:T(128)} %bitcast.3.at_ref.head_ref, f32[8,1024]{1,0:T(8,128)S(1)} %copy-done.33, bf16[1024,1024]{1,0:T(8,128)(2,1)} %copy-done.3, bf16[1024,1024]{1,0:T(8,128)(2,1)} %copy-done.5, ...), custom_call_target="tpu_custom_call" | custom-call | flops 2684354560 | bytes 20971520 | tf_op jit(solution)/shard_map/cell/pallas_call | solution.py:59
  183.8 6.1 %convolution_convert_fusion.2 = bf16[1024,2048]{1,0:T(8,128)(2,1)} fusion(bf16[1024,1024]{1,0:T(8,128)(2,1)S(1)} %copy-done.39, bf16[1024,2048]{1,0:T(8,128)(2,1)S(1)} %constant_dynamic-slice_fusion.down_ref), kind=kOutput, calls=%fused_computation.3 | convolution fusion | flops 4297064448 | bytes 10485760 | tf_op jit(solution)/shard_map/dot_general | solution.py:16
  190.0 4.8 merge.3.bg_ref
  194.7 8.3 %convolution_convert_fusion.1 = bf16[1024,2048]{1,0:T(8,128)(2,1)} fusion(bf16[1024,1024]{1,0:T(8,128)(2,1)S(1)} %copy-done.39, bf16[1024,2048]{1,0:T(8,128)(2,1)} %merge.3.bg_ref), kind=kOutput, calls=%fused_computation.2 | convolution fusion | flops 4297064448 | bytes 10485760 | tf_op jit(solution)/shard_map/dot_general | solution.py:24
  207.8 17.4 %tail_back.1 = (bf16[1024,1024]{1,0:T(8,128)(2,1)S(1)}, bf16[1024,1024]{1,0:T(8,128)(2,1)}, f32[1024,1024]{1,0:T(8,128)}, f32[16,1024]{1,0:T(8,128)S(1)}) custom-call(s32[1]{0:T(128)} %bitcast.3.at_ref.head_ref, bf16[1024,2048]{1,0:T(8,128)(2,1)} %merge.3.bg_ref, f32[1024,1024]{1,0:T(8,128)} %get-tuple-element.204.num_ref, ...), custom_call_target="tpu_custom_call" | custom-call | flops 4294967296 | bytes 25165824 | tf_op jit(solution)/shard_map/tail_back/pallas_call | solution.py:59
  229.5 7.7 %convolution_convert_fusion = bf16[2048,1024]{1,0:T(8,128)(2,1)} fusion(bf16[1024,2048]{1,0:T(8,128)(2,1)S(1)} %copy-done.51, bf16[1024,1024]{1,0:T(8,128)(2,1)} %get-tuple-element.222), kind=kOutput, calls=%fused_computation.1 | convolution fusion | flops 4297064448 | bytes 10485760 | tf_op jit(solution)/shard_map/dot_general | solution.py:24
  237.3 4.0 fusion.17
  241.4 4.2 collective-permute-start.18
  249.0 17.9 %cell_back.1 = (f32[1024,1024]{1,0:T(8,128)}, f32[1024,1024]{1,0:T(8,128)}, f32[1024,1024]{1,0:T(8,128)}, f32[2,1024]{1,0:T(2,128)S(1)}) custom-call(f32[8,1024]{1,0:T(8,128)S(1)} %copy-done.34, bf16[1024,1024]{1,0:T(8,128)(2,1)S(1)} %copy-done.4, bf16[1024,1024]{1,0:T(8,128)(2,1)S(1)} %copy-done.6, bf16[1024,1024]{1,0:T(8,128)(2,1)} %get-tuple-element.186.v_ref, ...), custom_call_target="tpu_custom_call" | custom-call | flops 5368709120 | bytes 25165824 | tf_op jit(solution)/shard_map/cell_back/pallas_call | solution.py:450
  266.9 3.9 collective-permute-done.17
  272.8 5.0 collective-permute-start.24
  277.8 10.8 %fusion.27 = f32[1024,2048]{1,0:T(8,128)} fusion(bf16[1024,1024]{1,0:T(8,128)(2,1)} %get-tuple-element.222, bf16[2048,1024]{1,0:T(8,128)(2,1)} %all-gather.8.cloned.1.call-done), kind=kOutput, calls=%fused_computation.68 | convolution fusion | flops 4294967296 | bytes 14680064 | tf_op jit(solution)/shard_map/dot_general | solution.py:20
  291.0 4.7 collective-permute-start.23
  297.7 22.1 %back.1 = (bf16[1024,1024]{1,0:T(8,128)(2,1)S(1)}, f32[48,1024]{1,0:T(8,128)S(1)}) custom-call(s32[1]{0:T(128)} %bitcast.3.at_ref.head_ref, f32[1024,1024]{1,0:T(8,128)} %get-tuple-element.223.dq_ref, f32[1024,1024]{1,0:T(8,128)} %get-tuple-element.224.dk_ref, f32[1024,1024]{1,0:T(8,128)} %get-tuple-element.225.dv_ref, bf16[1024,1024]{1,0:T(8,128)(2,1)S(1)} %copy-done.4, ...), custom_call_target="tpu_custom_call" | custom-call | flops 12000000000 | bytes 31457280 | tf_op jit(solution)/shard_map/back/pallas_call | solution.py:59
  324.2 9.4 %mix_grads.1 = bf16[8,272,1024]{2,1,0:T(8,128)(2,1)} custom-call(bf16[1024,2048]{1,0:T(8,128)(2,1)} %merge.2.x_ref, bf16[1024,1024]{1,0:T(8,128)(2,1)S(1)} %copy-done.41, f32[8,6,1024]{2,1,0:T(8,128)S(1)} %reshape.101.pack_ref), custom_call_target="tpu_custom_call" | custom-call | flops 4294967296 | bytes 12582912 | tf_op jit(solution)/shard_map/mix_grads/pallas_call | solution.py:732
  336.5 4.3 collective-permute-start.27
  342.8 4.2 collective-permute-start.25
  347.0 10.1 %add_convert_fusion = bf16[1024,2048]{1,0:T(8,128)(2,1)S(1)} fusion(f32[1024,2048]{1,0:T(8,128)} %fusion.27, bf16[1024,1024]{1,0:T(8,128)(2,1)} %copy-done.40, bf16[2048,1024]{1,0:T(8,128)(2,1)} %all-gather.6.cloned.1.call-done), kind=kOutput, calls=%fused_computation | convolution fusion | flops 4299161600 | bytes 18874368 | tf_op jit(solution)/shard_map/dot_general | solution.py:20
  357.2 3.6 collective-permute-done.26.refs_2_
  362.0 4.4 collective-permute-start.31
  369.6 4.6 collective-permute-start.32
  386.7 7.3 %collective-permute-done.34.refs_4_ = bf16[256,1024]{1,0:T(8,128)(2,1)S(1)} collective-permute-done((bf16[256,1024]{1,0:T(8,128)(2,1)S(1)}, bf16[256,1024]{1,0:T(8,128)(2,1)S(1)}, u32[]{:S(2)}, u32[]{:S(2)}) %collective-permute-start.34) | collective-permute-done | bytes 524320 | tf_op jit(solution)/shard_map/ppermute | solution.py:839
  396.9 4.5 collective-permute-start.42
  410.0 3.8 collective-permute-done.42.refs_3_
  416.4 4.0 collective-permute-done.40.refs_6_
  420.5 4.3 collective-permute-start.38
  425.3 14.1 %all-gather = bf16[64,1024]{1,0:T(8,128)(2,1)S(1)} all-gather(bf16[8,1024]{1,0:T(8,128)(2,1)S(1)} %slice_select_fusion), channel_id=2, replica_groups=mesh['dp'=8,'ctx'=4] {'dp'}, dimensions={0}, use_global_device_ids=true | all-gather | bytes 147456 | tf_op jit(solution)/shard_map/all_gather | solution.py:1034
  439.4 14.5 %all-gather.1 = bf16[32,8,1024]{2,1,0:T(8,128)(2,1)S(1)} all-gather(bf16[8,8,1024]{2,1,0:T(8,128)(2,1)S(1)} %bitcast.94), channel_id=3, replica_groups=mesh['dp'=8,'ctx'=4] {'ctx'}, dimensions={0}, use_global_device_ids=true | all-gather | bytes 655360 | tf_op jit(solution)/shard_map/all_gather | solution.py:1035
  459.7 4.9 collective-permute-start.43
  470.9 20.5 %collective-permute-done.45.refs_4_ = bf16[256,1024]{1,0:T(8,128)(2,1)} collective-permute-done((bf16[256,1024]{1,0:T(8,128)(2,1)}, bf16[256,1024]{1,0:T(8,128)(2,1)}, u32[]{:S(2)}, u32[]{:S(2)}) %collective-permute-start.45) | collective-permute-done | bytes 524320 | tf_op jit(solution)/shard_map/ppermute | solution.py:838
  491.4 4.6 collective-permute-done.46.refs_5_
  500.1 4.4 collective-permute-start.48
  509.7 4.3 fusion.12
  514.0 4.1 assemble_half.3
  (266 shorter events, 122.5 us)
Async XLA Ops:
  7.2 61.7 %all-gather.6.cloned.1.call-start = ((), (), s32[]{:S(2)}) async-start(), calls=%async_computation.3 | async-start | bytes 4718592 | tf_op jit(solution)/shard_map/all_gather | solution.py:922
  9.7 103.9 %all-gather.8.cloned.1.call-start = ((), (), s32[]{:S(2)}) async-start(), calls=%async_computation.4 | async-start | bytes 4718592 | tf_op jit(solution)/shard_map/all_gather | solution.py:925
  10.8 26.8 %collective-permute-start.1 = (bf16[256,2048]{1,0:T(8,128)(2,1)S(1)}, bf16[256,2048]{1,0:T(8,128)(2,1)S(1)}, u32[]{:S(2)}, u32[]{:S(2)}) collective-permute-start(bf16[256,2048]{1,0:T(8,128)(2,1)S(1)} %fusion.7.refs_0_), channel_id=1, source_target_pairs={{0,1},{1,2},{2,3},{4,5},{5,6},{6,7},{8,9},{9,10},{10,11},{12,13},{... | collective-permute-start | bytes 3145736 | tf_op jit(solution)/shard_map/ppermute | solution.py:839
  14.3 26.5 %collective-permute-start = (bf16[256,2048]{1,0:T(8,128)(2,1)S(1)}, bf16[256,2048]{1,0:T(8,128)(2,1)S(1)}, u32[]{:S(2)}, u32[]{:S(2)}) collective-permute-start(bf16[256,2048]{1,0:T(8,128)(2,1)S(1)} %fusion.7.refs_0_), channel_id=1, source_target_pairs={{1,0},{2,1},{3,2},{5,4},{6,5},{7,6},{9,8},{10,9},{11,10},{13,12},{... | collective-permute-start | bytes 3145736 | tf_op jit(solution)/shard_map/ppermute | solution.py:838
  40.9 140.0 %all-gather.10.cloned.1.call-start = ((), (), s32[]{:S(2)}) async-start(), calls=%async_computation.5 | async-start | bytes 18874368 | tf_op jit(solution)/shard_map/all_gather | solution.py:930
  40.9 23.7 %collective-permute-start.2 = (bf16[256,2048]{1,0:T(8,128)(2,1)S(1)}, bf16[256,2048]{1,0:T(8,128)(2,1)S(1)}, u32[]{:S(2)}, u32[]{:S(2)}) collective-permute-start(bf16[256,2048]{1,0:T(8,128)(2,1)S(1)} %collective-permute-done.refs_1_), channel_id=1, source_target_pairs={{1,0},{2,1},{5,4},{6,5},{9,8},{10,9},{13,12},{14,13},{17,16},{18,1... | collective-permute-start | bytes 3145736 | tf_op jit(solution)/shard_map/ppermute | solution.py:838
  43.3 25.5 %collective-permute-start.3 = (bf16[256,2048]{1,0:T(8,128)(2,1)S(1)}, bf16[256,2048]{1,0:T(8,128)(2,1)}, u32[]{:S(2)}, u32[]{:S(2)}) collective-permute-start(bf16[256,2048]{1,0:T(8,128)(2,1)S(1)} %collective-permute-done.1.refs_2_), channel_id=1, source_target_pairs={{1,2},{2,3},{5,6},{6,7},{9,10},{10,11},{13,14},{14,15},{17,18},{18... | collective-permute-start | bytes 3145736 | tf_op jit(solution)/shard_map/ppermute | solution.py:839
  68.9 201.8 %reduce-scatter.4.cloned.1.call-start = ((), (), s32[]{:S(2)}) async-start(), calls=%async_computation.6 | async-start | bytes 4718592 | tf_op jit(solution)/shard_map/reduce_scatter | solution.py:976
  70.6 22.9 %collective-permute-start.5 = (bf16[256,2048]{1,0:T(8,128)(2,1)}, bf16[256,2048]{1,0:T(8,128)(2,1)}, u32[]{:S(2)}, u32[]{:S(2)}) collective-permute-start(bf16[256,2048]{1,0:T(8,128)(2,1)} %collective-permute-done.3.refs_4_), channel_id=1, source_target_pairs={{2,3},{6,7},{10,11},{14,15},{18,19},{22,23},{26,27},{30,31}} | collective-permute-start | bytes 3145736 | tf_op jit(solution)/shard_map/ppermute | solution.py:839
  93.5 30.0 %collective-permute-start.7 = (bf16[256,2048]{1,0:T(8,128)(2,1)S(1)}, bf16[256,2048]{1,0:T(8,128)(2,1)S(1)}, u32[]{:S(2)}, u32[]{:S(2)}) collective-permute-start(bf16[256,2048]{1,0:T(8,128)(2,1)S(1)} %fusion.20.refs_0_), channel_id=1, source_target_pairs={{0,1},{1,2},{2,3},{4,5},{5,6},{6,7},{8,9},{9,10},{10,11},{12,13},{... | collective-permute-start | bytes 3145736 | tf_op jit(solution)/shard_map/ppermute | solution.py:839
  97.9 25.7 %collective-permute-start.6 = (bf16[256,2048]{1,0:T(8,128)(2,1)S(1)}, bf16[256,2048]{1,0:T(8,128)(2,1)}, u32[]{:S(2)}, u32[]{:S(2)}) collective-permute-start(bf16[256,2048]{1,0:T(8,128)(2,1)S(1)} %fusion.20.refs_0_), channel_id=1, source_target_pairs={{1,0},{2,1},{3,2},{5,4},{6,5},{7,6},{9,8},{10,9},{11,10},{13,12},{... | collective-permute-start | bytes 3145736 | tf_op jit(solution)/shard_map/ppermute | solution.py:838
  123.5 31.7 %collective-permute-start.8 = (bf16[256,2048]{1,0:T(8,128)(2,1)}, bf16[256,2048]{1,0:T(8,128)(2,1)S(1)}, u32[]{:S(2)}, u32[]{:S(2)}) collective-permute-start(bf16[256,2048]{1,0:T(8,128)(2,1)} %collective-permute-done.6.refs_1_), channel_id=1, source_target_pairs={{1,0},{2,1},{5,4},{6,5},{9,8},{10,9},{13,12},{14,13},{17,16},{18,1... | collective-permute-start | bytes 3145736 | tf_op jit(solution)/shard_map/ppermute | solution.py:838
  125.1 30.1 %collective-permute-start.9 = (bf16[256,2048]{1,0:T(8,128)(2,1)S(1)}, bf16[256,2048]{1,0:T(8,128)(2,1)}, u32[]{:S(2)}, u32[]{:S(2)}) collective-permute-start(bf16[256,2048]{1,0:T(8,128)(2,1)S(1)} %collective-permute-done.7.refs_2_), channel_id=1, source_target_pairs={{1,2},{2,3},{5,6},{6,7},{9,10},{10,11},{13,14},{14,15},{17,18},{18... | collective-permute-start | bytes 3145736 | tf_op jit(solution)/shard_map/ppermute | solution.py:839
  155.2 34.7 %collective-permute-start.13 = (bf16[256,2048]{1,0:T(8,128)(2,1)S(1)}, bf16[256,2048]{1,0:T(8,128)(2,1)}, u32[]{:S(2)}, u32[]{:S(2)}) collective-permute-start(bf16[256,2048]{1,0:T(8,128)(2,1)S(1)} %collective-permute-done.8.refs_3_), channel_id=1, source_target_pairs={{1,0},{5,4},{9,8},{13,12},{17,16},{21,20},{25,24},{29,28}} | collective-permute-start | bytes 3145736 | tf_op jit(solution)/shard_map/ppermute | solution.py:838
  156.9 33.1 %collective-permute-start.14 = (bf16[256,2048]{1,0:T(8,128)(2,1)}, bf16[256,2048]{1,0:T(8,128)(2,1)}, u32[]{:S(2)}, u32[]{:S(2)}) collective-permute-start(bf16[256,2048]{1,0:T(8,128)(2,1)} %collective-permute-done.9.refs_4_), channel_id=1, source_target_pairs={{2,3},{6,7},{10,11},{14,15},{18,19},{22,23},{26,27},{30,31}} | collective-permute-start | bytes 3145736 | tf_op jit(solution)/shard_map/ppermute | solution.py:839
  203.0 130.5 %reduce-scatter.6.cloned.1.call-start = ((), (), s32[]{:S(2)}) async-start(), calls=%async_computation.7 | async-start | bytes 4718592 | tf_op jit(solution)/shard_map/reduce_scatter | solution.py:984
  204.9 24.6 %collective-permute-start.16 = (bf16[256,2048]{1,0:T(8,128)(2,1)S(1)}, bf16[256,2048]{1,0:T(8,128)(2,1)}, u32[]{:S(2)}, u32[]{:S(2)}) collective-permute-start(bf16[256,2048]{1,0:T(8,128)(2,1)S(1)} %get-tuple-element.322), channel_id=1, source_target_pairs={{3,2},{7,6},{11,10},{15,14},{19,18},{23,22},{27,26},{31,30}} | collective-permute-start | bytes 3145736 | tf_op jit(solution)/shard_map/ppermute | solution.py:851
  206.2 23.3 %collective-permute-start.15 = (bf16[256,2048]{1,0:T(8,128)(2,1)S(1)}, bf16[256,2048]{1,0:T(8,128)(2,1)}, u32[]{:S(2)}, u32[]{:S(2)}) collective-permute-start(bf16[256,2048]{1,0:T(8,128)(2,1)S(1)} %get-tuple-element.323), channel_id=1, source_target_pairs={{0,1},{4,5},{8,9},{12,13},{16,17},{20,21},{24,25},{28,29}} | collective-permute-start | bytes 3145736 | tf_op jit(solution)/shard_map/ppermute | solution.py:850
  237.3 158.6 %reduce-scatter.8.cloned.1.call-start = ((), (), s32[]{:S(2)}) async-start(), calls=%async_computation.8 | async-start | bytes 5013504 | tf_op jit(solution)/shard_map/reduce_scatter | solution.py:1004
  241.4 25.5 %collective-permute-start.18 = (bf16[256,2048]{1,0:T(8,128)(2,1)}, bf16[256,2048]{1,0:T(8,128)(2,1)}, u32[]{:S(2)}, u32[]{:S(2)}) collective-permute-start(bf16[256,2048]{1,0:T(8,128)(2,1)} %get-tuple-element.320), channel_id=1, source_target_pairs={{2,1},{3,2},{6,5},{7,6},{10,9},{11,10},{14,13},{15,14},{18,17},{19... | collective-permute-start | bytes 3145736 | tf_op jit(solution)/shard_map/ppermute | solution.py:851
  245.6 25.1 %collective-permute-start.17 = (bf16[256,2048]{1,0:T(8,128)(2,1)}, bf16[256,2048]{1,0:T(8,128)(2,1)}, u32[]{:S(2)}, u32[]{:S(2)}) collective-permute-start(bf16[256,2048]{1,0:T(8,128)(2,1)} %get-tuple-element.321), channel_id=1, source_target_pairs={{0,1},{1,2},{4,5},{5,6},{8,9},{9,10},{12,13},{13,14},{16,17},{17,1... | collective-permute-start | bytes 3145736 | tf_op jit(solution)/shard_map/ppermute | solution.py:850
  270.7 17.8 %collective-permute-start.21 = (f32[2,1024]{1,0:T(2,128)S(1)}, f32[2,1024]{1,0:T(2,128)S(1)}, u32[]{:S(2)}, u32[]{:S(2)}) collective-permute-start(f32[2,1024]{1,0:T(2,128)S(1)} %get-tuple-element.227.refs_0_), channel_id=1, source_target_pairs={{0,1},{1,2},{2,3},{3,0},{4,5},{5,6},{6,7},{7,4},{8,9},{9,10},{10,1... | collective-permute-start | bytes 24584 | tf_op jit(solution)/shard_map/ppermute | solution.py:865
  270.7 17.8 %collective-permute-start.20 = (f32[2,1024]{1,0:T(2,128)S(1)}, f32[2,1024]{1,0:T(2,128)S(1)}, u32[]{:S(2)}, u32[]{:S(2)}) collective-permute-start(f32[2,1024]{1,0:T(2,128)S(1)} %get-tuple-element.227.refs_0_), channel_id=1, source_target_pairs={{0,2},{1,3},{2,0},{3,1},{4,6},{5,7},{6,4},{7,5},{8,10},{9,11},{10,... | collective-permute-start | bytes 24584 | tf_op jit(solution)/shard_map/ppermute | solution.py:865
  271.8 16.8 %collective-permute-start.19 = (f32[2,1024]{1,0:T(2,128)S(1)}, f32[2,1024]{1,0:T(2,128)S(1)}, u32[]{:S(2)}, u32[]{:S(2)}) collective-permute-start(f32[2,1024]{1,0:T(2,128)S(1)} %get-tuple-element.227.refs_0_), channel_id=1, source_target_pairs={{0,3},{1,0},{2,1},{3,2},{4,7},{5,4},{6,5},{7,6},{8,11},{9,8},{10,9... | collective-permute-start | bytes 24584 | tf_op jit(solution)/shard_map/ppermute | solution.py:865
  272.8 48.4 %collective-permute-start.24 = (bf16[128,2048]{1,0:T(8,128)(2,1)}, bf16[128,2048]{1,0:T(8,128)(2,1)S(1)}, u32[]{:S(2)}, u32[]{:S(2)}) collective-permute-start(bf16[128,2048]{1,0:T(8,128)(2,1)} %reduce-scatter.4.cloned.1.call-done), channel_id=1, source_target_pairs={{0,0},{4,1},{8,2},{12,3},{16,4},{20,5},{24,6},{28,7},{1,8},{5,9},{... | collective-permute-start | bytes 1572872 | tf_op jit(solution)/shard_map/ppermute | solution.py:995
  291.0 30.2 %collective-permute-start.23 = (bf16[256,2048]{1,0:T(8,128)(2,1)S(1)}, bf16[256,2048]{1,0:T(8,128)(2,1)S(1)}, u32[]{:S(2)}, u32[]{:S(2)}) collective-permute-start(bf16[256,2048]{1,0:T(8,128)(2,1)S(1)} %get-tuple-element.318), channel_id=1, source_target_pairs={{1,0},{2,1},{3,2},{5,4},{6,5},{7,6},{9,8},{10,9},{11,10},{13,12},{... | collective-permute-start | bytes 3145736 | tf_op jit(solution)/shard_map/ppermute | solution.py:851
  295.8 25.4 %collective-permute-start.22 = (bf16[256,2048]{1,0:T(8,128)(2,1)S(1)}, bf16[256,2048]{1,0:T(8,128)(2,1)S(1)}, u32[]{:S(2)}, u32[]{:S(2)}) collective-permute-start(bf16[256,2048]{1,0:T(8,128)(2,1)S(1)} %get-tuple-element.319), channel_id=1, source_target_pairs={{0,1},{1,2},{2,3},{4,5},{5,6},{6,7},{8,9},{9,10},{10,11},{12,13},{... | collective-permute-start | bytes 3145736 | tf_op jit(solution)/shard_map/ppermute | solution.py:850
  334.6 22.5 %collective-permute-start.28 = (bf16[256,1024]{1,0:T(8,128)(2,1)S(1)}, bf16[256,1024]{1,0:T(8,128)(2,1)S(1)}, u32[]{:S(2)}, u32[]{:S(2)}) collective-permute-start(bf16[256,1024]{1,0:T(8,128)(2,1)S(1)} %copy-done.2), channel_id=1, source_target_pairs={{0,1},{1,2},{2,3},{4,5},{5,6},{6,7},{8,9},{9,10},{10,11},{12,13},{... | collective-permute-start | bytes 1572872 | tf_op jit(solution)/shard_map/ppermute | solution.py:839
  336.5 20.6 %collective-permute-start.27 = (bf16[256,1024]{1,0:T(8,128)(2,1)S(1)}, bf16[256,1024]{1,0:T(8,128)(2,1)S(1)}, u32[]{:S(2)}, u32[]{:S(2)}) collective-permute-start(bf16[256,1024]{1,0:T(8,128)(2,1)S(1)} %copy-done.2), channel_id=1, source_target_pairs={{1,0},{2,1},{3,2},{5,4},{6,5},{7,6},{9,8},{10,9},{11,10},{13,12},{... | collective-permute-start | bytes 1572872 | tf_op jit(solution)/shard_map/ppermute | solution.py:838
  340.9 19.9 %collective-permute-start.26 = (bf16[128,2048]{1,0:T(8,128)(2,1)S(1)}, bf16[128,2048]{1,0:T(8,128)(2,1)S(1)}, u32[]{:S(2)}, u32[]{:S(2)}) collective-permute-start(bf16[128,2048]{1,0:T(8,128)(2,1)S(1)} %collective-permute-done.24.refs_0_), channel_id=1, source_target_pairs={{0,1},{1,2},{2,3},{4,5},{5,6},{6,7},{8,9},{9,10},{10,11},{12,13},{... | collective-permute-start | bytes 1572872 | tf_op jit(solution)/shard_map/ppermute | solution.py:839
  342.8 19.2 %collective-permute-start.25 = (bf16[128,2048]{1,0:T(8,128)(2,1)S(1)}, bf16[128,2048]{1,0:T(8,128)(2,1)S(1)}, u32[]{:S(2)}, u32[]{:S(2)}) collective-permute-start(bf16[128,2048]{1,0:T(8,128)(2,1)S(1)} %collective-permute-done.24.refs_0_), channel_id=1, source_target_pairs={{1,0},{2,1},{3,2},{5,4},{6,5},{7,6},{9,8},{10,9},{11,10},{13,12},{... | collective-permute-start | bytes 1572872 | tf_op jit(solution)/shard_map/ppermute | solution.py:838
  362.0 16.0 %collective-permute-start.31 = (bf16[128,2048]{1,0:T(8,128)(2,1)S(1)}, bf16[128,2048]{1,0:T(8,128)(2,1)S(1)}, u32[]{:S(2)}, u32[]{:S(2)}) collective-permute-start(bf16[128,2048]{1,0:T(8,128)(2,1)S(1)} %collective-permute-done.25.refs_1_), channel_id=1, source_target_pairs={{1,0},{2,1},{5,4},{6,5},{9,8},{10,9},{13,12},{14,13},{17,16},{18,1... | collective-permute-start | bytes 1572872 | tf_op jit(solution)/shard_map/ppermute | solution.py:838
  366.7 27.4 %collective-permute-start.30 = (bf16[256,2048]{1,0:T(8,128)(2,1)S(1)}, bf16[256,2048]{1,0:T(8,128)(2,1)S(1)}, u32[]{:S(2)}, u32[]{:S(2)}) collective-permute-start(bf16[256,2048]{1,0:T(8,128)(2,1)S(1)} %get-tuple-element.316), channel_id=1, source_target_pairs={{3,2},{7,6},{11,10},{15,14},{19,18},{23,22},{27,26},{31,30}} | collective-permute-start | bytes 3145736 | tf_op jit(solution)/shard_map/ppermute | solution.py:851
  368.0 27.8 %collective-permute-start.29 = (bf16[256,2048]{1,0:T(8,128)(2,1)S(1)}, bf16[256,2048]{1,0:T(8,128)(2,1)}, u32[]{:S(2)}, u32[]{:S(2)}) collective-permute-start(bf16[256,2048]{1,0:T(8,128)(2,1)S(1)} %get-tuple-element.317), channel_id=1, source_target_pairs={{0,1},{4,5},{8,9},{12,13},{16,17},{20,21},{24,25},{28,29}} | collective-permute-start | bytes 3145736 | tf_op jit(solution)/shard_map/ppermute | solution.py:850
  369.6 17.0 %collective-permute-start.32 = (bf16[128,2048]{1,0:T(8,128)(2,1)S(1)}, bf16[128,2048]{1,0:T(8,128)(2,1)S(1)}, u32[]{:S(2)}, u32[]{:S(2)}) collective-permute-start(bf16[128,2048]{1,0:T(8,128)(2,1)S(1)} %collective-permute-done.26.refs_2_), channel_id=1, source_target_pairs={{1,2},{2,3},{5,6},{6,7},{9,10},{10,11},{13,14},{14,15},{17,18},{18... | collective-permute-start | bytes 1572872 | tf_op jit(solution)/shard_map/ppermute | solution.py:839
  378.8 15.2 %collective-permute-start.34 = (bf16[256,1024]{1,0:T(8,128)(2,1)S(1)}, bf16[256,1024]{1,0:T(8,128)(2,1)S(1)}, u32[]{:S(2)}, u32[]{:S(2)}) collective-permute-start(bf16[256,1024]{1,0:T(8,128)(2,1)S(1)} %collective-permute-done.28.refs_2_), channel_id=1, source_target_pairs={{1,2},{2,3},{5,6},{6,7},{9,10},{10,11},{13,14},{14,15},{17,18},{18... | collective-permute-start | bytes 1572872 | tf_op jit(solution)/shard_map/ppermute | solution.py:839
  396.9 16.8 %collective-permute-start.42 = (bf16[256,1024]{1,0:T(8,128)(2,1)S(1)}, bf16[256,1024]{1,0:T(8,128)(2,1)}, u32[]{:S(2)}, u32[]{:S(2)}) collective-permute-start(bf16[256,1024]{1,0:T(8,128)(2,1)S(1)} %slice.44.refs_1_), channel_id=1, source_target_pairs={{0,1},{1,2},{2,3},{4,5},{5,6},{6,7},{8,9},{9,10},{10,11},{12,13},{... | collective-permute-start | bytes 1572872 | tf_op jit(solution)/shard_map/ppermute | solution.py:839
  402.1 18.3 %collective-permute-start.40 = (bf16[256,1024]{1,0:T(8,128)(2,1)}, bf16[256,1024]{1,0:T(8,128)(2,1)S(1)}, u32[]{:S(2)}, u32[]{:S(2)}) collective-permute-start(bf16[256,1024]{1,0:T(8,128)(2,1)} %copy-done.23), channel_id=1, source_target_pairs={{2,3},{6,7},{10,11},{14,15},{18,19},{22,23},{26,27},{30,31}} | collective-permute-start | bytes 1572872 | tf_op jit(solution)/shard_map/ppermute | solution.py:839
  406.2 49.3 %collective-permute-start.36 = (bf16[256,2048]{1,0:T(8,128)(2,1)S(1)}, bf16[256,2048]{1,0:T(8,128)(2,1)S(1)}, u32[]{:S(2)}, u32[]{:S(2)}) collective-permute-start(bf16[256,2048]{1,0:T(8,128)(2,1)S(1)} %get-tuple-element.314), channel_id=1, source_target_pairs={{2,1},{3,2},{6,5},{7,6},{10,9},{11,10},{14,13},{15,14},{18,17},{19... | collective-permute-start | bytes 3145736 | tf_op jit(solution)/shard_map/ppermute | solution.py:851
  408.7 46.9 %collective-permute-start.35 = (bf16[256,2048]{1,0:T(8,128)(2,1)S(1)}, bf16[256,2048]{1,0:T(8,128)(2,1)S(1)}, u32[]{:S(2)}, u32[]{:S(2)}) collective-permute-start(bf16[256,2048]{1,0:T(8,128)(2,1)S(1)} %get-tuple-element.315), channel_id=1, source_target_pairs={{0,1},{1,2},{4,5},{5,6},{8,9},{9,10},{12,13},{13,14},{16,17},{17,1... | collective-permute-start | bytes 3145736 | tf_op jit(solution)/shard_map/ppermute | solution.py:850
  413.8 40.1 %collective-permute-start.41 = (bf16[256,1024]{1,0:T(8,128)(2,1)S(1)}, bf16[256,1024]{1,0:T(8,128)(2,1)}, u32[]{:S(2)}, u32[]{:S(2)}) collective-permute-start(bf16[256,1024]{1,0:T(8,128)(2,1)S(1)} %slice.44.refs_1_), channel_id=1, source_target_pairs={{1,0},{2,1},{3,2},{5,4},{6,5},{7,6},{9,8},{10,9},{11,10},{13,12},{... | collective-permute-start | bytes 1572872 | tf_op jit(solution)/shard_map/ppermute | solution.py:838
  415.7 38.2 %collective-permute-start.37 = (bf16[128,2048]{1,0:T(8,128)(2,1)S(1)}, bf16[128,2048]{1,0:T(8,128)(2,1)S(1)}, u32[]{:S(2)}, u32[]{:S(2)}) collective-permute-start(bf16[128,2048]{1,0:T(8,128)(2,1)S(1)} %copy-done.16), channel_id=1, source_target_pairs={{1,0},{5,4},{9,8},{13,12},{17,16},{21,20},{25,24},{29,28}} | collective-permute-start | bytes 1572872 | tf_op jit(solution)/shard_map/ppermute | solution.py:838
  420.5 34.3 %collective-permute-start.38 = (bf16[128,2048]{1,0:T(8,128)(2,1)S(1)}, bf16[128,2048]{1,0:T(8,128)(2,1)S(1)}, u32[]{:S(2)}, u32[]{:S(2)}) collective-permute-start(bf16[128,2048]{1,0:T(8,128)(2,1)S(1)} %copy-done.21), channel_id=1, source_target_pairs={{2,3},{6,7},{10,11},{14,15},{18,19},{22,23},{26,27},{30,31}} | collective-permute-start | bytes 1572872 | tf_op jit(solution)/shard_map/ppermute | solution.py:839
  457.8 38.3 %collective-permute-start.44 = (bf16[256,2048]{1,0:T(8,128)(2,1)}, bf16[256,2048]{1,0:T(8,128)(2,1)}, u32[]{:S(2)}, u32[]{:S(2)}) collective-permute-start(bf16[256,2048]{1,0:T(8,128)(2,1)} %get-tuple-element.312), channel_id=1, source_target_pairs={{1,0},{2,1},{3,2},{5,4},{6,5},{7,6},{9,8},{10,9},{11,10},{13,12},{... | collective-permute-start | bytes 3145736 | tf_op jit(solution)/shard_map/ppermute | solution.py:851
  459.7 36.4 %collective-permute-start.43 = (bf16[256,2048]{1,0:T(8,128)(2,1)}, bf16[256,2048]{1,0:T(8,128)(2,1)}, u32[]{:S(2)}, u32[]{:S(2)}) collective-permute-start(bf16[256,2048]{1,0:T(8,128)(2,1)} %get-tuple-element.313), channel_id=1, source_target_pairs={{0,1},{1,2},{2,3},{4,5},{5,6},{6,7},{8,9},{9,10},{10,11},{12,13},{... | collective-permute-start | bytes 3145736 | tf_op jit(solution)/shard_map/ppermute | solution.py:850
  464.6 26.8 %collective-permute-start.45 = (bf16[256,1024]{1,0:T(8,128)(2,1)}, bf16[256,1024]{1,0:T(8,128)(2,1)}, u32[]{:S(2)}, u32[]{:S(2)}) collective-permute-start(bf16[256,1024]{1,0:T(8,128)(2,1)} %collective-permute-done.41.refs_2_), channel_id=1, source_target_pairs={{1,0},{2,1},{5,4},{6,5},{9,8},{10,9},{13,12},{14,13},{17,16},{18,1... | collective-permute-start | bytes 1572872 | tf_op jit(solution)/shard_map/ppermute | solution.py:838
  467.1 29.0 %collective-permute-start.46 = (bf16[256,1024]{1,0:T(8,128)(2,1)}, bf16[256,1024]{1,0:T(8,128)(2,1)}, u32[]{:S(2)}, u32[]{:S(2)}) collective-permute-start(bf16[256,1024]{1,0:T(8,128)(2,1)} %collective-permute-done.42.refs_3_), channel_id=1, source_target_pairs={{1,2},{2,3},{5,6},{6,7},{9,10},{10,11},{13,14},{14,15},{17,18},{18... | collective-permute-start | bytes 1572872 | tf_op jit(solution)/shard_map/ppermute | solution.py:839
  499.2 14.8 %collective-permute-start.47 = (bf16[256,1024]{1,0:T(8,128)(2,1)}, bf16[256,1024]{1,0:T(8,128)(2,1)S(1)}, u32[]{:S(2)}, u32[]{:S(2)}) collective-permute-start(bf16[256,1024]{1,0:T(8,128)(2,1)} %collective-permute-done.45.refs_4_), channel_id=1, source_target_pairs={{1,0},{5,4},{9,8},{13,12},{17,16},{21,20},{25,24},{29,28}} | collective-permute-start | bytes 1572872 | tf_op jit(solution)/shard_map/ppermute | solution.py:838
  (72 other events, 1023.9 us)
Sparse Core Ops, SparseCore 0:
  9.9 37.7 all-gather.5
  49.6 36.7 all-gather.7
  88.3 89.8 all-gather.9
  203.1 51.3 reduce-scatter.3
  258.1 58.5 reduce-scatter.5
  333.7 53.2 reduce-scatter.7
